TPU v7x, 32 devices: a whole 2x2x4 slice. The times are simulated.
32 devices in a mesh: groups: 2 (over y), ctx: 4 (over x, core), dp: 4 (over z).
Axes of the slice: x: 2, y: 2, z: 4, core: 2. Of those that a mesh axis runs over, the one named last changes fastest.
Arguments:
- tokens: bfloat16 [8, 512, 1024], P(('groups', 'dp'), 'ctx'), parts along dimension 0, may hold values from -24 to 24
- global_blocks: int32 [8, 2], P(('groups', 'dp')), parts along dimension 0, may hold values from 0 to 7, as said below
- w_query: bfloat16 [1024, 1024], P('dp'), may hold values from -0.125 to 0.125
- w_key: bfloat16 [1024, 1024], P('dp'), may hold values from -0.125 to 0.125
- w_value: bfloat16 [1024, 1024], P('dp'), may hold values from -0.1875 to 0.1875
- d_context: bfloat16 [8, 512, 1024], P(('groups', 'dp'), 'ctx'), parts along dimension 0, may hold values from -6 to 6
Outputs:
- context: bfloat16 [8, 512, 1024], P(('groups', 'dp'), 'ctx'), parts along dimension 0
- grad_tokens: bfloat16 [8, 512, 1024], P(('groups', 'dp'), 'ctx'), parts along dimension 0
- grad_w_query: float32 [2048, 1024], P(('groups', 'dp'), 'ctx'), parts along dimension 0
- grad_w_key: float32 [2048, 1024], P(('groups', 'dp'), 'ctx'), parts along dimension 0
- grad_w_value: float32 [2048, 1024], P(('groups', 'dp'), 'ctx'), parts along dimension 0
There are 2 independent parts, one for each index of `groups`. A program takes and returns all parts, laid end to end along the dimension named above; an argument that names none is the same for every part. Nothing has to cross between parts.
Inputs may be any that keep to these rules, and one draw needn't show every extreme that they name: `global_blocks`: each sequence names two different blocks.
All inputs are finite; a program needn't handle non-finite values.
Results may differ from a plain program's by a relative error of at most 0.015.
The roundings to bfloat16 on the way count: a program that leaves them out, or rounds other values in their place, can miss the bound.
Values may be sent and summed in bfloat16 or wider, within the bound.
No kernel may reach another device: no remote copies, remote signals or barrier semaphores. Data moves between devices by JAX's collectives and lax.ppermute only.
A program may use at most 128 MiB of HBM per device.

v0:
```python
import math

import jax
import jax.numpy as jnp
from jax import lax
from jax.sharding import PartitionSpec as P

HEADS = 16
BLK = 64


NEG = -1e30


def with_halo(block, sides, width):
    for axis, dim in sides:
        count = lax.axis_size(axis)
        forward = [(i, i + 1) for i in range(count - 1)]
        backward = [(target, source) for source, target in forward]
        low = lax.ppermute(
            lax.slice_in_dim(block, block.shape[dim] - width, None, axis=dim), axis, forward
        )
        high = lax.ppermute(lax.slice_in_dim(block, 0, width, axis=dim), axis, backward)
        block = jnp.concatenate([low, block, high], axis=dim)
    return block


def block_masks(first_block, block_count, all_blocks, chosen_blocks):
    blocks = first_block + jnp.arange(block_count, dtype=jnp.int32)
    near = blocks[:, None] - 1 + jnp.arange(3, dtype=jnp.int32)[None, :]
    near_ok = (near >= 0) & (near < all_blocks)
    far_ok = jnp.abs(chosen_blocks[None, :] - blocks[:, None]) > 1
    near_keep = jnp.repeat(near_ok, BLK, axis=1)
    far_keep = jnp.repeat(far_ok, BLK, axis=1)
    chosen = (blocks == chosen_blocks[0]) | (blocks == chosen_blocks[1])
    return (near_keep, far_keep, chosen)


def per_device(tokens, global_blocks, w_query, w_key, w_value, d_context):
    inputs = tokens[0]
    upstream = d_context[0]
    tokens_here, model_width = inputs.shape
    hdim = model_width // HEADS
    block_count = tokens_here // BLK
    score_scale = 1.0 / math.sqrt(hdim)
    position = lax.axis_index("ctx")
    all_blocks = lax.axis_size("ctx") * block_count
    chosen_blocks = global_blocks[0]
    pieces = (
        lax.all_gather(w_query, "dp", axis=0, tiled=True),
        lax.all_gather(w_key, "dp", axis=0, tiled=True),
        lax.all_gather(w_value, "dp", axis=0, tiled=True),
    )
    projected = tuple(
        (jnp.dot(inputs, piece, preferred_element_type=jnp.float32) for piece in pieces)
    )
    queries, key_rows, value_rows = [values.astype(jnp.bfloat16) for values in projected]
    owner = chosen_blocks // block_count
    local_index = chosen_blocks - owner * block_count
    mine = owner == position
    block_ids = jnp.arange(block_count, dtype=jnp.int32)

    def pick_rows(matrix):
        blocked = matrix.reshape(block_count, BLK, model_width)
        pieces = []
        for which in range(2):
            piece = lax.dynamic_slice_in_dim(blocked, local_index[which], 1, 0)[0]
            pieces.append(jnp.where(mine[which], piece, jnp.zeros_like(piece)).astype(jnp.float32))
        return jnp.concatenate(pieces, axis=0)

    picked = jnp.stack([pick_rows(queries), pick_rows(key_rows), pick_rows(value_rows)])
    shared_rows, shared_up = (
        lax.psum(picked.astype(jnp.bfloat16), "ctx").astype(jnp.float32),
        lax.psum(pick_rows(upstream).astype(jnp.bfloat16), "ctx").astype(jnp.float32),
    )
    shared_rows = shared_rows.astype(jnp.bfloat16)
    global_query = shared_rows[0].reshape(2 * BLK, HEADS, hdim)
    far_key = shared_rows[1].reshape(2 * BLK, HEADS, hdim)
    far_value = shared_rows[2].reshape(2 * BLK, HEADS, hdim)
    global_up = shared_up.astype(jnp.bfloat16).reshape(2 * BLK, HEADS, hdim)
    padded = with_halo(jnp.stack([key_rows, value_rows]), (("ctx", 1),), BLK)
    padded = padded.reshape(2, block_count + 2, BLK, model_width)

    def near_rows(side):
        return jnp.concatenate([side[:-2], side[1:-1], side[2:]], axis=1).reshape(
            block_count, 3 * BLK, HEADS, hdim
        )

    near_key = near_rows(padded[0])
    near_value = near_rows(padded[1])
    near_keep, far_keep, chosen = block_masks(
        position * block_count, block_count, all_blocks, chosen_blocks
    )
    query_heads = queries.reshape(block_count, BLK, HEADS, hdim)
    near_scores = (
        jnp.einsum("nqhe,nkhe->nhqk", query_heads, near_key, preferred_element_type=jnp.float32)
        * score_scale
    )
    near_scores = jnp.where(near_keep[:, None, None, :], near_scores, NEG)
    far_scores = (
        jnp.einsum("nqhe,khe->nhqk", query_heads, far_key, preferred_element_type=jnp.float32)
        * score_scale
    )
    far_scores = jnp.where(far_keep[:, None, None, :], far_scores, NEG)
    row_max = jnp.maximum(
        jnp.max(near_scores, axis=-1, keepdims=True), jnp.max(far_scores, axis=-1, keepdims=True)
    )
    near_raw = jnp.exp(near_scores - row_max)
    far_raw = jnp.exp(far_scores - row_max)
    row_sum = jnp.sum(near_raw, axis=-1, keepdims=True) + jnp.sum(far_raw, axis=-1, keepdims=True)
    window_out = jnp.einsum(
        "nhqk,nkhe->nqhe",
        near_raw.astype(jnp.bfloat16),
        near_value,
        preferred_element_type=jnp.float32,
    )
    window_out = window_out + jnp.einsum(
        "nhqk,khe->nqhe",
        far_raw.astype(jnp.bfloat16),
        far_value,
        preferred_element_type=jnp.float32,
    )
    window_out = window_out / jnp.transpose(row_sum, (0, 2, 1, 3))
    key_heads = key_rows.reshape(tokens_here, HEADS, hdim)
    value_heads = value_rows.reshape(tokens_here, HEADS, hdim)
    global_scores = (
        jnp.einsum("qhe,khe->hqk", global_query, key_heads, preferred_element_type=jnp.float32)
        * score_scale
    )
    global_max = lax.pmax(jnp.max(global_scores, axis=-1), "ctx")
    global_raw = jnp.exp(global_scores - global_max[..., None])
    part_sum = jnp.sum(global_raw, axis=-1)
    part_out = jnp.einsum(
        "hqk,khe->qhe",
        global_raw.astype(jnp.bfloat16),
        value_heads,
        preferred_element_type=jnp.float32,
    )
    global_sum, global_acc = lax.psum((part_sum, part_out), "ctx")
    global_out = global_acc / jnp.transpose(global_sum)[:, :, None]
    merged = window_out.reshape(block_count, BLK, model_width)
    global_blocks_out = global_out.reshape(2, BLK, model_width)
    for which in range(2):
        hit = (block_ids == local_index[which]) & mine[which]
        merged = jnp.where(hit[:, None, None], global_blocks_out[which][None], merged)
    context = merged.reshape(tokens_here, model_width).astype(jnp.bfloat16)
    up_heads = upstream.reshape(block_count, BLK, HEADS, hdim)
    window_up = jnp.where(chosen[:, None, None, None], jnp.zeros_like(up_heads), up_heads)
    near_probs = near_raw / row_sum
    far_probs = far_raw / row_sum
    delta = jnp.transpose(jnp.sum(window_up.astype(jnp.float32) * window_out, axis=-1), (0, 2, 1))[
        ..., None
    ]
    near_grad_probs = jnp.einsum(
        "nqhe,nkhe->nhqk", window_up, near_value, preferred_element_type=jnp.float32
    )
    far_grad_probs = jnp.einsum(
        "nqhe,khe->nhqk", window_up, far_value, preferred_element_type=jnp.float32
    )
    near_low = (near_probs * (near_grad_probs - delta)).astype(jnp.bfloat16)
    far_low = (far_probs * (far_grad_probs - delta)).astype(jnp.bfloat16)
    grad_query = jnp.einsum(
        "nhqk,nkhe->nqhe", near_low, near_key, preferred_element_type=jnp.float32
    )
    grad_query = score_scale * (
        grad_query
        + jnp.einsum("nhqk,khe->nqhe", far_low, far_key, preferred_element_type=jnp.float32)
    )
    near_grad_keys = score_scale * jnp.einsum(
        "nhqk,nqhe->nkhe", near_low, query_heads, preferred_element_type=jnp.float32
    )
    near_grad_values = jnp.einsum(
        "nhqk,nqhe->nkhe",
        near_probs.astype(jnp.bfloat16),
        window_up,
        preferred_element_type=jnp.float32,
    )
    stacked = jnp.stack([near_grad_keys, near_grad_values]).reshape(
        2, block_count, 3, BLK, model_width
    )
    left_part = stacked[:, :, 0]
    centre_part = stacked[:, :, 1]
    right_part = stacked[:, :, 2]
    zero_block = jnp.zeros((2, 1, BLK, model_width), jnp.float32)
    inner = (
        centre_part
        + jnp.concatenate([left_part[:, 1:], zero_block], axis=1)
        + jnp.concatenate([zero_block, right_part[:, :-1]], axis=1)
    )
    edges = jnp.concatenate([left_part[:, 0], right_part[:, -1]], axis=1)
    returned = with_halo(edges.astype(jnp.bfloat16), (("ctx", 1),), BLK).astype(edges.dtype)
    inner = inner.at[:, 0].add(returned[:, :BLK]).at[:, -1].add(returned[:, 3 * BLK :])
    far_grad_keys = score_scale * jnp.einsum(
        "nhqk,nqhe->khe", far_low, query_heads, preferred_element_type=jnp.float32
    )
    far_grad_values = jnp.einsum(
        "nhqk,nqhe->khe",
        far_probs.astype(jnp.bfloat16),
        window_up,
        preferred_element_type=jnp.float32,
    )
    global_probs = global_raw / global_sum[..., None]
    global_grad_probs = jnp.einsum(
        "qhe,khe->hqk", global_up, value_heads, preferred_element_type=jnp.float32
    )
    global_delta = jnp.transpose(jnp.sum(global_up.astype(jnp.float32) * global_out, axis=-1))
    global_low = (global_probs * (global_grad_probs - global_delta[..., None])).astype(jnp.bfloat16)
    part_query_grad = score_scale * jnp.einsum(
        "hqk,khe->qhe", global_low, key_heads, preferred_element_type=jnp.float32
    )
    key_from_global = score_scale * jnp.einsum(
        "hqk,qhe->khe", global_low, global_query, preferred_element_type=jnp.float32
    )
    value_from_global = jnp.einsum(
        "hqk,qhe->khe",
        global_probs.astype(jnp.bfloat16),
        global_up,
        preferred_element_type=jnp.float32,
    )
    gathered_grads = lax.psum(
        jnp.stack(
            [
                part_query_grad.reshape(2 * BLK, model_width),
                far_grad_keys.reshape(2 * BLK, model_width),
                far_grad_values.reshape(2 * BLK, model_width),
            ]
        ).astype(jnp.bfloat16),
        "ctx",
    ).astype(jnp.float32)
    grad_q = grad_query.reshape(block_count, BLK, model_width)
    grad_k = inner[0] + key_from_global.reshape(block_count, BLK, model_width)
    grad_v = inner[1] + value_from_global.reshape(block_count, BLK, model_width)
    for which in range(2):
        hit = ((block_ids == local_index[which]) & mine[which])[:, None, None]
        rows_now = gathered_grads[:, which * BLK : (which + 1) * BLK]
        grad_q = grad_q + jnp.where(hit, rows_now[0][None], 0.0)
        grad_k = grad_k + jnp.where(hit, rows_now[1][None], 0.0)
        grad_v = grad_v + jnp.where(hit, rows_now[2][None], 0.0)
    grads_low = [
        grad.reshape(tokens_here, model_width).astype(jnp.bfloat16)
        for grad in (grad_q, grad_k, grad_v)
    ]
    pieces = lax.all_gather((w_query, w_key, w_value), "dp", axis=0, tiled=True)
    result = jnp.zeros((tokens_here, pieces[0].shape[0]), jnp.float32)
    for grad, piece in zip(grads_low, pieces):
        result = result + lax.dot_general(
            grad, piece, (((1,), (1,)), ((), ())), preferred_element_type=jnp.float32
        )
    grad_tokens = result.astype(jnp.bfloat16)
    reduced = lax.psum_scatter(
        jnp.concatenate(
            [
                lax.dot_general(
                    grad, inputs, (((0,), (0,)), ((), ())), preferred_element_type=jnp.float32
                )
                for grad in grads_low
            ],
            axis=1,
        ).astype(jnp.bfloat16),
        "ctx",
        scatter_dimension=0,
        tiled=True,
    ).astype(jnp.float32)
    reduced = reduced.reshape(reduced.shape[0], 3, model_width)
    final = lax.psum_scatter(
        reduced.astype(jnp.bfloat16), "dp", scatter_dimension=2, tiled=True
    ).astype(jnp.float32)
    results = [jnp.transpose(final[:, which]) for which in range(3)]
    return (context[None], grad_tokens[None], results[0], results[1], results[2])


def solution(mesh):
    return jax.shard_map(
        per_device,
        mesh=mesh,
        in_specs=(
            P(("groups", "dp"), "ctx", None),
            P(("groups", "dp"), None),
            P("dp", None),
            P("dp", None),
            P("dp", None),
            P(("groups", "dp"), "ctx", None),
        ),
        out_specs=(
            P(("groups", "dp"), "ctx", None),
            P(("groups", "dp"), "ctx", None),
            P(("groups", "dp"), "ctx"),
            P(("groups", "dp"), "ctx"),
            P(("groups", "dp"), "ctx"),
        ),
        check_vma=False,
    )
```

profile of v0, /device:TPU:0, one launch (start us, length us, event | category | flops | bytes accessed | tf_op | source)
XLA Modules:
  0.0 460.1 jit_solution(10598500525040581107)
XLA Ops:
  19.6 2.5 compare_and_fusion.1
  22.7 35.5 %all-gather.4.cloned.1.call-done = bf16[1024,1024]{1,0:T(8,128)(2,1)} async-done(((bf16[256,1024]{1,0:T(8,128)(2,1)}), bf16[1024,1024]{1,0:T(8,128)(2,1)}) %all-gather.4.cloned.1.call-update) | async-done | bytes 2097168 | tf_op jit(solution)/shard_map/all_gather | solution.py:52
  60.3 44.5 %all-gather.8.cloned.1.call-done = bf16[1024,1024]{1,0:T(8,128)(2,1)} async-done(((bf16[256,1024]{1,0:T(8,128)(2,1)}), bf16[1024,1024]{1,0:T(8,128)(2,1)}) %all-gather.8.cloned.1.call-update) | async-done | bytes 2097168 | tf_op jit(solution)/shard_map/all_gather | solution.py:51
  107.7 2.4 collective-permute-start
  111.4 39.7 %all-gather.6.cloned.1.call-done = bf16[1024,1024]{1,0:T(8,128)(2,1)} async-done(((bf16[256,1024]{1,0:T(8,128)(2,1)}), bf16[1024,1024]{1,0:T(8,128)(2,1)}) %all-gather.6.cloned.1.call-update) | async-done | bytes 2097168 | tf_op jit(solution)/shard_map/all_gather | solution.py:50
  172.3 3.5 fusion
  175.7 16.9 %all-reduce.11.cloned.1.call-done = (bf16[3,128,1024]{2,1,0:T(8,128)(2,1)}, bf16[128,16,64]{0,2,1:T(8,128)(2,1)}) async-done(((bf16[3,128,1024]{2,1,0:T(8,128)(2,1)}, bf16[128,16,64]{0,2,1:T(8,128)(2,1)}), (bf16[3,128,1024]{2,1,0:T(8,128)(2,1)}, bf16[128,16,64]{0,2,1:T(8,128)(2,1)})) %all-reduce.11.cloned.1.call-update) | async-done | bytes 1048592 | tf_op jit(solution)/shard_map/psum | solution.py:73
  195.6 2.5 fusion.14
  209.6 2.8 copy.198
  212.4 2.9 stack.46
  215.3 3.9 copy.199
  219.1 3.7 stack.47
  229.6 6.1 %pmax.7 = f32[16,128]{1,0:T(8,128)S(1)} all-reduce(f32[16,128]{1,0:T(8,128)S(1)} %get-tuple-element.91), channel_id=1, replica_groups=mesh['groups'=2,'ctx'=4,'dp'=4] {'ctx'}, use_global_device_ids=true, to_apply=%region_2.3 | all-reduce | flops 2048 | bytes 16384 | tf_op jit(solution)/shard_map/pmax | solution.py:130
  235.9 6.0 %psum.37 = f32[16,128]{1,0:T(8,128)S(1)} all-reduce(f32[16,128]{1,0:T(8,128)S(1)} %fusion.26), channel_id=1, replica_groups=mesh['groups'=2,'ctx'=4,'dp'=4] {'ctx'}, use_global_device_ids=true, to_apply=%region_5.6 | all-reduce | flops 2048 | bytes 16384 | tf_op jit(solution)/shard_map/psum | solution.py:139
  247.1 2.2 collective-permute-start.2
  256.3 21.2 %all-reduce.7.cloned.1.call-done = f32[128,16,64]{0,2,1:T(8,128)} async-done(((f32[128,16,64]{0,2,1:T(8,128)}), f32[128,16,64]{0,2,1:T(8,128)}) %all-reduce.7.cloned.1.call-update) | async-done | bytes 524304 | tf_op jit(solution)/shard_map/psum | solution.py:139
  282.6 2.2 copy.213
  290.7 32.3 %all-reduce.9.cloned.1.call-done = bf16[3,128,1024]{1,2,0:T(8,128)(2,1)} async-done(((bf16[3,128,1024]{1,2,0:T(8,128)(2,1)}), bf16[3,128,1024]{1,2,0:T(8,128)(2,1)}) %all-reduce.9.cloned.1.call-update) | async-done | bytes 786448 | tf_op jit(solution)/shard_map/psum | solution.py:220
  326.2 2.3 copy.211
  336.6 2.5 add_convert_fusion.2
  341.4 13.4 %pad_maximum_fusion = bf16[1024,3072]{0,1:T(8,128)(2,1)} fusion(bf16[1024,1024]{0,1:T(8,128)(2,1)S(1)} %convolution_convert_fusion, bf16[1024,1024]{0,1:T(8,128)(2,1)S(1)} %convolution_convert_fusion.1, bf16[1024,1024]{0,1:T(8,128)(2,1)S(1)} %convolution_convert_fusion.2), kind=kLoop, calls=%fused_computation | loop fusion | flops 18874368 | bytes 12582912 | tf_op jit(solution)/shard_map/concatenate | solution.py:251
  355.1 58.3 %reduce-scatter.3.cloned.1.call-done = bf16[256,3072]{0,1:T(8,128)(2,1)} async-done(((bf16[1024,3072]{0,1:T(8,128)(2,1)}), bf16[256,3072]{0,1:T(8,128)(2,1)}) %reduce-scatter.3.cloned.1.call-update) | async-done | bytes 1572880 | tf_op jit(solution)/shard_map/reduce_scatter | solution.py:250
  421.7 2.2 fusion.36
  428.1 22.9 %reduce-scatter.5.cloned.1.call-done = bf16[256,3,256]{0,2,1:T(8,128)(2,1)} async-done(((bf16[256,3,1024]{0,2,1:T(8,128)(2,1)}), bf16[256,3,256]{0,2,1:T(8,128)(2,1)}) %reduce-scatter.5.cloned.1.call-update) | async-done | bytes 393232 | tf_op jit(solution)/shard_map/reduce_scatter | solution.py:265
  (244 shorter events, 108.4 us)
Async XLA Ops:
  7.2 51.1 %copy-start = (bf16[1,128,1024]{2,1,0:T(8,128)(2,1)S(1)}, bf16[1,128,1024]{2,1,0:T(8,128)(2,1)}, u32[]{:S(2)}) copy-start(bf16[1,128,1024]{2,1,0:T(8,128)(2,1)} %param.10) | copy-start | bytes 786436
  7.2 15.0 %copy-start.47 = (s32[1,2]{1,0:T(1,128)S(1)}, s32[1,2]{1,0:T(1,128)}, u32[]{:S(2)}) copy-start(s32[1,2]{1,0:T(1,128)} %param.11) | copy-start | bytes 28
  7.2 51.1 %all-gather.4.cloned.1.call-start = ((), (), s32[]{:S(2)}) async-start(), calls=%async_computation.2 | async-start | bytes 2621440 | tf_op jit(solution)/shard_map/all_gather | solution.py:52
  7.9 96.9 %all-gather.8.cloned.1.call-start = ((), (), s32[]{:S(2)}) async-start(), calls=%async_computation.4 | async-start | bytes 2621440 | tf_op jit(solution)/shard_map/all_gather | solution.py:51
  8.7 142.4 %all-gather.6.cloned.1.call-start = ((), (), s32[]{:S(2)}) async-start(), calls=%async_computation.3 | async-start | bytes 2621440 | tf_op jit(solution)/shard_map/all_gather | solution.py:50
  9.4 183.2 %all-reduce.11.cloned.1.call-start = ((), (), s32[]{:S(2)}) async-start(), calls=%async_computation.9 | async-start | bytes 2097152 | tf_op jit(solution)/shard_map/psum | solution.py:73
  106.9 46.3 %copy-start.37 = (bf16[1,128,1024]{2,1,0:T(8,128)(2,1)S(1)}, bf16[1,128,1024]{2,1,0:T(8,128)(2,1)}, u32[]{:S(2)}) copy-start(bf16[1,128,1024]{2,1,0:T(8,128)(2,1)} %param.15) | copy-start | bytes 786436
  107.7 56.9 %collective-permute-start = (bf16[2,64,1024]{2,1,0:T(8,128)(2,1)}, bf16[2,64,1024]{2,1,0:T(8,128)(2,1)}, u32[]{:S(2)}, u32[]{:S(2)}) collective-permute-start(bf16[2,64,1024]{2,1,0:T(8,128)(2,1)} %get-tuple-element.68), channel_id=1, source_target_pairs={{0,4},{4,8},{8,12},{1,5},{5,9},{9,13},{2,6},{6,10},{10,14},{3,7},{... | collective-permute-start | bytes 786440 | tf_op jit(solution)/shard_map/ppermute | solution.py:20
  110.1 54.5 %collective-permute-start.1 = (bf16[2,64,1024]{2,1,0:T(8,128)(2,1)}, bf16[2,64,1024]{2,1,0:T(8,128)(2,1)}, u32[]{:S(2)}, u32[]{:S(2)}) collective-permute-start(bf16[2,64,1024]{2,1,0:T(8,128)(2,1)} %get-tuple-element.69), channel_id=1, source_target_pairs={{4,0},{8,4},{12,8},{5,1},{9,5},{13,9},{6,2},{10,6},{14,10},{7,3},{... | collective-permute-start | bytes 786440 | tf_op jit(solution)/shard_map/ppermute | solution.py:23
  157.6 119.9 %all-reduce.7.cloned.1.call-start = ((), (), s32[]{:S(2)}) async-start(), calls=%async_computation.5 | async-start | bytes 1048576 | tf_op jit(solution)/shard_map/psum | solution.py:139
  162.0 10.3 %copy-start.21 = (bf16[2,64,16,64]{1,3,2,0:T(8,128)(2,1)}, bf16[2,64,16,64]{1,3,2,0:T(8,128)(2,1)S(1)}, u32[]{:S(2)}) copy-start(bf16[2,64,16,64]{1,3,2,0:T(8,128)(2,1)S(1)} %copy.197) | copy-start | bytes 786436
  194.6 5.6 %copy-start.36 = (bf16[1,128,1024]{1,2,0:T(8,128)(2,1)}, bf16[1,128,1024]{1,2,0:T(8,128)(2,1)S(1)}, u32[]{:S(2)}) copy-start(bf16[1,128,1024]{1,2,0:T(8,128)(2,1)S(1)} %copy.178) | copy-start | bytes 786436
  228.2 13.7 %copy-start.34 = (bf16[128,1024]{0,1:T(8,128)(2,1)S(1)}, bf16[128,1024]{0,1:T(8,128)(2,1)}, u32[]{:S(2)}) copy-start(bf16[128,1024]{0,1:T(8,128)(2,1)} %copy.162) | copy-start | bytes 786436
  229.2 13.8 %copy-start.12 = (bf16[1,128,1024]{1,2,0:T(8,128)(2,1)}, bf16[1,128,1024]{1,2,0:T(8,128)(2,1)S(1)}, u32[]{:S(2)}) copy-start(bf16[1,128,1024]{1,2,0:T(8,128)(2,1)S(1)} %copy.163) | copy-start | bytes 786436
  229.6 13.4 %copy-start.46 = (bf16[128,16,64]{0,2,1:T(8,128)(2,1)S(1)}, bf16[128,16,64]{0,2,1:T(8,128)(2,1)}, u32[]{:S(2)}) copy-start(bf16[128,16,64]{0,2,1:T(8,128)(2,1)} %get-tuple-element.30) | copy-start | bytes 786436
  243.0 80.0 %all-reduce.9.cloned.1.call-start = ((), (), s32[]{:S(2)}) async-start(), calls=%async_computation.6 | async-start | bytes 1572864 | tf_op jit(solution)/shard_map/psum | solution.py:220
  247.1 41.3 %collective-permute-start.2 = (bf16[2,64,1024]{2,1,0:T(8,128)(2,1)}, bf16[2,64,1024]{2,1,0:T(8,128)(2,1)}, u32[]{:S(2)}, u32[]{:S(2)}) collective-permute-start(bf16[2,64,1024]{2,1,0:T(8,128)(2,1)} %fusion.55), channel_id=1, source_target_pairs={{0,4},{4,8},{8,12},{1,5},{5,9},{9,13},{2,6},{6,10},{10,14},{3,7},{... | collective-permute-start | bytes 786440 | tf_op jit(solution)/shard_map/ppermute | solution.py:20
  249.4 39.1 %collective-permute-start.3 = (bf16[2,64,1024]{2,1,0:T(8,128)(2,1)}, bf16[2,64,1024]{2,1,0:T(8,128)(2,1)}, u32[]{:S(2)}, u32[]{:S(2)}) collective-permute-start(bf16[2,64,1024]{2,1,0:T(8,128)(2,1)} %fusion.56), channel_id=1, source_target_pairs={{4,0},{8,4},{12,8},{5,1},{9,5},{13,9},{6,2},{10,6},{14,10},{7,3},{... | collective-permute-start | bytes 786440 | tf_op jit(solution)/shard_map/ppermute | solution.py:23
  253.5 25.3 %copy-start.35 = (bf16[128,1024]{0,1:T(8,128)(2,1)S(1)}, bf16[128,1024]{0,1:T(8,128)(2,1)}, u32[]{:S(2)}) copy-start(bf16[128,1024]{0,1:T(8,128)(2,1)} %copy.162) | copy-start | bytes 786436
  288.2 125.2 %reduce-scatter.3.cloned.1.call-start = ((), (), s32[]{:S(2)}) async-start(), calls=%async_computation.7 | async-start | bytes 7864320 | tf_op jit(solution)/shard_map/reduce_scatter | solution.py:250
  289.6 34.7 %copy-start.11 = (bf16[1,128,1024]{1,2,0:T(8,128)(2,1)S(1)}, bf16[1,128,1024]{1,2,0:T(8,128)(2,1)}, u32[]{:S(2)}) copy-start(bf16[1,128,1024]{1,2,0:T(8,128)(2,1)} %copy-done.10) | copy-start | bytes 786436
  354.8 59.0 %copy-start.20 = (f32[16,64,128]{2,1,0:T(8,128)S(1)}, f32[16,64,128]{2,1,0:T(8,128)}, u32[]{:S(2)}) copy-start(f32[16,64,128]{2,1,0:T(8,128)} %fusion.49) | copy-start | bytes 1572868
  354.8 59.9 %copy-start.39 = (bf16[2,64,16,64]{1,3,2,0:T(8,128)(2,1)S(1)}, bf16[2,64,16,64]{1,3,2,0:T(8,128)(2,1)}, u32[]{:S(2)}) copy-start(bf16[2,64,16,64]{1,3,2,0:T(8,128)(2,1)} %get-tuple-element.93) | copy-start | bytes 786436
  354.8 96.2 %reduce-scatter.5.cloned.1.call-start = ((), (), s32[]{:S(2)}) async-start(), calls=%async_computation.8 | async-start | bytes 1966080 | tf_op jit(solution)/shard_map/reduce_scatter | solution.py:265
  (36 other events, 86.3 us)
Sparse Core Ops, SparseCore 0:
  9.6 48.6 all-gather.3
  59.8 44.9 all-gather.7
  106.4 44.6 all-gather.5
  157.7 34.8 all-reduce.10
  243.1 34.3 all-reduce.6
  288.3 34.6 all-reduce.8
  354.9 58.4 reduce-scatter.2
  415.7 35.2 reduce-scatter.4
where the time goes:
time: 464 us; the launch traced here: 460 us
  waiting for transfers between devices  273 us (59%)
  local copies, waits for them, and re-layouts  69.4 us (15%)
  other arithmetic  42.1 us (9%)
  matrix products  35.3 us (8%)
  between operations  19.4 us (4%)
  blocking collectives  12.1 us (3%)
  starting transfers between devices  8.54 us (2%)
    reduce_scatter x1, waiting for transfers between devices, per_device(): lax.psum_scatter(jnp.concatenate([lax.dot_general(grad, inputs, (((0,), (...  58.3 us
    all_gather x1, waiting for transfers between devices, per_device(): lax.all_gather(w_key, 'dp', axis=0, tiled=True)  44.5 us
    all_gather x1, waiting for transfers between devices, per_device(): lax.all_gather(w_query, 'dp', axis=0, tiled=True)  39.7 us
    all_gather x1, waiting for transfers between devices, per_device(): lax.all_gather(w_value, 'dp', axis=0, tiled=True)  35.5 us
    psum x1, waiting for transfers between devices, per_device(): lax.psum(jnp.stack([part_query_grad.reshape(2 * BLK, model_width), far_gr...  32.3 us
    reduce_scatter x1, waiting for transfers between devices, per_device(): lax.psum_scatter(reduced.astype(jnp.bfloat16), 'dp', scatter_dimension=2,...  22.9 us
    psum x1, waiting for transfers between devices, per_device(): global_sum, global_acc = lax.psum((part_sum, part_out), 'ctx')  21.2 us
    psum x1, waiting for transfers between devices, per_device(): lax.psum(picked.astype(jnp.bfloat16), 'ctx').astype(jnp.float32)  16.9 us
  transfers between devices with their start and end apart: 12, of which 8 were waited for; matrix products, arithmetic and copies ran while one was open for 16% of the time, Pallas kernels for 0%

commit v1 on v0

v1 whole, which is shorter than its diff:
```python
import math

import jax
import jax.numpy as jnp
from jax import lax
from jax.experimental import pallas as pl
from jax.experimental.pallas import tpu as pltpu
from jax.sharding import PartitionSpec as P

HEADS = 16
BLK = 64
NEG = -1e30
SPLIT = 1

NT = (((1,), (1,)), ((), ()))
TN = (((0,), (0,)), ((), ()))
F32 = jnp.float32
BF16 = jnp.bfloat16


def xor_permute(value, axis, bit):
    count = lax.axis_size(axis)
    return lax.ppermute(value, axis, [(i, i ^ bit) for i in range(count)])


def attention_kernel(
    where_ref, chosen_ref, *refs, seqs, chunks, rows, heads, hdim, parts, scale
):
    pieces = seqs * chunks
    token_refs = refs[:pieces]
    up_refs = refs[pieces : 2 * pieces]
    weight_refs = refs[2 * pieces : 2 * pieces + parts]
    context_ref, grad_in_ref, grad_w_ref = refs[2 * pieces + parts : 2 * pieces + parts + 3]
    all_tokens, weight, q_s, k_s, v_s, up_s, dk_s, dv_s, grads = refs[2 * pieces + parts + 3 :]
    length = chunks * rows
    width = heads * hdim
    model = all_tokens.shape[1]
    part_rows = model // parts
    position = where_ref[0]
    line = where_ref[1]

    for j in range(parts):
        start = pl.multiple_of((line ^ j) * part_rows, part_rows)
        weight[pl.ds(start, part_rows), :] = weight_refs[j][...]
    for b in range(pieces):
        all_tokens[b * rows : (b + 1) * rows, :] = token_refs[b][...]
        for h in range(heads):
            up_s[h, b * rows : (b + 1) * rows, :] = up_refs[b][:, h * hdim : (h + 1) * hdim]

    tile = min(256, length)

    @pl.loop(0, seqs * length // tile)
    def _(t):
        at = pl.ds(pl.multiple_of(t * tile, tile), tile)
        out = jnp.dot(all_tokens[at, :], weight[...], preferred_element_type=F32)
        for h in range(heads):
            lo = h * hdim
            q_s[h, at, :] = (out[:, lo : lo + hdim].astype(BF16) * scale).astype(BF16)
            k_s[h, at, :] = out[:, width + lo : width + lo + hdim].astype(BF16)
            v_s[h, at, :] = out[:, 2 * width + lo : 2 * width + lo + hdim].astype(BF16)

    dk_s[...] = jnp.zeros_like(dk_s)
    dv_s[...] = jnp.zeros_like(dv_s)
    blocks_per_chunk = rows // BLK

    @pl.loop(0, pieces)
    def _(b):
        i = b // chunks
        j = b - i * chunks
        at = pl.ds(pl.multiple_of(b * rows, rows), rows)
        keys_at = pl.ds(pl.multiple_of(i * length, length), length)
        first = chosen_ref[2 * i]
        second = chosen_ref[2 * i + 1]
        key_pos = lax.broadcasted_iota(jnp.int32, (length, rows), 0)
        query_pos = lax.broadcasted_iota(jnp.int32, (length, rows), 1)
        key_block = (lax.shift_right_logical(key_pos, int(math.log2(rows))) ^ position) * (
            blocks_per_chunk
        ) + lax.shift_right_logical(key_pos & (rows - 1), int(math.log2(BLK)))
        query_block = (position ^ j) * blocks_per_chunk + lax.shift_right_logical(
            query_pos, int(math.log2(BLK))
        )
        keep = (
            (jnp.abs(key_block - query_block) <= 1)
            | (key_block == first)
            | (key_block == second)
            | (query_block == first)
            | (query_block == second)
        )
        for h in range(heads):
            q = q_s[h, at, :]
            k = k_s[h, keys_at, :]
            v = v_s[h, keys_at, :]
            up = up_s[h, at, :]
            scores = lax.dot_general(k, q, NT, preferred_element_type=F32)
            scores = jnp.where(keep, scores, NEG)
            top = jnp.max(scores, axis=0, keepdims=True)
            raw = jnp.exp(scores - top)
            inverse = 1.0 / jnp.sum(raw, axis=0, keepdims=True)
            out_t = lax.dot_general(v, raw.astype(BF16), TN, preferred_element_type=F32) * inverse
            probs = raw * inverse
            grad_probs = lax.dot_general(v, up, NT, preferred_element_type=F32)
            delta = jnp.sum(jnp.transpose(up.astype(F32)) * out_t, axis=0, keepdims=True)
            low = (probs * (grad_probs - delta)).astype(BF16)
            grad_q = lax.dot_general(k, low, TN, preferred_element_type=F32) * scale
            dk_s[h, keys_at, :] += jnp.dot(low, q, preferred_element_type=F32)
            dv_s[h, keys_at, :] += jnp.dot(probs.astype(BF16), up, preferred_element_type=F32)
            lo = h * hdim
            context_ref[at, lo : lo + hdim] = jnp.transpose(out_t).astype(BF16)
            grads[at, lo : lo + hdim] = jnp.transpose(grad_q).astype(BF16)

    for h in range(heads):
        lo = h * hdim
        grads[:, width + lo : width + lo + hdim] = dk_s[h].astype(BF16)
        grads[:, 2 * width + lo : 2 * width + lo + hdim] = dv_s[h].astype(BF16)

    @pl.loop(0, seqs * length // tile)
    def _(t):
        at = pl.ds(pl.multiple_of(t * tile, tile), tile)
        grad_in_ref[at, :] = lax.dot_general(
            grads[at, :], weight[...], NT, preferred_element_type=F32
        ).astype(BF16)

    @pl.loop(0, parts)
    def _(j):
        cols = pl.ds(pl.multiple_of((line ^ j) * part_rows, part_rows), part_rows)
        grad_w_ref[j] = lax.dot_general(
            all_tokens[:, cols], grads[...], TN, preferred_element_type=F32
        ).astype(BF16)


def per_device(tokens, global_blocks, w_query, w_key, w_value, d_context):
    own_tokens = tokens[0]
    upstream = d_context[0]
    rows, model = own_tokens.shape
    hdim = model // HEADS
    chunks = lax.axis_size("ctx")
    parts = lax.axis_size("dp")
    seqs = SPLIT if HEADS % (SPLIT * chunks) == 0 and parts % SPLIT == 0 else 1
    groups = chunks * seqs
    width = model // groups
    heads = width // hdim
    position = lax.axis_index("ctx")
    line = lax.axis_index("dp")
    side = line % seqs

    hops = [("dp", 1, chunks)] if seqs == 2 else []
    bit = chunks // 2
    while bit:
        hops.append(("ctx", bit, bit))
        bit //= 2

    def slice_of(value, offset):
        which = (position ^ (offset % chunks)) * seqs + (side ^ (offset // chunks))
        return lax.dynamic_slice_in_dim(value, which * width, width, 1)

    sends = []
    for i in range(seqs):
        sends.append(
            jnp.concatenate(
                [slice_of(w, i * chunks) for w in (w_query, w_key, w_value)], axis=1
            )
        )
    weights = [sends[0]]
    for j in range(1, parts):
        weights.append(xor_permute(sends[j % seqs], "dp", j))

    token_pieces = {0: own_tokens}
    up_pieces = {0: jnp.concatenate([slice_of(upstream, o) for o in range(groups)], axis=1)}
    chosen = [global_blocks[0]]
    for axis, bit, offset in hops:
        for key in list(token_pieces):
            token_pieces[key + offset] = xor_permute(token_pieces[key], axis, bit)
        if axis == "dp":
            chosen.append(xor_permute(global_blocks, axis, bit)[0])
        for key in list(up_pieces):
            held = up_pieces[key]
            half = held.shape[1] // 2
            up_pieces[key + offset] = xor_permute(held[:, half:], axis, bit)
            up_pieces[key] = held[:, :half]

    length = chunks * rows
    total = seqs * length
    context, grad_in, grad_w = pl.pallas_call(
        lambda *refs: attention_kernel(
            *refs,
            seqs=seqs,
            chunks=chunks,
            rows=rows,
            heads=heads,
            hdim=hdim,
            parts=parts,
            scale=1.0 / math.sqrt(hdim),
        ),
        out_shape=(
            jax.ShapeDtypeStruct((total, width), BF16),
            jax.ShapeDtypeStruct((total, model), BF16),
            jax.ShapeDtypeStruct((parts, model // parts, 3 * width), BF16),
        ),
        in_specs=[pl.BlockSpec(memory_space=pltpu.SMEM)] * 2
        + [pl.BlockSpec(memory_space=pltpu.VMEM)] * (2 * groups + parts),
        out_specs=(pl.BlockSpec(memory_space=pltpu.VMEM),) * 3,
        scratch_shapes=[
            pltpu.VMEM((total, model), BF16),
            pltpu.VMEM((model, 3 * width), BF16),
            pltpu.VMEM((heads, total, hdim), BF16),
            pltpu.VMEM((heads, total, hdim), BF16),
            pltpu.VMEM((heads, total, hdim), BF16),
            pltpu.VMEM((heads, total, hdim), BF16),
            pltpu.VMEM((heads, total, hdim), F32),
            pltpu.VMEM((heads, total, hdim), F32),
            pltpu.VMEM((total, 3 * width), BF16),
        ],
        compiler_params=pltpu.CompilerParams(vmem_limit_bytes=48 * 1024 * 1024),
        name="attention",
    )(
        jnp.stack([position, line]).astype(jnp.int32),
        jnp.concatenate(chosen),
        *[token_pieces[o] for o in range(groups)],
        *[up_pieces[o] for o in range(groups)],
        *weights,
    )

    moved = [grad_w[0]] + [xor_permute(grad_w[j], "dp", j) for j in range(1, parts)]
    sums = []
    for i in range(seqs):
        acc = moved[i].astype(F32)
        for j in range(i + seqs, parts, seqs):
            acc = acc + moved[j].astype(F32)
        sums.append(acc.reshape(-1, 3, width))
    if seqs == 2:
        low = jnp.where(side == 0, sums[0], sums[1])
        high = jnp.where(side == 0, sums[1], sums[0])
        final = jnp.concatenate([low, high], axis=2)
    else:
        final = sums[0]

    grad_in = grad_in.reshape(groups, rows, model)
    for axis, bit, _ in reversed(hops):
        view = grad_in.reshape(-1, 2, rows, model)
        got = xor_permute(view[:, 1], axis, bit)
        grad_in = (view[:, 0].astype(F32) + got.astype(F32)).astype(BF16)
    grad_tokens = grad_in

    context = context.reshape(groups, rows, width)
    back = [context[0]]
    for o in range(1, groups):
        value = context[o]
        if o % chunks:
            value = xor_permute(value, "ctx", o % chunks)
        if o // chunks:
            value = xor_permute(value, "dp", o // chunks)
        back.append(value)
    stacked = jnp.stack(back)
    index = jnp.arange(groups, dtype=jnp.int32)
    home = ((index // seqs) ^ position) + ((index % seqs) ^ side) * chunks
    full = jnp.take(stacked, home, axis=0)
    full = jnp.transpose(full, (1, 0, 2)).reshape(rows, model)
    return (full[None], grad_tokens, final[:, 0], final[:, 1], final[:, 2])


def solution(mesh):
    return jax.shard_map(
        per_device,
        mesh=mesh,
        in_specs=(
            P(("groups", "dp"), "ctx", None),
            P(("groups", "dp"), None),
            P("dp", None),
            P("dp", None),
            P("dp", None),
            P(("groups", "dp"), "ctx", None),
        ),
        out_specs=(
            P(("groups", "dp"), "ctx", None),
            P(("groups", "dp"), "ctx", None),
            P(("groups", "dp"), "ctx"),
            P(("groups", "dp"), "ctx"),
            P(("groups", "dp"), "ctx"),
        ),
        check_vma=False,
    )
```

time: 464 us -> 117 us (0.25)
  the two profiles are of different devices: /device:TPU:0 before, /device:TPU:8 now
where the time goes in v1:
time: 117 us
  waiting for transfers between devices  56.6 us (48%)
  local copies, waits for them, and re-layouts  27.3 us (23%)
  Pallas kernels  15.7 us (13%)
  starting transfers between devices  11.1 us (9%)
  other arithmetic  5.11 us (4%)
    ppermute x17, waiting for transfers between devices, xor_permute(): return lax.ppermute(value, axis, [(i, i ^ bit) for i in range(count)])  56.6 us
    unnamed x52, local copies, waits for them, and re-layouts  19.1 us
    pallas_call x1, Pallas kernels, per_device(): pl.pallas_call(lambda *refs: attention_kernel(*refs, seqs=seqs, chunks=ch...  15.7 us
    ppermute x17, starting transfers between devices, xor_permute(): return lax.ppermute(value, axis, [(i, i ^ bit) for i in range(count)])  11.1 us
    dynamic_slice x3, local copies, waits for them, and re-layouts, slice_of(): return lax.dynamic_slice_in_dim(value, which * width, width, 1)  2.67 us
  transfers between devices with their start and end apart: 17, of which 9 were waited for; matrix products, arithmetic and copies ran while one was open for 11% of the time, Pallas kernels for 0%

profile of v1, /device:TPU:8, one launch (start us, length us, event | category | flops | bytes accessed | tf_op | source)
XLA Modules:
  0.0 116.7 jit_solution(8166537606267951108)
XLA Ops:
  0.7 1.7 %dynamic-slice_bitcast_fusion.1 = (bf16[128,256]{1,0:T(8,128)(2,1)S(1)}, bf16[128,256]{1,0:T(8,128)(2,1)S(1)}, bf16[128,256]{1,0:T(8,128)(2,1)}, bf16[128,256]{1,0:T(8,128)(2,1)S(1)}) fusion(bf16[1,128,1024]{2,1,0:T(8,128)(2,1)} %param.11, s32[]{:T(128)S(6)} %select_n.61, s32[]{:T(128)S(6)} %select_n.60, s32[]{:T(128)S(6)} %select_n.59, s32[]{:T(128)S(6)} %select_n.62), kind=kLoop, calls=%fused_computation.25 | loop fusion | bytes 524304 | tf_op jit(solution)/shard_map/dynamic_slice | solution.py:154
  2.4 1.6 %collective-permute-start.4 = (bf16[128,512]{1,0:T(8,128)(2,1)S(1)}, bf16[128,512]{1,0:T(8,128)(2,1)S(1)}, u32[]{:S(2)}, u32[]{:S(2)}) collective-permute-start(bf16[128,512]{1,0:T(8,128)(2,1)S(1)} %pad_maximum_fusion.2), channel_id=1, source_target_pairs={{0,8},{4,12},{8,0},{12,4},{1,9},{5,13},{9,1},{13,5},{2,10},{6,14},... | collective-permute-start | bytes 393224 | tf_op jit(solution)/shard_map/ppermute | solution.py:23
  3.9 1.0 constant_dynamic-slice_fusion
  5.5 2.6 %collective-permute-start.7 = (bf16[256,768]{1,0:T(8,128)(2,1)S(1)}, bf16[256,768]{1,0:T(8,128)(2,1)S(1)}, u32[]{:S(2)}, u32[]{:S(2)}) collective-permute-start(bf16[256,768]{1,0:T(8,128)(2,1)S(1)} %pad_maximum_fusion.refs_10_), channel_id=1, source_target_pairs={{0,2},{1,3},{2,0},{3,1},{4,6},{5,7},{6,4},{7,5},{8,10},{9,11},{10,... | collective-permute-start | bytes 1179656 | tf_op jit(solution)/shard_map/ppermute | solution.py:23
  10.6 1.1 collective-permute-done.5.refs_9_
  12.5 4.8 %collective-permute-done.1.refs_4_ = bf16[128,1024]{1,0:T(8,128)(2,1)S(1)} collective-permute-done((bf16[128,1024]{1,0:T(8,128)(2,1)S(1)}, bf16[128,1024]{1,0:T(8,128)(2,1)S(1)}, u32[]{:S(2)}, u32[]{:S(2)}) %collective-permute-start.1) | collective-permute-done | bytes 262176 | tf_op jit(solution)/shard_map/ppermute | solution.py:23
  18.8 2.3 %collective-permute-done.6.refs_11_ = bf16[256,768]{1,0:T(8,128)(2,1)S(1)} collective-permute-done((bf16[256,768]{1,0:T(8,128)(2,1)S(1)}, bf16[256,768]{1,0:T(8,128)(2,1)S(1)}, u32[]{:S(2)}, u32[]{:S(2)}) %collective-permute-start.6) | collective-permute-done | bytes 393248 | tf_op jit(solution)/shard_map/ppermute | solution.py:23
  21.9 12.7 %collective-permute-done.7.refs_12_ = bf16[256,768]{1,0:T(8,128)(2,1)S(1)} collective-permute-done((bf16[256,768]{1,0:T(8,128)(2,1)S(1)}, bf16[256,768]{1,0:T(8,128)(2,1)S(1)}, u32[]{:S(2)}, u32[]{:S(2)}) %collective-permute-start.7) | collective-permute-done | bytes 393248 | tf_op jit(solution)/shard_map/ppermute | solution.py:23
  35.3 6.8 %collective-permute-done.8.refs_13_ = bf16[256,768]{1,0:T(8,128)(2,1)S(1)} collective-permute-done((bf16[256,768]{1,0:T(8,128)(2,1)S(1)}, bf16[256,768]{1,0:T(8,128)(2,1)S(1)}, u32[]{:S(2)}, u32[]{:S(2)}) %collective-permute-start.8) | collective-permute-done | bytes 393248 | tf_op jit(solution)/shard_map/ppermute | solution.py:23
  43.6 1.0 copy-done.2
  44.6 1.0 copy-done.4
  45.6 1.0 copy-done.6
  53.7 15.7 %attention.1 = (bf16[512,256]{1,0:T(8,128)(2,1)S(1)}, bf16[512,1024]{1,0:T(8,128)(2,1)S(1)}, bf16[4,256,768]{2,1,0:T(8,128)(2,1)S(1)}) custom-call(s32[2]{0:T(128)S(1)} %pad_add_fusion.refs_0_, s32[2]{0:T(128)S(1)} %bitcast.64, bf16[128,1024]{1,0:T(8,128)(2,1)S(1)} %bitcast.63, bf16[128,1024]{1,0:T(8,128)(2,1)S(1)} %copy-done.12, ...), custom_call_target="tpu_custom_call" | custom-call | tf_op jit(solution)/shard_map/attention/pallas_call | solution.py:183
  70.9 1.3 %collective-permute-start.11 = (bf16[128,256]{1,0:T(8,128)(2,1)S(1)}, bf16[128,256]{1,0:T(8,128)(2,1)S(1)}, u32[]{:S(2)}, u32[]{:S(2)}) collective-permute-start(bf16[128,256]{1,0:T(8,128)(2,1)S(1)} %get-tuple-element.23), channel_id=1, source_target_pairs={{0,12},{4,8},{8,4},{12,0},{1,13},{5,9},{9,5},{13,1},{2,14},{6,10},... | collective-permute-start | bytes 196616 | tf_op jit(solution)/shard_map/ppermute | solution.py:23
  72.5 1.1 slice_bitcast_fusion.4
  73.5 1.7 %collective-permute-done.10 = bf16[128,256]{1,0:T(8,128)(2,1)S(1)} collective-permute-done((bf16[128,256]{1,0:T(8,128)(2,1)S(1)}, bf16[128,256]{1,0:T(8,128)(2,1)S(1)}, u32[]{:S(2)}, u32[]{:S(2)}) %collective-permute-start.10) | collective-permute-done | bytes 65568 | tf_op jit(solution)/shard_map/ppermute | solution.py:23
  75.2 1.3 %collective-permute-start.15 = (bf16[256,768]{1,0:T(8,128)(2,1)}, bf16[256,768]{1,0:T(8,128)(2,1)}, u32[]{:S(2)}, u32[]{:S(2)}) collective-permute-start(bf16[256,768]{1,0:T(8,128)(2,1)} %get-tuple-element.18), channel_id=1, source_target_pairs={{0,2},{1,3},{2,0},{3,1},{4,6},{5,7},{6,4},{7,5},{8,10},{9,11},{10,... | collective-permute-start | bytes 1179656 | tf_op jit(solution)/shard_map/ppermute | solution.py:23
  78.2 1.5 %gather_fusion = bf16[4,128,256]{2,1,0:T(8,128)(2,1)S(1)} fusion(bf16[4,128,256]{2,1,0:T(8,128)(2,1)} %pad_maximum_fusion.1, s32[1024]{0:T(1024)S(1)} %pad_clamp_fusion), kind=kCustom, calls=%fused_computation | custom fusion | bytes 524304 | tf_op jit(solution)/shard_map/jit(_take)/gather | solution.py:256
  80.5 1.1 copy.16
  82.5 1.2 %fusion.3 = bf16[1,2,128,1024]{3,2,1,0:T(8,128)(2,1)S(1)} fusion(bf16[2,128,1024]{2,1,0:T(8,128)(2,1)} %collective-permute-done.12, bf16[2,2,128,1024]{3,2,1,0:T(8,128)(2,1)S(1)} %bitcast.60), kind=kLoop, calls=%fused_computation.6 | loop fusion | flops 1048576 | bytes 1572864 | tf_op jit(solution)/shard_map/reshape | solution.py:239
  84.5 6.3 %collective-permute-done.14 = bf16[256,768]{1,0:T(8,128)(2,1)} collective-permute-done((bf16[256,768]{1,0:T(8,128)(2,1)}, bf16[256,768]{1,0:T(8,128)(2,1)}, u32[]{:S(2)}, u32[]{:S(2)}) %collective-permute-start.14) | collective-permute-done | bytes 393248 | tf_op jit(solution)/shard_map/ppermute | solution.py:23
  90.8 12.5 %collective-permute-done.15 = bf16[256,768]{1,0:T(8,128)(2,1)} collective-permute-done((bf16[256,768]{1,0:T(8,128)(2,1)}, bf16[256,768]{1,0:T(8,128)(2,1)}, u32[]{:S(2)}, u32[]{:S(2)}) %collective-permute-start.15) | collective-permute-done | bytes 393248 | tf_op jit(solution)/shard_map/ppermute | solution.py:23
  103.2 8.4 %collective-permute-done.16 = bf16[256,768]{1,0:T(8,128)(2,1)} collective-permute-done((bf16[256,768]{1,0:T(8,128)(2,1)}, bf16[256,768]{1,0:T(8,128)(2,1)}, u32[]{:S(2)}, u32[]{:S(2)}) %collective-permute-start.16) | collective-permute-done | bytes 393248 | tf_op jit(solution)/shard_map/ppermute | solution.py:23
  111.6 1.4 %fusion.2 = f32[256,768]{1,0:T(8,128)S(1)} fusion(bf16[256,768]{1,0:T(8,128)(2,1)} %collective-permute-done.16, bf16[256,768]{1,0:T(8,128)(2,1)} %collective-permute-done.15, bf16[256,768]{1,0:T(8,128)(2,1)} %collective-permute-done.14, bf16[4,256,768]{2,1,0:T(8,128)(2,1)S(1)} %get-tuple-element.10), kind=kLoop, calls=%fused_computation.5 | loop fusion | flops 1376256 | bytes 2359296 | tf_op jit(solution)/shard_map/add | solution.py:228
  (86 shorter events, 24.8 us)
Async XLA Ops:
  0.6 4.3 %copy-start = (bf16[256,1024]{1,0:T(8,128)(2,1)S(1)}, bf16[256,1024]{1,0:T(8,128)(2,1)}, u32[]{:S(2)}) copy-start(bf16[256,1024]{1,0:T(8,128)(2,1)} %param.8) | copy-start | bytes 1572868
  0.6 7.9 %copy-start.7 = (bf16[1,128,1024]{2,1,0:T(8,128)(2,1)S(1)}, bf16[1,128,1024]{2,1,0:T(8,128)(2,1)}, u32[]{:S(2)}) copy-start(bf16[1,128,1024]{2,1,0:T(8,128)(2,1)} %param.6) | copy-start | bytes 786436
  0.7 42.9 %copy-start.21 = (s32[1,2]{1,0:T(1,128)S(1)}, s32[1,2]{1,0:T(1,128)}, u32[]{:S(2)}) copy-start(s32[1,2]{1,0:T(1,128)} %param.7) | copy-start | bytes 28
  2.4 6.2 %collective-permute-start.4 = (bf16[128,512]{1,0:T(8,128)(2,1)S(1)}, bf16[128,512]{1,0:T(8,128)(2,1)S(1)}, u32[]{:S(2)}, u32[]{:S(2)}) collective-permute-start(bf16[128,512]{1,0:T(8,128)(2,1)S(1)} %pad_maximum_fusion.2), channel_id=1, source_target_pairs={{0,8},{4,12},{8,0},{12,4},{1,9},{5,13},{9,1},{13,5},{2,10},{6,14},... | collective-permute-start | bytes 393224 | tf_op jit(solution)/shard_map/ppermute | solution.py:23
  5.0 16.1 %collective-permute-start.6 = (bf16[256,768]{1,0:T(8,128)(2,1)S(1)}, bf16[256,768]{1,0:T(8,128)(2,1)S(1)}, u32[]{:S(2)}, u32[]{:S(2)}) collective-permute-start(bf16[256,768]{1,0:T(8,128)(2,1)S(1)} %pad_maximum_fusion.refs_10_), channel_id=1, source_target_pairs={{0,1},{1,0},{2,3},{3,2},{4,5},{5,4},{6,7},{7,6},{8,9},{9,8},{10,11... | collective-permute-start | bytes 1179656 | tf_op jit(solution)/shard_map/ppermute | solution.py:23
  5.5 29.0 %collective-permute-start.7 = (bf16[256,768]{1,0:T(8,128)(2,1)S(1)}, bf16[256,768]{1,0:T(8,128)(2,1)S(1)}, u32[]{:S(2)}, u32[]{:S(2)}) collective-permute-start(bf16[256,768]{1,0:T(8,128)(2,1)S(1)} %pad_maximum_fusion.refs_10_), channel_id=1, source_target_pairs={{0,2},{1,3},{2,0},{3,1},{4,6},{5,7},{6,4},{7,5},{8,10},{9,11},{10,... | collective-permute-start | bytes 1179656 | tf_op jit(solution)/shard_map/ppermute | solution.py:23
  8.1 34.0 %collective-permute-start.8 = (bf16[256,768]{1,0:T(8,128)(2,1)S(1)}, bf16[256,768]{1,0:T(8,128)(2,1)S(1)}, u32[]{:S(2)}, u32[]{:S(2)}) collective-permute-start(bf16[256,768]{1,0:T(8,128)(2,1)S(1)} %pad_maximum_fusion.refs_10_), channel_id=1, source_target_pairs={{0,3},{1,2},{2,1},{3,0},{4,7},{5,6},{6,5},{7,4},{8,11},{9,10},{10,... | collective-permute-start | bytes 1179656 | tf_op jit(solution)/shard_map/ppermute | solution.py:23
  8.5 1.3 %collective-permute-start.3 = (bf16[128,256]{1,0:T(8,128)(2,1)S(1)}, bf16[128,256]{1,0:T(8,128)(2,1)S(1)}, u32[]{:S(2)}, u32[]{:S(2)}) collective-permute-start(bf16[128,256]{1,0:T(8,128)(2,1)S(1)} %get-tuple-element.27), channel_id=1, source_target_pairs={{0,4},{4,0},{8,12},{12,8},{1,5},{5,1},{9,13},{13,9},{2,6},{6,2},{1... | collective-permute-start | bytes 196616 | tf_op jit(solution)/shard_map/ppermute | solution.py:23
  8.6 8.7 %collective-permute-start.1 = (bf16[128,1024]{1,0:T(8,128)(2,1)S(1)}, bf16[128,1024]{1,0:T(8,128)(2,1)S(1)}, u32[]{:S(2)}, u32[]{:S(2)}) collective-permute-start(bf16[128,1024]{1,0:T(8,128)(2,1)S(1)} %bitcast.61), channel_id=1, source_target_pairs={{0,8},{4,12},{8,0},{12,4},{1,9},{5,13},{9,1},{13,5},{2,10},{6,14},... | collective-permute-start | bytes 786440 | tf_op jit(solution)/shard_map/ppermute | solution.py:23
  10.4 1.3 %collective-permute-start.5 = (bf16[128,256]{1,0:T(8,128)(2,1)S(1)}, bf16[128,256]{1,0:T(8,128)(2,1)S(1)}, u32[]{:S(2)}, u32[]{:S(2)}) collective-permute-start(bf16[128,256]{1,0:T(8,128)(2,1)S(1)} %get-tuple-element.30), channel_id=1, source_target_pairs={{0,4},{4,0},{8,12},{12,8},{1,5},{5,1},{9,13},{13,9},{2,6},{6,2},{1... | collective-permute-start | bytes 196616 | tf_op jit(solution)/shard_map/ppermute | solution.py:23
  12.3 5.8 %collective-permute-start = (bf16[128,1024]{1,0:T(8,128)(2,1)S(1)}, bf16[128,1024]{1,0:T(8,128)(2,1)S(1)}, u32[]{:S(2)}, u32[]{:S(2)}) collective-permute-start(bf16[128,1024]{1,0:T(8,128)(2,1)S(1)} %bitcast.62), channel_id=1, source_target_pairs={{0,4},{4,0},{8,12},{12,8},{1,5},{5,1},{9,13},{13,9},{2,6},{6,2},{1... | collective-permute-start | bytes 786440 | tf_op jit(solution)/shard_map/ppermute | solution.py:23
  17.3 25.6 %collective-permute-start.2 = (bf16[128,1024]{1,0:T(8,128)(2,1)S(1)}, bf16[128,1024]{1,0:T(8,128)(2,1)S(1)}, u32[]{:S(2)}, u32[]{:S(2)}) collective-permute-start(bf16[128,1024]{1,0:T(8,128)(2,1)S(1)} %collective-permute-done.1.refs_4_), channel_id=1, source_target_pairs={{0,4},{4,0},{8,12},{12,8},{1,5},{5,1},{9,13},{13,9},{2,6},{6,2},{1... | collective-permute-start | bytes 786440 | tf_op jit(solution)/shard_map/ppermute | solution.py:23
  43.6 1.0 copy-start.2
  44.6 1.0 copy-start.4
  70.2 12.2 %collective-permute-start.12 = (bf16[2,128,1024]{2,1,0:T(8,128)(2,1)}, bf16[2,128,1024]{2,1,0:T(8,128)(2,1)}, u32[]{:S(2)}, u32[]{:S(2)}) collective-permute-start(bf16[2,128,1024]{2,1,0:T(8,128)(2,1)} %slice_bitcast_fusion), channel_id=1, source_target_pairs={{0,4},{4,0},{8,12},{12,8},{1,5},{5,1},{9,13},{13,9},{2,6},{6,2},{1... | collective-permute-start | bytes 1572872 | tf_op jit(solution)/shard_map/ppermute | solution.py:23
  70.3 5.0 %collective-permute-start.10 = (bf16[128,256]{1,0:T(8,128)(2,1)S(1)}, bf16[128,256]{1,0:T(8,128)(2,1)S(1)}, u32[]{:S(2)}, u32[]{:S(2)}) collective-permute-start(bf16[128,256]{1,0:T(8,128)(2,1)S(1)} %get-tuple-element.24), channel_id=1, source_target_pairs={{0,8},{4,12},{8,0},{12,4},{1,9},{5,13},{9,1},{13,5},{2,10},{6,14},... | collective-permute-start | bytes 196616 | tf_op jit(solution)/shard_map/ppermute | solution.py:23
  70.9 5.7 %collective-permute-start.11 = (bf16[128,256]{1,0:T(8,128)(2,1)S(1)}, bf16[128,256]{1,0:T(8,128)(2,1)S(1)}, u32[]{:S(2)}, u32[]{:S(2)}) collective-permute-start(bf16[128,256]{1,0:T(8,128)(2,1)S(1)} %get-tuple-element.23), channel_id=1, source_target_pairs={{0,12},{4,8},{8,4},{12,0},{1,13},{5,9},{9,5},{13,1},{2,14},{6,10},... | collective-permute-start | bytes 196616 | tf_op jit(solution)/shard_map/ppermute | solution.py:23
  72.2 5.2 %collective-permute-start.9 = (bf16[128,256]{1,0:T(8,128)(2,1)S(1)}, bf16[128,256]{1,0:T(8,128)(2,1)S(1)}, u32[]{:S(2)}, u32[]{:S(2)}) collective-permute-start(bf16[128,256]{1,0:T(8,128)(2,1)S(1)} %get-tuple-element.25), channel_id=1, source_target_pairs={{0,4},{4,0},{8,12},{12,8},{1,5},{5,1},{9,13},{13,9},{2,6},{6,2},{1... | collective-permute-start | bytes 196616 | tf_op jit(solution)/shard_map/ppermute | solution.py:23
  73.5 17.2 %collective-permute-start.14 = (bf16[256,768]{1,0:T(8,128)(2,1)}, bf16[256,768]{1,0:T(8,128)(2,1)}, u32[]{:S(2)}, u32[]{:S(2)}) collective-permute-start(bf16[256,768]{1,0:T(8,128)(2,1)} %get-tuple-element.16), channel_id=1, source_target_pairs={{0,1},{1,0},{2,3},{3,2},{4,5},{5,4},{6,7},{7,6},{8,9},{9,8},{10,11... | collective-permute-start | bytes 1179656 | tf_op jit(solution)/shard_map/ppermute | solution.py:23
  75.2 28.0 %collective-permute-start.15 = (bf16[256,768]{1,0:T(8,128)(2,1)}, bf16[256,768]{1,0:T(8,128)(2,1)}, u32[]{:S(2)}, u32[]{:S(2)}) collective-permute-start(bf16[256,768]{1,0:T(8,128)(2,1)} %get-tuple-element.18), channel_id=1, source_target_pairs={{0,2},{1,3},{2,0},{3,1},{4,6},{5,7},{6,4},{7,5},{8,10},{9,11},{10,... | collective-permute-start | bytes 1179656 | tf_op jit(solution)/shard_map/ppermute | solution.py:23
  76.6 35.0 %collective-permute-start.16 = (bf16[256,768]{1,0:T(8,128)(2,1)}, bf16[256,768]{1,0:T(8,128)(2,1)}, u32[]{:S(2)}, u32[]{:S(2)}) collective-permute-start(bf16[256,768]{1,0:T(8,128)(2,1)} %get-tuple-element.17), channel_id=1, source_target_pairs={{0,3},{1,2},{2,1},{3,0},{4,7},{5,6},{6,5},{7,4},{8,11},{9,10},{10,... | collective-permute-start | bytes 1179656 | tf_op jit(solution)/shard_map/ppermute | solution.py:23
  83.7 27.9 %copy-start.22 = (bf16[1,2,128,1024]{3,2,1,0:T(8,128)(2,1)}, bf16[1,2,128,1024]{3,2,1,0:T(8,128)(2,1)S(1)}, u32[]{:S(2)}) copy-start(bf16[1,2,128,1024]{3,2,1,0:T(8,128)(2,1)S(1)} %fusion.3) | copy-start | bytes 1572868
  83.8 32.2 %collective-permute-start.13 = (bf16[1,128,1024]{2,1,0:T(8,128)(2,1)S(1)}, bf16[1,128,1024]{2,1,0:T(8,128)(2,1)S(1)}, u32[]{:S(2)}, u32[]{:S(2)}) collective-permute-start(bf16[1,128,1024]{2,1,0:T(8,128)(2,1)S(1)} %slice_bitcast_fusion.8), channel_id=1, source_target_pairs={{0,8},{4,12},{8,0},{12,4},{1,9},{5,13},{9,1},{13,5},{2,10},{6,14},... | collective-permute-start | bytes 786440 | tf_op jit(solution)/shard_map/ppermute | solution.py:23
  113.3 2.6 %copy-start.23 = (bf16[1,2,128,1024]{3,2,1,0:T(8,128)(2,1)S(1)}, bf16[1,2,128,1024]{3,2,1,0:T(8,128)(2,1)}, u32[]{:S(2)}) copy-start(bf16[1,2,128,1024]{3,2,1,0:T(8,128)(2,1)} %copy-done.22) | copy-start | bytes 1572868
  (17 other events, 13.8 us)

commit v2 on v1

--- a/solution.py
+++ b/solution.py
@@ -10,7 +10,7 @@
 HEADS = 16
 BLK = 64
 NEG = -1e30
-SPLIT = 1
+SPLIT = 2
 
 NT = (((1,), (1,)), ((), ()))
 TN = (((0,), (0,)), ((), ()))
@@ -24,14 +24,19 @@
 
 
 def attention_kernel(
-    where_ref, chosen_ref, *refs, seqs, chunks, rows, heads, hdim, parts, scale
+    where_ref, chosen_ref, *refs, seqs, chunks, rows, heads, hdim, parts, scale, up_starts
 ):
     pieces = seqs * chunks
+    half = pieces // 2
     token_refs = refs[:pieces]
     up_refs = refs[pieces : 2 * pieces]
     weight_refs = refs[2 * pieces : 2 * pieces + parts]
-    context_ref, grad_in_ref, grad_w_ref = refs[2 * pieces + parts : 2 * pieces + parts + 3]
-    all_tokens, weight, q_s, k_s, v_s, up_s, dk_s, dv_s, grads = refs[2 * pieces + parts + 3 :]
+    outs = refs[2 * pieces + parts :]
+    grad_w_refs = outs[:parts]
+    keep_ref, send_ref = outs[parts : parts + 2]
+    all_tokens, weight, up_all, q_s, k_s, v_s, up_s, dk_s, dv_s, grads, context_s, sems = outs[
+        parts + 2 :
+    ]
     length = chunks * rows
     width = heads * hdim
     model = all_tokens.shape[1]
@@ -39,13 +44,26 @@
     position = where_ref[0]
     line = where_ref[1]
 
+    copies = []
     for j in range(parts):
         start = pl.multiple_of((line ^ j) * part_rows, part_rows)
-        weight[pl.ds(start, part_rows), :] = weight_refs[j][...]
+        copies.append((weight_refs[j], weight.at[pl.ds(start, part_rows), :]))
     for b in range(pieces):
-        all_tokens[b * rows : (b + 1) * rows, :] = token_refs[b][...]
-        for h in range(heads):
-            up_s[h, b * rows : (b + 1) * rows, :] = up_refs[b][:, h * hdim : (h + 1) * hdim]
+        copies.append((token_refs[b].at[:, :model], all_tokens.at[pl.ds(b * rows, rows), :]))
+    for b in range(pieces):
+        source = up_refs[b]
+        start = up_starts[b]
+        copies.append((source.at[:, start : start + width], up_all.at[pl.ds(b * rows, rows), :]))
+    copies = [
+        pltpu.make_async_copy(source, target, sems.at[index])
+        for index, (source, target) in enumerate(copies)
+    ]
+    for copy in copies:
+        copy.start()
+    for copy in copies:
+        copy.wait()
+    for h in range(heads):
+        up_s[h] = up_all[:, h * hdim : (h + 1) * hdim]
 
     tile = min(256, length)
 
@@ -105,7 +123,7 @@
             dk_s[h, keys_at, :] += jnp.dot(low, q, preferred_element_type=F32)
             dv_s[h, keys_at, :] += jnp.dot(probs.astype(BF16), up, preferred_element_type=F32)
             lo = h * hdim
-            context_ref[at, lo : lo + hdim] = jnp.transpose(out_t).astype(BF16)
+            context_s[at, lo : lo + hdim] = jnp.transpose(out_t).astype(BF16)
             grads[at, lo : lo + hdim] = jnp.transpose(grad_q).astype(BF16)
 
     for h in range(heads):
@@ -113,19 +131,80 @@
         grads[:, width + lo : width + lo + hdim] = dk_s[h].astype(BF16)
         grads[:, 2 * width + lo : 2 * width + lo + hdim] = dv_s[h].astype(BF16)
 
-    @pl.loop(0, seqs * length // tile)
-    def _(t):
-        at = pl.ds(pl.multiple_of(t * tile, tile), tile)
-        grad_in_ref[at, :] = lax.dot_general(
-            grads[at, :], weight[...], NT, preferred_element_type=F32
-        ).astype(BF16)
-
-    @pl.loop(0, parts)
-    def _(j):
+    for j in range(parts):
         cols = pl.ds(pl.multiple_of((line ^ j) * part_rows, part_rows), part_rows)
-        grad_w_ref[j] = lax.dot_general(
+        grad_w_refs[j][...] = lax.dot_general(
             all_tokens[:, cols], grads[...], TN, preferred_element_type=F32
         ).astype(BF16)
+
+    @pl.loop(0, half)
+    def _(t):
+        at = pl.ds(pl.multiple_of(t * 2 * rows, 2 * rows), 2 * rows)
+        out = lax.dot_general(grads[at, :], weight[...], NT, preferred_element_type=F32)
+        keep_ref[t, :, :model] = out[:rows].astype(BF16)
+        send_ref[t, :, :model] = out[rows:].astype(BF16)
+        keep_ref[t, :, model:] = context_s[pl.ds(pl.multiple_of(t * 2 * rows, rows), rows), :]
+        send_ref[t, :, model:] = context_s[
+            pl.ds(pl.multiple_of(t * 2 * rows + rows, rows), rows), :
+        ]
+
+
+def add_and_join(mine, theirs, model):
+    total = (mine[:, :model].astype(F32) + theirs[:, :model].astype(F32)).astype(BF16)
+    return [total, mine[:, model:], theirs[:, model:]]
+
+
+def combine_kernel(*refs, model):
+    count = len(refs) - 2
+    keep_ref, got_ref = refs[:2]
+    for t in range(count):
+        out_ref = refs[2 + t]
+        lo = 0
+        for value in add_and_join(keep_ref[t], got_ref[t], model):
+            out_ref[:, lo : lo + value.shape[1]] = value
+            lo += value.shape[1]
+
+
+def join_kernel(mine_ref, theirs_ref, out_ref, *, model):
+    lo = 0
+    for value in add_and_join(mine_ref[...], theirs_ref[...], model):
+        out_ref[:, lo : lo + value.shape[1]] = value
+        lo += value.shape[1]
+
+
+def final_kernel(where_ref, mine_ref, theirs_ref, grad_ref, context_ref, *, model, seqs, chunks):
+    total, mine, theirs = add_and_join(mine_ref[...], theirs_ref[...], model)
+    grad_ref[...] = total
+    groups = seqs * chunks
+    width = model // groups
+    values = [mine[:, k * width : (k + 1) * width] for k in range(groups // 2)]
+    values += [theirs[:, k * width : (k + 1) * width] for k in range(groups // 2)]
+    own = where_ref[0] + where_ref[2] * chunks
+    bit = 1
+    while bit < groups:
+        flip = (own & bit) != 0
+        values = [jnp.where(flip, values[o ^ bit], values[o]) for o in range(groups)]
+        bit *= 2
+    for o in range(groups):
+        lo = ((o % chunks) * seqs + o // chunks) * width
+        context_ref[:, lo : lo + width] = values[o]
+
+
+def sum_kernel(where_ref, *refs, parts, seqs, width):
+    outs = refs[parts:]
+    for m in range(3):
+        sums = []
+        for i in range(seqs):
+            acc = refs[i][:, m * width : (m + 1) * width].astype(F32)
+            for j in range(i + seqs, parts, seqs):
+                acc = acc + refs[j][:, m * width : (m + 1) * width].astype(F32)
+            sums.append(acc)
+        if seqs == 1:
+            outs[m][...] = sums[0]
+        else:
+            flip = where_ref[2] != 0
+            outs[m][:, :width] = jnp.where(flip, sums[1], sums[0])
+            outs[m][:, width:] = jnp.where(flip, sums[0], sums[1])
 
 
 def per_device(tokens, global_blocks, w_query, w_key, w_value, d_context):
@@ -143,6 +222,7 @@
     line = lax.axis_index("dp")
     side = line % seqs
 
+    where = jnp.stack([position, line, side]).astype(jnp.int32)
     hops = [("dp", 1, chunks)] if seqs == 2 else []
     bit = chunks // 2
     while bit:
@@ -164,23 +244,34 @@
     for j in range(1, parts):
         weights.append(xor_permute(sends[j % seqs], "dp", j))
 
-    token_pieces = {0: own_tokens}
-    up_pieces = {0: jnp.concatenate([slice_of(upstream, o) for o in range(groups)], axis=1)}
+    ups = [slice_of(upstream, o) for o in range(groups)]
+    pieces = {0: None}
     chosen = [global_blocks[0]]
+    left = groups
     for axis, bit, offset in hops:
-        for key in list(token_pieces):
-            token_pieces[key + offset] = xor_permute(token_pieces[key], axis, bit)
+        left //= 2
+        for key in list(pieces):
+            held = pieces[key]
+            if held is None:
+                send = [own_tokens] + ups[left : 2 * left]
+            else:
+                lo = model + left * width
+                send = [held[:, :model], held[:, lo : lo + left * width]]
+            pieces[key + offset] = xor_permute(jnp.concatenate(send, axis=1), axis, bit)
         if axis == "dp":
             chosen.append(xor_permute(global_blocks, axis, bit)[0])
-        for key in list(up_pieces):
-            held = up_pieces[key]
-            half = held.shape[1] // 2
-            up_pieces[key + offset] = xor_permute(held[:, half:], axis, bit)
-            up_pieces[key] = held[:, :half]
+    token_pieces = [own_tokens] + [pieces[o] for o in range(1, groups)]
+    if width % 128 == 0:
+        up_pieces = [ups[0]] + token_pieces[1:]
+        up_starts = [0] + [model] * (groups - 1)
+    else:
+        up_pieces = [ups[0]] + [v[:, model : model + width] for v in token_pieces[1:]]
+        token_pieces = [v[:, :model] for v in token_pieces]
+        up_starts = [0] * groups
 
     length = chunks * rows
     total = seqs * length
-    context, grad_in, grad_w = pl.pallas_call(
+    results = pl.pallas_call(
         lambda *refs: attention_kernel(
             *refs,
             seqs=seqs,
@@ -190,18 +281,17 @@
             hdim=hdim,
             parts=parts,
             scale=1.0 / math.sqrt(hdim),
+            up_starts=up_starts,
         ),
-        out_shape=(
-            jax.ShapeDtypeStruct((total, width), BF16),
-            jax.ShapeDtypeStruct((total, model), BF16),
-            jax.ShapeDtypeStruct((parts, model // parts, 3 * width), BF16),
-        ),
+        out_shape=(jax.ShapeDtypeStruct((model // parts, 3 * width), BF16),) * parts
+        + (jax.ShapeDtypeStruct((groups // 2, rows, model + width), BF16),) * 2,
         in_specs=[pl.BlockSpec(memory_space=pltpu.SMEM)] * 2
-        + [pl.BlockSpec(memory_space=pltpu.VMEM)] * (2 * groups + parts),
-        out_specs=(pl.BlockSpec(memory_space=pltpu.VMEM),) * 3,
+        + [pl.BlockSpec(memory_space=pl.ANY)] * (2 * groups + parts),
+        out_specs=(pl.BlockSpec(memory_space=pltpu.VMEM),) * (parts + 2),
         scratch_shapes=[
             pltpu.VMEM((total, model), BF16),
             pltpu.VMEM((model, 3 * width), BF16),
+            pltpu.VMEM((total, width), BF16),
             pltpu.VMEM((heads, total, hdim), BF16),
             pltpu.VMEM((heads, total, hdim), BF16),
             pltpu.VMEM((heads, total, hdim), BF16),
@@ -209,53 +299,65 @@
             pltpu.VMEM((heads, total, hdim), F32),
             pltpu.VMEM((heads, total, hdim), F32),
             pltpu.VMEM((total, 3 * width), BF16),
+            pltpu.VMEM((total, width), BF16),
+            pltpu.SemaphoreType.DMA((2 * groups + parts,)),
         ],
         compiler_params=pltpu.CompilerParams(vmem_limit_bytes=48 * 1024 * 1024),
         name="attention",
     )(
-        jnp.stack([position, line]).astype(jnp.int32),
+        where,
         jnp.concatenate(chosen),
-        *[token_pieces[o] for o in range(groups)],
-        *[up_pieces[o] for o in range(groups)],
+        *token_pieces,
+        *up_pieces,
         *weights,
     )
-
+    grad_w = results[:parts]
+    keep, send = results[parts:]
+    smem = pl.BlockSpec(memory_space=pltpu.SMEM)
+    vmem = pl.BlockSpec(memory_space=pltpu.VMEM)
+
+    axis, bit, _ = hops[-1]
+    got = xor_permute(send, axis, bit)
     moved = [grad_w[0]] + [xor_permute(grad_w[j], "dp", j) for j in range(1, parts)]
-    sums = []
-    for i in range(seqs):
-        acc = moved[i].astype(F32)
-        for j in range(i + seqs, parts, seqs):
-            acc = acc + moved[j].astype(F32)
-        sums.append(acc.reshape(-1, 3, width))
-    if seqs == 2:
-        low = jnp.where(side == 0, sums[0], sums[1])
-        high = jnp.where(side == 0, sums[1], sums[0])
-        final = jnp.concatenate([low, high], axis=2)
-    else:
-        final = sums[0]
-
-    grad_in = grad_in.reshape(groups, rows, model)
-    for axis, bit, _ in reversed(hops):
-        view = grad_in.reshape(-1, 2, rows, model)
-        got = xor_permute(view[:, 1], axis, bit)
-        grad_in = (view[:, 0].astype(F32) + got.astype(F32)).astype(BF16)
-    grad_tokens = grad_in
-
-    context = context.reshape(groups, rows, width)
-    back = [context[0]]
-    for o in range(1, groups):
-        value = context[o]
-        if o % chunks:
-            value = xor_permute(value, "ctx", o % chunks)
-        if o // chunks:
-            value = xor_permute(value, "dp", o // chunks)
-        back.append(value)
-    stacked = jnp.stack(back)
-    index = jnp.arange(groups, dtype=jnp.int32)
-    home = ((index // seqs) ^ position) + ((index % seqs) ^ side) * chunks
-    full = jnp.take(stacked, home, axis=0)
-    full = jnp.transpose(full, (1, 0, 2)).reshape(rows, model)
-    return (full[None], grad_tokens, final[:, 0], final[:, 1], final[:, 2])
+    columns = model + 2 * width
+    held = pl.pallas_call(
+        lambda *refs: combine_kernel(*refs, model=model),
+        out_shape=(jax.ShapeDtypeStruct((rows, columns), BF16),) * (groups // 2),
+        in_specs=[vmem] * 2,
+        out_specs=(vmem,) * (groups // 2),
+        name="combine",
+    )(keep, got)
+    held = list(held)
+    for axis, bit, offset in reversed(hops[:-1]):
+        arrived = [xor_permute(value, axis, bit) for value in reversed(held[1::2])][::-1]
+        held = held[::2]
+        if len(held) == 1:
+            break
+        columns = 2 * columns - model
+        held = [
+            pl.pallas_call(
+                lambda *refs: join_kernel(*refs, model=model),
+                out_shape=jax.ShapeDtypeStruct((rows, columns), BF16),
+                in_specs=[vmem] * 2,
+                out_specs=vmem,
+                name="join",
+            )(mine, theirs)
+            for mine, theirs in zip(held, arrived)
+        ]
+    grad_tokens, context = pl.pallas_call(
+        lambda *refs: final_kernel(*refs, model=model, seqs=seqs, chunks=chunks),
+        out_shape=(jax.ShapeDtypeStruct((rows, model), BF16),) * 2,
+        in_specs=[smem, vmem, vmem],
+        name="rows_out",
+    )(where, held[0], arrived[0])
+
+    final = pl.pallas_call(
+        lambda *refs: sum_kernel(*refs, parts=parts, seqs=seqs, width=width),
+        out_shape=(jax.ShapeDtypeStruct((model // parts, seqs * width), F32),) * 3,
+        in_specs=[smem] + [vmem] * parts,
+        name="weights_out",
+    )(where, *moved)
+    return (context[None], grad_tokens[None], *final)
 
 
 def solution(mesh):

time: 117 us -> 117 us (level)
  the two profiles are of different devices: /device:TPU:8 before, /device:TPU:0 now
where the time goes in v2:
time: 117 us; the launch traced here: 116 us
  waiting for transfers between devices  56.6 us (48%)
  Pallas kernels  31 us (26%)
  starting transfers between devices  19.6 us (17%)
  local copies, waits for them, and re-layouts  7.84 us (7%)
    ppermute x18, waiting for transfers between devices, xor_permute(): return lax.ppermute(value, axis, [(i, i ^ bit) for i in range(count)])  56.6 us
    pallas_call x1, Pallas kernels, per_device(): pl.pallas_call(lambda *refs: attention_kernel(*refs, seqs=seqs, chunks=ch...  20.3 us
    ppermute x18, starting transfers between devices, xor_permute(): return lax.ppermute(value, axis, [(i, i ^ bit) for i in range(count)])  19.6 us
    unnamed x30, local copies, waits for them, and re-layouts  5.85 us
    pallas_call x2, Pallas kernels, per_device(): pl.pallas_call(lambda *refs: join_kernel(*refs, model=model), out_shape=j...  3.76 us
    pallas_call x1, Pallas kernels, per_device(): pl.pallas_call(lambda *refs: combine_kernel(*refs, model=model), out_shap...  2.75 us
  transfers between devices with their start and end apart: 18, of which 7 were waited for; matrix products, arithmetic and copies ran while one was open for 2% of the time, Pallas kernels for 3%

profile of v2, /device:TPU:0, one launch (start us, length us, event | category | flops | bytes accessed | tf_op | source)
XLA Modules:
  0.0 116.3 jit_solution(655872089111348631)
XLA Ops:
  0.7 3.1 %collective-permute-start = (s32[1,2]{1,0:T(1,128)}, s32[1,2]{1,0:T(1,128)S(1)}, u32[]{:S(2)}, u32[]{:S(2)}) collective-permute-start(s32[1,2]{1,0:T(1,128)} %param.7), channel_id=1, source_target_pairs={{0,1},{1,0},{2,3},{3,2},{4,5},{5,4},{6,7},{7,6},{8,9},{9,8},{10,11... | collective-permute-start | bytes 32 | tf_op jit(solution)/shard_map/ppermute | solution.py:23
  5.6 2.7 %collective-permute-start.9 = (bf16[256,384]{1,0:T(8,128)(2,1)S(1)}, bf16[256,384]{1,0:T(8,128)(2,1)S(1)}, u32[]{:S(2)}, u32[]{:S(2)}) collective-permute-start(bf16[256,384]{1,0:T(8,128)(2,1)S(1)} %pad_maximum_fusion.6.refs_18_), channel_id=1, source_target_pairs={{0,2},{1,3},{2,0},{3,1},{4,6},{5,7},{6,4},{7,5},{8,10},{9,11},{10,... | collective-permute-start | bytes 589832 | tf_op jit(solution)/shard_map/ppermute | solution.py:23
  9.1 1.6 %collective-permute-start.2 = (bf16[128,1280]{1,0:T(8,128)(2,1)S(1)}, bf16[128,1280]{1,0:T(8,128)(2,1)S(1)}, u32[]{:S(2)}, u32[]{:S(2)}) collective-permute-start(bf16[128,1280]{1,0:T(8,128)(2,1)S(1)} %pad_maximum_fusion), channel_id=1, source_target_pairs={{0,8},{4,12},{8,0},{12,4},{1,9},{5,13},{9,1},{13,5},{2,10},{6,14},... | collective-permute-start | bytes 983048 | tf_op jit(solution)/shard_map/ppermute | solution.py:23
  10.6 1.4 %collective-permute-start.10 = (bf16[256,384]{1,0:T(8,128)(2,1)S(1)}, bf16[256,384]{1,0:T(8,128)(2,1)S(1)}, u32[]{:S(2)}, u32[]{:S(2)}) collective-permute-start(bf16[256,384]{1,0:T(8,128)(2,1)S(1)} %pad_maximum_fusion.7), channel_id=1, source_target_pairs={{0,3},{1,2},{2,1},{3,0},{4,7},{5,6},{6,5},{7,4},{8,11},{9,10},{10,... | collective-permute-start | bytes 589832 | tf_op jit(solution)/shard_map/ppermute | solution.py:23
  12.1 5.6 %collective-permute-done.2.refs_4_.refs_12_ = bf16[128,1280]{1,0:T(8,128)(2,1)S(1)} collective-permute-done((bf16[128,1280]{1,0:T(8,128)(2,1)S(1)}, bf16[128,1280]{1,0:T(8,128)(2,1)S(1)}, u32[]{:S(2)}, u32[]{:S(2)}) %collective-permute-start.2) | collective-permute-done | bytes 327712 | tf_op jit(solution)/shard_map/ppermute | solution.py:23
  17.8 9.4 %collective-permute-done.4.refs_6_.refs_14_ = bf16[128,1536]{1,0:T(8,128)(2,1)S(1)} collective-permute-done((bf16[128,1536]{1,0:T(8,128)(2,1)S(1)}, bf16[128,1536]{1,0:T(8,128)(2,1)S(1)}, u32[]{:S(2)}, u32[]{:S(2)}) %collective-permute-start.4) | collective-permute-done | bytes 393248 | tf_op jit(solution)/shard_map/ppermute | solution.py:23
  27.2 1.6 %collective-permute-start.6 = (bf16[128,1280]{1,0:T(8,128)(2,1)S(1)}, bf16[128,1280]{1,0:T(8,128)(2,1)S(1)}, u32[]{:S(2)}, u32[]{:S(2)}) collective-permute-start(bf16[128,1280]{1,0:T(8,128)(2,1)S(1)} %pad_maximum_fusion.1), channel_id=1, source_target_pairs={{0,8},{4,12},{8,0},{12,4},{1,9},{5,13},{9,1},{13,5},{2,10},{6,14},... | collective-permute-start | bytes 983048 | tf_op jit(solution)/shard_map/ppermute | solution.py:23
  28.9 6.4 %collective-permute-done.6.refs_8_.refs_16_ = bf16[128,1280]{1,0:T(8,128)(2,1)S(1)} collective-permute-done((bf16[128,1280]{1,0:T(8,128)(2,1)S(1)}, bf16[128,1280]{1,0:T(8,128)(2,1)S(1)}, u32[]{:S(2)}, u32[]{:S(2)}) %collective-permute-start.6) | collective-permute-done | bytes 327712 | tf_op jit(solution)/shard_map/ppermute | solution.py:23
  36.2 7.1 %collective-permute-done.8.refs_19_ = bf16[256,384]{1,0:T(8,128)(2,1)S(1)} collective-permute-done((bf16[256,384]{1,0:T(8,128)(2,1)S(1)}, bf16[256,384]{1,0:T(8,128)(2,1)S(1)}, u32[]{:S(2)}, u32[]{:S(2)}) %collective-permute-start.8) | collective-permute-done | bytes 196640 | tf_op jit(solution)/shard_map/ppermute | solution.py:23
  43.3 20.3 %attention.1 = (bf16[256,384]{1,0:T(8,128)(2,1)S(1)}, bf16[256,384]{1,0:T(8,128)(2,1)S(1)}, bf16[256,384]{1,0:T(8,128)(2,1)S(1)}, bf16[256,384]{1,0:T(8,128)(2,1...) custom-call(s32[3]{0:T(128)S(1)} %pad_add_fusion.refs_0_, s32[4]{0:T(128)S(1)} %pad_add_fusion.1.refs_1_, ...), custom_call_target="tpu_custom_call" | custom-call | tf_op jit(solution)/shard_map/attention/pallas_call | solution.py:274
  63.7 1.0 copy-done.1
  65.4 3.1 %collective-permute-done.11.refs_1_ = bf16[4,128,1152]{2,1,0:T(8,128)(2,1)S(1)} collective-permute-done((bf16[4,128,1152]{2,1,0:T(8,128)(2,1)}, bf16[4,128,1152]{2,1,0:T(8,128)(2,1)S(1)}, u32[]{:S(2)}, u32[]{:S(2)}) %collective-permute-start.11) | collective-permute-done | bytes 1179680 | tf_op jit(solution)/shard_map/ppermute | solution.py:23
  68.4 1.0 copy-done.4
  69.5 2.8 %combine.1 = (bf16[128,1280]{1,0:T(8,128)(2,1)}, bf16[128,1280]{1,0:T(8,128)(2,1)}, bf16[128,1280]{1,0:T(8,128)(2,1)}, bf16[128,1280]{1,0:T(8,128)(2,1)}) custom-call(bf16[4,128,1152]{2,1,0:T(8,128)(2,1)} %copy-done.1, bf16[4,128,1152]{2,1,0:T(8,128)(2,1)} %copy-done.4), custom_call_target="tpu_custom_call" | custom-call | tf_op jit(solution)/shard_map/combine/pallas_call | solution.py:323
  72.2 1.7 %collective-permute-start.13 = (bf16[128,1280]{1,0:T(8,128)(2,1)}, bf16[128,1280]{1,0:T(8,128)(2,1)S(1)}, u32[]{:S(2)}, u32[]{:S(2)}) collective-permute-start(bf16[128,1280]{1,0:T(8,128)(2,1)} %get-tuple-element.25), channel_id=1, source_target_pairs={{0,8},{4,12},{8,0},{12,4},{1,9},{5,13},{9,1},{13,5},{2,10},{6,14},... | collective-permute-start | bytes 983048 | tf_op jit(solution)/shard_map/ppermute | solution.py:23
  74.0 8.2 %collective-permute-done.13.refs_1_ = bf16[128,1280]{1,0:T(8,128)(2,1)S(1)} collective-permute-done((bf16[128,1280]{1,0:T(8,128)(2,1)}, bf16[128,1280]{1,0:T(8,128)(2,1)S(1)}, u32[]{:S(2)}, u32[]{:S(2)}) %collective-permute-start.13) | collective-permute-done | bytes 327712 | tf_op jit(solution)/shard_map/ppermute | solution.py:23
  82.9 1.9 %join.3 = bf16[128,1536]{1,0:T(8,128)(2,1)} custom-call(bf16[128,1280]{1,0:T(8,128)(2,1)} %get-tuple-element.24.refs_0_, bf16[128,1280]{1,0:T(8,128)(2,1)} %copy-done.7), custom_call_target="tpu_custom_call" | custom-call | tf_op jit(solution)/shard_map/join/pallas_call | solution.py:338
  85.1 1.7 %collective-permute-start.12 = (bf16[128,1280]{1,0:T(8,128)(2,1)}, bf16[128,1280]{1,0:T(8,128)(2,1)S(1)}, u32[]{:S(2)}, u32[]{:S(2)}) collective-permute-start(bf16[128,1280]{1,0:T(8,128)(2,1)} %get-tuple-element.23), channel_id=1, source_target_pairs={{0,8},{4,12},{8,0},{12,4},{1,9},{5,13},{9,1},{13,5},{2,10},{6,14},... | collective-permute-start | bytes 983048 | tf_op jit(solution)/shard_map/ppermute | solution.py:23
  86.8 1.8 %collective-permute-start.15 = (bf16[256,384]{1,0:T(8,128)(2,1)S(1)}, bf16[256,384]{1,0:T(8,128)(2,1)S(1)}, u32[]{:S(2)}, u32[]{:S(2)}) collective-permute-start(bf16[256,384]{1,0:T(8,128)(2,1)S(1)} %get-tuple-element.29), channel_id=1, source_target_pairs={{0,1},{1,0},{2,3},{3,2},{4,5},{5,4},{6,7},{7,6},{8,9},{9,8},{10,11... | collective-permute-start | bytes 589832 | tf_op jit(solution)/shard_map/ppermute | solution.py:23
  88.6 2.6 %collective-permute-start.17 = (bf16[256,384]{1,0:T(8,128)(2,1)S(1)}, bf16[256,384]{1,0:T(8,128)(2,1)S(1)}, u32[]{:S(2)}, u32[]{:S(2)}) collective-permute-start(bf16[256,384]{1,0:T(8,128)(2,1)S(1)} %get-tuple-element.31), channel_id=1, source_target_pairs={{0,3},{1,2},{2,1},{3,0},{4,7},{5,6},{6,5},{7,4},{8,11},{9,10},{10,... | collective-permute-start | bytes 589832 | tf_op jit(solution)/shard_map/ppermute | solution.py:23
  91.2 16.8 %collective-permute-done.15.refs_2_ = bf16[256,384]{1,0:T(8,128)(2,1)S(1)} collective-permute-done((bf16[256,384]{1,0:T(8,128)(2,1)S(1)}, bf16[256,384]{1,0:T(8,128)(2,1)S(1)}, u32[]{:S(2)}, u32[]{:S(2)}) %collective-permute-start.15) | collective-permute-done | bytes 196640 | tf_op jit(solution)/shard_map/ppermute | solution.py:23
  108.8 2.1 %weights_out.1 = (f32[256,256]{1,0:T(8,128)}, f32[256,256]{1,0:T(8,128)}, f32[256,256]{1,0:T(8,128)}) custom-call(s32[3]{0:T(128)} %copy-done.3, bf16[256,384]{1,0:T(8,128)(2,1)} %copy-done.2, bf16[256,384]{1,0:T(8,128)(2,1)} %copy-done.9, bf16[256,384]{1,0:T(8,128)(2,1)} %copy-done.10, bf16[256,384]{1,0:T(8,128)(2,1)} %copy-done.11), custom_call_target="tpu_custom_call" | custom-call | tf_op jit(solution)/shard_map/weights_out/pallas_call | solution.py:354
  111.7 1.9 %join.2.refs_1_ = bf16[128,1536]{1,0:T(8,128)(2,1)} custom-call(bf16[128,1280]{1,0:T(8,128)(2,1)} %get-tuple-element.22.refs_0_, bf16[128,1280]{1,0:T(8,128)(2,1)} %copy-done.6), custom_call_target="tpu_custom_call" | custom-call | tf_op jit(solution)/shard_map/join/pallas_call | solution.py:338
  114.3 2.0 %rows_out.1 = (bf16[128,1024]{1,0:T(8,128)(2,1)}, bf16[128,1024]{1,0:T(8,128)(2,1)}) custom-call(s32[3]{0:T(128)} %copy-done.3, bf16[128,1536]{1,0:T(8,128)(2,1)} %join.2.refs_1_, bf16[128,1536]{1,0:T(8,128)(2,1)} %copy-done.5), custom_call_target="tpu_custom_call" | custom-call | tf_op jit(solution)/shard_map/rows_out/pallas_call | solution.py:347
  (69 shorter events, 7.6 us)
Async XLA Ops:
  0.6 7.7 %copy-start = (bf16[1,128,1024]{2,1,0:T(8,128)(2,1)S(1)}, bf16[1,128,1024]{2,1,0:T(8,128)(2,1)}, u32[]{:S(2)}) copy-start(bf16[1,128,1024]{2,1,0:T(8,128)(2,1)} %param.6) | copy-start | bytes 786436
  0.6 7.7 %copy-start.8 = (bf16[1,128,1024]{2,1,0:T(8,128)(2,1)S(1)}, bf16[1,128,1024]{2,1,0:T(8,128)(2,1)}, u32[]{:S(2)}) copy-start(bf16[1,128,1024]{2,1,0:T(8,128)(2,1)} %param.11) | copy-start | bytes 786436
  0.7 34.7 %collective-permute-start = (s32[1,2]{1,0:T(1,128)}, s32[1,2]{1,0:T(1,128)S(1)}, u32[]{:S(2)}, u32[]{:S(2)}) collective-permute-start(s32[1,2]{1,0:T(1,128)} %param.7), channel_id=1, source_target_pairs={{0,1},{1,0},{2,3},{3,2},{4,5},{5,4},{6,7},{7,6},{8,9},{9,8},{10,11... | collective-permute-start | bytes 32 | tf_op jit(solution)/shard_map/ppermute | solution.py:23
  5.6 30.3 %collective-permute-start.9 = (bf16[256,384]{1,0:T(8,128)(2,1)S(1)}, bf16[256,384]{1,0:T(8,128)(2,1)S(1)}, u32[]{:S(2)}, u32[]{:S(2)}) collective-permute-start(bf16[256,384]{1,0:T(8,128)(2,1)S(1)} %pad_maximum_fusion.6.refs_18_), channel_id=1, source_target_pairs={{0,2},{1,3},{2,0},{3,1},{4,6},{5,7},{6,4},{7,5},{8,10},{9,11},{10,... | collective-permute-start | bytes 589832 | tf_op jit(solution)/shard_map/ppermute | solution.py:23
  8.5 18.7 %collective-permute-start.4 = (bf16[128,1536]{1,0:T(8,128)(2,1)S(1)}, bf16[128,1536]{1,0:T(8,128)(2,1)S(1)}, u32[]{:S(2)}, u32[]{:S(2)}) collective-permute-start(bf16[128,1536]{1,0:T(8,128)(2,1)S(1)} %bitcast_dynamic-update-slice_fusion), channel_id=1, source_target_pairs={{0,1},{1,0},{2,3},{3,2},{4,5},{5,4},{6,7},{7,6},{8,9},{9,8},{10,11... | collective-permute-start | bytes 1179656 | tf_op jit(solution)/shard_map/ppermute | solution.py:23
  9.1 8.7 %collective-permute-start.2 = (bf16[128,1280]{1,0:T(8,128)(2,1)S(1)}, bf16[128,1280]{1,0:T(8,128)(2,1)S(1)}, u32[]{:S(2)}, u32[]{:S(2)}) collective-permute-start(bf16[128,1280]{1,0:T(8,128)(2,1)S(1)} %pad_maximum_fusion), channel_id=1, source_target_pairs={{0,8},{4,12},{8,0},{12,4},{1,9},{5,13},{9,1},{13,5},{2,10},{6,14},... | collective-permute-start | bytes 983048 | tf_op jit(solution)/shard_map/ppermute | solution.py:23
  10.6 25.4 %collective-permute-start.10 = (bf16[256,384]{1,0:T(8,128)(2,1)S(1)}, bf16[256,384]{1,0:T(8,128)(2,1)S(1)}, u32[]{:S(2)}, u32[]{:S(2)}) collective-permute-start(bf16[256,384]{1,0:T(8,128)(2,1)S(1)} %pad_maximum_fusion.7), channel_id=1, source_target_pairs={{0,3},{1,2},{2,1},{3,0},{4,7},{5,6},{6,5},{7,4},{8,11},{9,10},{10,... | collective-permute-start | bytes 589832 | tf_op jit(solution)/shard_map/ppermute | solution.py:23
  17.7 25.6 %collective-permute-start.1 = (bf16[128,1152]{1,0:T(8,128)(2,1)S(1)}, bf16[128,1152]{1,0:T(8,128)(2,1)S(1)}, u32[]{:S(2)}, u32[]{:S(2)}) collective-permute-start(bf16[128,1152]{1,0:T(8,128)(2,1)S(1)} %pad_maximum_fusion.2), channel_id=1, source_target_pairs={{0,4},{4,0},{8,12},{12,8},{1,5},{5,1},{9,13},{13,9},{2,6},{6,2},{1... | collective-permute-start | bytes 884744 | tf_op jit(solution)/shard_map/ppermute | solution.py:23
  27.2 8.9 %copy-start.12 = (s32[1,2]{1,0:T(1,128)S(1)}, s32[1,2]{1,0:T(1,128)}, u32[]{:S(2)}) copy-start(s32[1,2]{1,0:T(1,128)} %param.7) | copy-start | bytes 28
  27.2 8.1 %collective-permute-start.6 = (bf16[128,1280]{1,0:T(8,128)(2,1)S(1)}, bf16[128,1280]{1,0:T(8,128)(2,1)S(1)}, u32[]{:S(2)}, u32[]{:S(2)}) collective-permute-start(bf16[128,1280]{1,0:T(8,128)(2,1)S(1)} %pad_maximum_fusion.1), channel_id=1, source_target_pairs={{0,8},{4,12},{8,0},{12,4},{1,9},{5,13},{9,1},{13,5},{2,10},{6,14},... | collective-permute-start | bytes 983048 | tf_op jit(solution)/shard_map/ppermute | solution.py:23
  35.3 8.0 %collective-permute-start.3 = (bf16[128,1152]{1,0:T(8,128)(2,1)S(1)}, bf16[128,1152]{1,0:T(8,128)(2,1)S(1)}, u32[]{:S(2)}, u32[]{:S(2)}) collective-permute-start(bf16[128,1152]{1,0:T(8,128)(2,1)S(1)} %pad_maximum_fusion.3), channel_id=1, source_target_pairs={{0,4},{4,0},{8,12},{12,8},{1,5},{5,1},{9,13},{13,9},{2,6},{6,2},{1... | collective-permute-start | bytes 884744 | tf_op jit(solution)/shard_map/ppermute | solution.py:23
  35.4 7.9 %collective-permute-start.5 = (bf16[128,1152]{1,0:T(8,128)(2,1)S(1)}, bf16[128,1152]{1,0:T(8,128)(2,1)S(1)}, u32[]{:S(2)}, u32[]{:S(2)}) collective-permute-start(bf16[128,1152]{1,0:T(8,128)(2,1)S(1)} %pad_maximum_fusion.4), channel_id=1, source_target_pairs={{0,4},{4,0},{8,12},{12,8},{1,5},{5,1},{9,13},{13,9},{2,6},{6,2},{1... | collective-permute-start | bytes 884744 | tf_op jit(solution)/shard_map/ppermute | solution.py:23
  36.0 7.4 %collective-permute-start.7 = (bf16[128,1152]{1,0:T(8,128)(2,1)S(1)}, bf16[128,1152]{1,0:T(8,128)(2,1)S(1)}, u32[]{:S(2)}, u32[]{:S(2)}) collective-permute-start(bf16[128,1152]{1,0:T(8,128)(2,1)S(1)} %pad_maximum_fusion.5), channel_id=1, source_target_pairs={{0,4},{4,0},{8,12},{12,8},{1,5},{5,1},{9,13},{13,9},{2,6},{6,2},{1... | collective-permute-start | bytes 884744 | tf_op jit(solution)/shard_map/ppermute | solution.py:23
  36.0 7.2 %collective-permute-start.8 = (bf16[256,384]{1,0:T(8,128)(2,1)S(1)}, bf16[256,384]{1,0:T(8,128)(2,1)S(1)}, u32[]{:S(2)}, u32[]{:S(2)}) collective-permute-start(bf16[256,384]{1,0:T(8,128)(2,1)S(1)} %pad_maximum_fusion.7), channel_id=1, source_target_pairs={{0,1},{1,0},{2,3},{3,2},{4,5},{5,4},{6,7},{7,6},{8,9},{9,8},{10,11... | collective-permute-start | bytes 589832 | tf_op jit(solution)/shard_map/ppermute | solution.py:23
  36.1 27.5 %copy-start.3 = (s32[3]{0:T(128)}, s32[3]{0:T(128)S(1)}, u32[]{:S(2)}) copy-start(s32[3]{0:T(128)S(1)} %pad_add_fusion.refs_0_) | copy-start | bytes 40
  63.7 1.0 copy-start.1
  65.4 3.1 %collective-permute-start.11 = (bf16[4,128,1152]{2,1,0:T(8,128)(2,1)}, bf16[4,128,1152]{2,1,0:T(8,128)(2,1)S(1)}, u32[]{:S(2)}, u32[]{:S(2)}) collective-permute-start(bf16[4,128,1152]{2,1,0:T(8,128)(2,1)} %get-tuple-element.21), channel_id=1, source_target_pairs={{0,4},{4,0},{8,12},{12,8},{1,5},{5,1},{9,13},{13,9},{2,6},{6,2},{1... | collective-permute-start | bytes 3538952 | tf_op jit(solution)/shard_map/ppermute | solution.py:23
  68.4 1.0 copy-start.4
  72.2 10.0 %collective-permute-start.13 = (bf16[128,1280]{1,0:T(8,128)(2,1)}, bf16[128,1280]{1,0:T(8,128)(2,1)S(1)}, u32[]{:S(2)}, u32[]{:S(2)}) collective-permute-start(bf16[128,1280]{1,0:T(8,128)(2,1)} %get-tuple-element.25), channel_id=1, source_target_pairs={{0,8},{4,12},{8,0},{12,4},{1,9},{5,13},{9,1},{13,5},{2,10},{6,14},... | collective-permute-start | bytes 983048 | tf_op jit(solution)/shard_map/ppermute | solution.py:23
  84.8 28.7 %collective-permute-start.14 = (bf16[128,1536]{1,0:T(8,128)(2,1)}, bf16[128,1536]{1,0:T(8,128)(2,1)S(1)}, u32[]{:S(2)}, u32[]{:S(2)}) collective-permute-start(bf16[128,1536]{1,0:T(8,128)(2,1)} %join.3), channel_id=1, source_target_pairs={{0,1},{1,0},{2,3},{3,2},{4,5},{5,4},{6,7},{7,6},{8,9},{9,8},{10,11... | collective-permute-start | bytes 1179656 | tf_op jit(solution)/shard_map/ppermute | solution.py:23
  85.1 25.9 %collective-permute-start.12 = (bf16[128,1280]{1,0:T(8,128)(2,1)}, bf16[128,1280]{1,0:T(8,128)(2,1)S(1)}, u32[]{:S(2)}, u32[]{:S(2)}) collective-permute-start(bf16[128,1280]{1,0:T(8,128)(2,1)} %get-tuple-element.23), channel_id=1, source_target_pairs={{0,8},{4,12},{8,0},{12,4},{1,9},{5,13},{9,1},{13,5},{2,10},{6,14},... | collective-permute-start | bytes 983048 | tf_op jit(solution)/shard_map/ppermute | solution.py:23
  86.8 21.2 %collective-permute-start.15 = (bf16[256,384]{1,0:T(8,128)(2,1)S(1)}, bf16[256,384]{1,0:T(8,128)(2,1)S(1)}, u32[]{:S(2)}, u32[]{:S(2)}) collective-permute-start(bf16[256,384]{1,0:T(8,128)(2,1)S(1)} %get-tuple-element.29), channel_id=1, source_target_pairs={{0,1},{1,0},{2,3},{3,2},{4,5},{5,4},{6,7},{7,6},{8,9},{9,8},{10,11... | collective-permute-start | bytes 589832 | tf_op jit(solution)/shard_map/ppermute | solution.py:23
  88.6 19.4 %collective-permute-start.16 = (bf16[256,384]{1,0:T(8,128)(2,1)S(1)}, bf16[256,384]{1,0:T(8,128)(2,1)S(1)}, u32[]{:S(2)}, u32[]{:S(2)}) collective-permute-start(bf16[256,384]{1,0:T(8,128)(2,1)S(1)} %get-tuple-element.30), channel_id=1, source_target_pairs={{0,2},{1,3},{2,0},{3,1},{4,6},{5,7},{6,4},{7,5},{8,10},{9,11},{10,... | collective-permute-start | bytes 589832 | tf_op jit(solution)/shard_map/ppermute | solution.py:23
  88.6 19.4 %collective-permute-start.17 = (bf16[256,384]{1,0:T(8,128)(2,1)S(1)}, bf16[256,384]{1,0:T(8,128)(2,1)S(1)}, u32[]{:S(2)}, u32[]{:S(2)}) collective-permute-start(bf16[256,384]{1,0:T(8,128)(2,1)S(1)} %get-tuple-element.31), channel_id=1, source_target_pairs={{0,3},{1,2},{2,1},{3,0},{4,7},{5,6},{6,5},{7,4},{8,11},{9,10},{10,... | collective-permute-start | bytes 589832 | tf_op jit(solution)/shard_map/ppermute | solution.py:23
  (7 other events, 5.1 us)

commit v3 on v2

--- a/solution.py
+++ b/solution.py
@@ -11,11 +11,21 @@
 BLK = 64
 NEG = -1e30
 SPLIT = 2
+SPAN = 4
 
 NT = (((1,), (1,)), ((), ()))
 TN = (((0,), (0,)), ((), ()))
 F32 = jnp.float32
 BF16 = jnp.bfloat16
+
+
+SMALL = pltpu.CompilerParams(vmem_limit_bytes=8 * 1024 * 1024)
+
+
+def cost(micros):
+    return pl.CostEstimate(
+        flops=0, transcendentals=0, bytes_accessed=int(micros * 3_000_000)
+    )
 
 
 def xor_permute(value, axis, bit):
@@ -34,7 +44,7 @@
     outs = refs[2 * pieces + parts :]
     grad_w_refs = outs[:parts]
     keep_ref, send_ref = outs[parts : parts + 2]
-    all_tokens, weight, up_all, q_s, k_s, v_s, up_s, dk_s, dv_s, grads, context_s, sems = outs[
+    all_tokens, weight, up_all, kv_s, kvt_s, pair_s, dkv_s, grads, context_s, sems = outs[
         parts + 2 :
     ]
     length = chunks * rows
@@ -62,10 +72,10 @@
         copy.start()
     for copy in copies:
         copy.wait()
-    for h in range(heads):
-        up_s[h] = up_all[:, h * hdim : (h + 1) * hdim]
-
-    tile = min(256, length)
+    pair_s[...] = jnp.zeros_like(pair_s)
+    if SPAN < chunks:
+        dkv_s[...] = jnp.zeros_like(dkv_s)
+    tile = min(512, length)
 
     @pl.loop(0, seqs * length // tile)
     def _(t):
@@ -73,63 +83,110 @@
         out = jnp.dot(all_tokens[at, :], weight[...], preferred_element_type=F32)
         for h in range(heads):
             lo = h * hdim
-            q_s[h, at, :] = (out[:, lo : lo + hdim].astype(BF16) * scale).astype(BF16)
-            k_s[h, at, :] = out[:, width + lo : width + lo + hdim].astype(BF16)
-            v_s[h, at, :] = out[:, 2 * width + lo : 2 * width + lo + hdim].astype(BF16)
-
-    dk_s[...] = jnp.zeros_like(dk_s)
-    dv_s[...] = jnp.zeros_like(dv_s)
+            kv = jnp.concatenate(
+                [
+                    out[:, width + lo : width + lo + hdim],
+                    out[:, 2 * width + lo : 2 * width + lo + hdim],
+                ],
+                axis=1,
+            )
+            kv_s[h, at, :] = kv.astype(BF16)
+            kvt_s[h, :, at] = jnp.transpose(kv).astype(BF16)
+            q = (out[:, lo : lo + hdim].astype(BF16) * scale).astype(BF16)
+            for p in range(tile // rows):
+                pair_s[h, t * (tile // rows) + p, :rows, :hdim] = q[p * rows : (p + 1) * rows]
+    for h in range(heads):
+        for b in range(pieces):
+            pair_s[h, b, rows:, hdim:] = up_all[
+                b * rows : (b + 1) * rows, h * hdim : (h + 1) * hdim
+            ]
+
     blocks_per_chunk = rows // BLK
-
-    @pl.loop(0, pieces)
-    def _(b):
-        i = b // chunks
-        j = b - i * chunks
-        at = pl.ds(pl.multiple_of(b * rows, rows), rows)
+    block_count = length // BLK
+    log_blocks = int(math.log2(blocks_per_chunk))
+
+    span = min(SPAN, chunks)
+
+    @pl.loop(0, pieces // span)
+    def _(t):
+        i = t // (chunks // span)
         keys_at = pl.ds(pl.multiple_of(i * length, length), length)
         first = chosen_ref[2 * i]
         second = chosen_ref[2 * i + 1]
-        key_pos = lax.broadcasted_iota(jnp.int32, (length, rows), 0)
-        query_pos = lax.broadcasted_iota(jnp.int32, (length, rows), 1)
-        key_block = (lax.shift_right_logical(key_pos, int(math.log2(rows))) ^ position) * (
-            blocks_per_chunk
-        ) + lax.shift_right_logical(key_pos & (rows - 1), int(math.log2(BLK)))
-        query_block = (position ^ j) * blocks_per_chunk + lax.shift_right_logical(
-            query_pos, int(math.log2(BLK))
+        shape = (block_count, 1, rows)
+        key = lax.broadcasted_iota(jnp.int32, shape, 0)
+        key_block = (lax.shift_right_logical(key, log_blocks) ^ position) * blocks_per_chunk + (
+            key & (blocks_per_chunk - 1)
         )
-        keep = (
-            (jnp.abs(key_block - query_block) <= 1)
-            | (key_block == first)
-            | (key_block == second)
-            | (query_block == first)
-            | (query_block == second)
+        offset = lax.shift_right_logical(
+            lax.broadcasted_iota(jnp.int32, shape, 2), int(math.log2(BLK))
         )
+        biases = []
+        for p in range(span):
+            j = t * span + p - i * chunks
+            query_block = (position ^ j) * blocks_per_chunk + offset
+            keep = (
+                (jnp.abs(key_block - query_block) <= 1)
+                | (key_block == first)
+                | (key_block == second)
+                | (query_block == first)
+                | (query_block == second)
+            )
+            biases.append(jnp.where(keep, 0.0, NEG))
         for h in range(heads):
-            q = q_s[h, at, :]
-            k = k_s[h, keys_at, :]
-            v = v_s[h, keys_at, :]
-            up = up_s[h, at, :]
-            scores = lax.dot_general(k, q, NT, preferred_element_type=F32)
-            scores = jnp.where(keep, scores, NEG)
-            top = jnp.max(scores, axis=0, keepdims=True)
-            raw = jnp.exp(scores - top)
-            inverse = 1.0 / jnp.sum(raw, axis=0, keepdims=True)
-            out_t = lax.dot_general(v, raw.astype(BF16), TN, preferred_element_type=F32) * inverse
-            probs = raw * inverse
-            grad_probs = lax.dot_general(v, up, NT, preferred_element_type=F32)
-            delta = jnp.sum(jnp.transpose(up.astype(F32)) * out_t, axis=0, keepdims=True)
-            low = (probs * (grad_probs - delta)).astype(BF16)
-            grad_q = lax.dot_general(k, low, TN, preferred_element_type=F32) * scale
-            dk_s[h, keys_at, :] += jnp.dot(low, q, preferred_element_type=F32)
-            dv_s[h, keys_at, :] += jnp.dot(probs.astype(BF16), up, preferred_element_type=F32)
+            pair = pair_s[h, pl.ds(t * span, span)].reshape(span * 2 * rows, 2 * hdim)
+            both = lax.dot_general(kv_s[h, keys_at, :], pair, NT, preferred_element_type=F32)
+            parts_of = [both[:, p * rows : (p + 1) * rows] for p in range(2 * span)]
+            forward = []
+            backward = []
+            inverses = []
+            for p in range(span):
+                scores = parts_of[2 * p].reshape(block_count, BLK, rows) + biases[p]
+                scores = scores.reshape(length, rows)
+                grad_probs = parts_of[2 * p + 1]
+                raw = jnp.exp(scores - jnp.max(scores, axis=0, keepdims=True))
+                inverse = 1.0 / jnp.sum(raw, axis=0, keepdims=True)
+                raw_low = raw.astype(BF16)
+                probs = raw * inverse
+                delta = inverse * jnp.sum(
+                    raw_low.astype(F32) * grad_probs, axis=0, keepdims=True
+                )
+                low = (probs * (grad_probs - delta)).astype(BF16)
+                forward += [raw_low, low]
+                backward += [low, probs.astype(BF16)]
+                inverses.append(inverse)
+            sums = jnp.dot(
+                kvt_s[h, :, keys_at],
+                jnp.concatenate(forward, axis=1),
+                preferred_element_type=F32,
+            )
+            dkv = jnp.dot(
+                jnp.concatenate(backward, axis=1), pair, preferred_element_type=F32
+            )
+            if span == chunks:
+                dkv_s[h, keys_at, :] = dkv
+            else:
+                dkv_s[h, keys_at, :] += dkv
             lo = h * hdim
-            context_s[at, lo : lo + hdim] = jnp.transpose(out_t).astype(BF16)
-            grads[at, lo : lo + hdim] = jnp.transpose(grad_q).astype(BF16)
+            for p in range(span):
+                at = pl.ds(pl.multiple_of((t * span + p) * rows, rows), rows)
+                lanes = 2 * p * rows
+                rows_out = jnp.transpose(
+                    jnp.concatenate(
+                        [
+                            sums[:hdim, lanes + rows : lanes + 2 * rows] * scale,
+                            sums[hdim:, lanes : lanes + rows] * inverses[p],
+                        ],
+                        axis=0,
+                    )
+                ).astype(BF16)
+                grads[at, lo : lo + hdim] = rows_out[:, :hdim]
+                context_s[at, lo : lo + hdim] = rows_out[:, hdim:]
 
     for h in range(heads):
         lo = h * hdim
-        grads[:, width + lo : width + lo + hdim] = dk_s[h].astype(BF16)
-        grads[:, 2 * width + lo : 2 * width + lo + hdim] = dv_s[h].astype(BF16)
+        grads[:, width + lo : width + lo + hdim] = dkv_s[h, :, :hdim].astype(BF16)
+        grads[:, 2 * width + lo : 2 * width + lo + hdim] = dkv_s[h, :, hdim:].astype(BF16)
 
     for j in range(parts):
         cols = pl.ds(pl.multiple_of((line ^ j) * part_rows, part_rows), part_rows)
@@ -292,17 +349,16 @@
             pltpu.VMEM((total, model), BF16),
             pltpu.VMEM((model, 3 * width), BF16),
             pltpu.VMEM((total, width), BF16),
-            pltpu.VMEM((heads, total, hdim), BF16),
-            pltpu.VMEM((heads, total, hdim), BF16),
-            pltpu.VMEM((heads, total, hdim), BF16),
-            pltpu.VMEM((heads, total, hdim), BF16),
-            pltpu.VMEM((heads, total, hdim), F32),
-            pltpu.VMEM((heads, total, hdim), F32),
+            pltpu.VMEM((heads, total, 2 * hdim), BF16),
+            pltpu.VMEM((heads, 2 * hdim, total), BF16),
+            pltpu.VMEM((heads, groups, 2 * rows, 2 * hdim), BF16),
+            pltpu.VMEM((heads, total, 2 * hdim), F32),
             pltpu.VMEM((total, 3 * width), BF16),
             pltpu.VMEM((total, width), BF16),
             pltpu.SemaphoreType.DMA((2 * groups + parts,)),
         ],
-        compiler_params=pltpu.CompilerParams(vmem_limit_bytes=48 * 1024 * 1024),
+        compiler_params=pltpu.CompilerParams(vmem_limit_bytes=24 * 1024 * 1024),
+        cost_estimate=cost(13),
         name="attention",
     )(
         where,
@@ -316,45 +372,64 @@
     smem = pl.BlockSpec(memory_space=pltpu.SMEM)
     vmem = pl.BlockSpec(memory_space=pltpu.VMEM)
 
-    axis, bit, _ = hops[-1]
-    got = xor_permute(send, axis, bit)
+    def send_rows(keep, send):
+        axis, bit, _ = hops[-1]
+        got = xor_permute(send, axis, bit)
+        columns = model + 2 * width
+        held = pl.pallas_call(
+            lambda *refs: combine_kernel(*refs, model=model),
+            out_shape=(jax.ShapeDtypeStruct((rows, columns), BF16),) * (groups // 2),
+            in_specs=[vmem] * 2,
+            out_specs=(vmem,) * (groups // 2),
+            compiler_params=SMALL,
+            cost_estimate=cost(2),
+            name="combine",
+        )(keep, got)
+        held = list(held)
+        for axis, bit, offset in reversed(hops[:-1]):
+            arrived = [xor_permute(value, axis, bit) for value in reversed(held[1::2])][::-1]
+            held = held[::2]
+            if len(held) == 1:
+                break
+            columns = 2 * columns - model
+            held = [
+                pl.pallas_call(
+                    lambda *refs: join_kernel(*refs, model=model),
+                    out_shape=jax.ShapeDtypeStruct((rows, columns), BF16),
+                    in_specs=[vmem] * 2,
+                    out_specs=vmem,
+                    compiler_params=SMALL,
+                    cost_estimate=cost(1),
+                    name="join",
+                )(mine, theirs)
+                for mine, theirs in zip(held, arrived)
+            ]
+        grad_tokens, context = pl.pallas_call(
+            lambda *refs: final_kernel(*refs, model=model, seqs=seqs, chunks=chunks),
+            out_shape=(jax.ShapeDtypeStruct((rows, model), BF16),) * 2,
+            in_specs=[smem, vmem, vmem],
+            compiler_params=SMALL,
+            cost_estimate=cost(2),
+            name="rows_out",
+        )(where, held[0], arrived[0])
+
+        return context, grad_tokens
+
     moved = [grad_w[0]] + [xor_permute(grad_w[j], "dp", j) for j in range(1, parts)]
-    columns = model + 2 * width
-    held = pl.pallas_call(
-        lambda *refs: combine_kernel(*refs, model=model),
-        out_shape=(jax.ShapeDtypeStruct((rows, columns), BF16),) * (groups // 2),
-        in_specs=[vmem] * 2,
-        out_specs=(vmem,) * (groups // 2),
-        name="combine",
-    )(keep, got)
-    held = list(held)
-    for axis, bit, offset in reversed(hops[:-1]):
-        arrived = [xor_permute(value, axis, bit) for value in reversed(held[1::2])][::-1]
-        held = held[::2]
-        if len(held) == 1:
-            break
-        columns = 2 * columns - model
-        held = [
-            pl.pallas_call(
-                lambda *refs: join_kernel(*refs, model=model),
-                out_shape=jax.ShapeDtypeStruct((rows, columns), BF16),
-                in_specs=[vmem] * 2,
-                out_specs=vmem,
-                name="join",
-            )(mine, theirs)
-            for mine, theirs in zip(held, arrived)
-        ]
-    grad_tokens, context = pl.pallas_call(
-        lambda *refs: final_kernel(*refs, model=model, seqs=seqs, chunks=chunks),
-        out_shape=(jax.ShapeDtypeStruct((rows, model), BF16),) * 2,
-        in_specs=[smem, vmem, vmem],
-        name="rows_out",
-    )(where, held[0], arrived[0])
+    context, grad_tokens = lax.cond(
+        global_blocks[0, 0] >= 0,
+        send_rows,
+        lambda keep, send: (jnp.zeros((rows, model), BF16),) * 2,
+        keep,
+        send,
+    )
 
     final = pl.pallas_call(
         lambda *refs: sum_kernel(*refs, parts=parts, seqs=seqs, width=width),
         out_shape=(jax.ShapeDtypeStruct((model // parts, seqs * width), F32),) * 3,
         in_specs=[smem] + [vmem] * parts,
+        compiler_params=SMALL,
+        cost_estimate=cost(2),
         name="weights_out",
     )(where, *moved)
     return (context[None], grad_tokens[None], *final)

time: 117 us -> 85.1 us (0.73)
  waiting for transfers between devices: 56.6 us -> 36.5 us
  Pallas kernels: 31 us -> 16 us
  starting transfers between devices: 19.6 us -> 23.9 us
    ppermute x18, waiting for transfers between devices: 56.6 us -> 36.5 us  [xor_permute(): return lax.ppermute(value, axis, [(i, i ^ bit) for i in range(count)])]
    pallas_call x1, Pallas kernels: 20.3 us -> 12.8 us  [per_device(): pl.pallas_call(lambda *refs: attention_kernel(*refs, seqs=seqs, chunks=ch...]
    pallas_call x4, Pallas kernels: 8.52 us -> 1.78 us  [the longest x1 1.42 us: send_rows(): pl.pallas_call(lambda *refs: final_kernel(*refs, model=model, seqs=seqs,...]
    ppermute x18, starting transfers between devices: 19.6 us -> 23.9 us  [xor_permute(): return lax.ppermute(value, axis, [(i, i ^ bit) for i in range(count)])]
    unnamed x30 -> x8, local copies, waits for them, and re-layouts: 5.85 us -> 3.33 us
  transfers between devices with their start and end apart: 18 -> 18, of which waited for: 7 -> 8; matrix products, arithmetic and copies ran while one was open for 2% -> 4% of each run, Pallas kernels for 3% -> 2%
where the time goes in v3:
time: 85.1 us; the launch traced here: 84.5 us
  waiting for transfers between devices  36.5 us (43%)
  starting transfers between devices  23.9 us (28%)
  Pallas kernels  16 us (19%)
  local copies, waits for them, and re-layouts  6.85 us (8%)
  between operations  0.92 us (1%)
    ppermute x18, waiting for transfers between devices, xor_permute(): return lax.ppermute(value, axis, [(i, i ^ bit) for i in range(count)])  36.5 us
    ppermute x18, starting transfers between devices, xor_permute(): return lax.ppermute(value, axis, [(i, i ^ bit) for i in range(count)])  23.9 us
    pallas_call x1, Pallas kernels, per_device(): pl.pallas_call(lambda *refs: attention_kernel(*refs, seqs=seqs, chunks=ch...  12.8 us
    unnamed x8, local copies, waits for them, and re-layouts  3.33 us
    dynamic_slice x3, local copies, waits for them, and re-layouts, slice_of(): return lax.dynamic_slice_in_dim(value, which * width, width, 1)  2.68 us
  transfers between devices with their start and end apart: 18, of which 8 were waited for; matrix products, arithmetic and copies ran while one was open for 4% of the time, Pallas kernels for 2%

profile of v3, /device:TPU:0, one launch (start us, length us, event | category | flops | bytes accessed | tf_op | source)
XLA Modules:
  0.0 84.5 jit_solution(18339571506457173809)
XLA Ops:
  0.7 1.0 %constant_dynamic-update-slice_fusion = bf16[128,1536]{1,0:T(8,128)(2,1)S(1)} fusion(bf16[1,128,1024]{2,1,0:T(8,128)(2,1)} %param.8), kind=kLoop, calls=%fused_computation.16 | loop fusion | bytes 524288
  4.8 3.1 %collective-permute-start.8 = (bf16[128,1536]{1,0:T(8,128)(2,1)S(1)}, bf16[128,1536]{1,0:T(8,128)(2,1)S(1)}, u32[]{:S(2)}, u32[]{:S(2)}) collective-permute-start(bf16[128,1536]{1,0:T(8,128)(2,1)S(1)} %bitcast_dynamic-update-slice_fusion), channel_id=1, source_target_pairs={{0,1},{1,0},{2,3},{3,2},{4,5},{5,4},{6,7},{7,6},{8,9},{9,8},{10,11... | collective-permute-start | bytes 1179656 | tf_op jit(solution)/shard_map/ppermute | solution.py:33
  8.8 1.6 %collective-permute-start.6 = (bf16[128,1280]{1,0:T(8,128)(2,1)S(1)}, bf16[128,1280]{1,0:T(8,128)(2,1)S(1)}, u32[]{:S(2)}, u32[]{:S(2)}) collective-permute-start(bf16[128,1280]{1,0:T(8,128)(2,1)S(1)} %pad_maximum_fusion), channel_id=1, source_target_pairs={{0,8},{4,12},{8,0},{12,4},{1,9},{5,13},{9,1},{13,5},{2,10},{6,14},... | collective-permute-start | bytes 983048 | tf_op jit(solution)/shard_map/ppermute | solution.py:33
  11.2 1.0 %constant_dynamic-slice_fusion = (bf16[256,128]{1,0:T(8,128)(2,1)S(1)}, bf16[256,128]{1,0:T(8,128)(2,1)S(1)}, bf16[256,128]{1,0:T(8,128)(2,1)S(1)}, bf16[256,128]{1,0:T(8,128)(2,1)S(1)}) fusion(bf16[256,1024]{1,0:T(8,128)(2,1)} %param.12, s32[]{:T(128)S(6)} %select_n.41, s32[]{:T(128)S(6)} %select_n.45, bf16[256,1024]{1,0:T(8,128)(2,1)} %param.11), kind=kLoop, calls=%fused_computation.17 | loop fusion | bytes 524296 | tf_op jit(solution)/shard_map/dynamic_slice | solution.py:291
  12.7 2.7 %collective-permute-start.13 = (bf16[256,384]{1,0:T(8,128)(2,1)S(1)}, bf16[256,384]{1,0:T(8,128)(2,1)S(1)}, u32[]{:S(2)}, u32[]{:S(2)}) collective-permute-start(bf16[256,384]{1,0:T(8,128)(2,1)S(1)} %pad_maximum_fusion.6.refs_18_), channel_id=1, source_target_pairs={{0,2},{1,3},{2,0},{3,1},{4,6},{5,7},{6,4},{7,5},{8,10},{9,11},{10,... | collective-permute-start | bytes 589832 | tf_op jit(solution)/shard_map/ppermute | solution.py:33
  15.5 2.5 %collective-permute-done.6.refs_4_.refs_12_ = bf16[128,1280]{1,0:T(8,128)(2,1)S(1)} collective-permute-done((bf16[128,1280]{1,0:T(8,128)(2,1)S(1)}, bf16[128,1280]{1,0:T(8,128)(2,1)S(1)}, u32[]{:S(2)}, u32[]{:S(2)}) %collective-permute-start.6) | collective-permute-done | bytes 327712 | tf_op jit(solution)/shard_map/ppermute | solution.py:33
  18.4 3.7 %collective-permute-done.8.refs_6_.refs_14_ = bf16[128,1536]{1,0:T(8,128)(2,1)S(1)} collective-permute-done((bf16[128,1536]{1,0:T(8,128)(2,1)S(1)}, bf16[128,1536]{1,0:T(8,128)(2,1)S(1)}, u32[]{:S(2)}, u32[]{:S(2)}) %collective-permute-start.8) | collective-permute-done | bytes 393248 | tf_op jit(solution)/shard_map/ppermute | solution.py:33
  22.1 2.0 %collective-permute-start.10 = (bf16[128,1280]{1,0:T(8,128)(2,1)S(1)}, bf16[128,1280]{1,0:T(8,128)(2,1)S(1)}, u32[]{:S(2)}, u32[]{:S(2)}) collective-permute-start(bf16[128,1280]{1,0:T(8,128)(2,1)S(1)} %pad_maximum_fusion.1), channel_id=1, source_target_pairs={{0,8},{4,12},{8,0},{12,4},{1,9},{5,13},{9,1},{13,5},{2,10},{6,14},... | collective-permute-start | bytes 983048 | tf_op jit(solution)/shard_map/ppermute | solution.py:33
  24.2 6.0 %collective-permute-done.10.refs_8_.refs_16_ = bf16[128,1280]{1,0:T(8,128)(2,1)S(1)} collective-permute-done((bf16[128,1280]{1,0:T(8,128)(2,1)S(1)}, bf16[128,1280]{1,0:T(8,128)(2,1)S(1)}, u32[]{:S(2)}, u32[]{:S(2)}) %collective-permute-start.10) | collective-permute-done | bytes 327712 | tf_op jit(solution)/shard_map/ppermute | solution.py:33
  31.0 3.4 %collective-permute-start.14 = (bf16[256,384]{1,0:T(8,128)(2,1)S(1)}, bf16[256,384]{1,0:T(8,128)(2,1)S(1)}, u32[]{:S(2)}, u32[]{:S(2)}) collective-permute-start(bf16[256,384]{1,0:T(8,128)(2,1)S(1)} %pad_maximum_fusion.7), channel_id=1, source_target_pairs={{0,3},{1,2},{2,1},{3,0},{4,7},{5,6},{6,5},{7,4},{8,11},{9,10},{10,... | collective-permute-start | bytes 589832 | tf_op jit(solution)/shard_map/ppermute | solution.py:33
  34.6 5.6 %collective-permute-done.14.refs_21_ = bf16[256,384]{1,0:T(8,128)(2,1)S(1)} collective-permute-done((bf16[256,384]{1,0:T(8,128)(2,1)S(1)}, bf16[256,384]{1,0:T(8,128)(2,1)S(1)}, u32[]{:S(2)}, u32[]{:S(2)}) %collective-permute-start.14) | collective-permute-done | bytes 196640 | tf_op jit(solution)/shard_map/ppermute | solution.py:33
  40.2 12.8 %attention.1 = (bf16[256,384]{1,0:T(8,128)(2,1)S(1)}, bf16[256,384]{1,0:T(8,128)(2,1)S(1)}, bf16[256,384]{1,0:T(8,128)(2,1)S(1)}, bf16[256,384]{1,0:T(8,128)(2,1...) custom-call(s32[3]{0:T(128)S(1)} %pad_add_fusion.refs_0_, s32[4]{0:T(128)S(1)} %pad_add_fusion.1.refs_1_, ...), custom_call_target="tpu_custom_call" | custom-call | bytes 39000000 | tf_op jit(solution)/shard_map/attention/pallas_call | solution.py:331
  52.9 2.6 %collective-permute-start.15 = (bf16[256,384]{1,0:T(8,128)(2,1)S(1)}, bf16[256,384]{1,0:T(8,128)(2,1)S(1)}, u32[]{:S(2)}, u32[]{:S(2)}) collective-permute-start(bf16[256,384]{1,0:T(8,128)(2,1)S(1)} %get-tuple-element.38), channel_id=1, source_target_pairs={{0,1},{1,0},{2,3},{3,2},{4,5},{5,4},{6,7},{7,6},{8,9},{9,8},{10,11... | collective-permute-start | bytes 589832 | tf_op jit(solution)/shard_map/ppermute | solution.py:33
  55.5 1.5 %collective-permute-start.16 = (bf16[256,384]{1,0:T(8,128)(2,1)S(1)}, bf16[256,384]{1,0:T(8,128)(2,1)S(1)}, u32[]{:S(2)}, u32[]{:S(2)}) collective-permute-start(bf16[256,384]{1,0:T(8,128)(2,1)S(1)} %get-tuple-element.39), channel_id=1, source_target_pairs={{0,2},{1,3},{2,0},{3,1},{4,6},{5,7},{6,4},{7,5},{8,10},{9,11},{10,... | collective-permute-start | bytes 589832 | tf_op jit(solution)/shard_map/ppermute | solution.py:33
  57.0 1.2 %collective-permute-start.17 = (bf16[256,384]{1,0:T(8,128)(2,1)S(1)}, bf16[256,384]{1,0:T(8,128)(2,1)S(1)}, u32[]{:S(2)}, u32[]{:S(2)}) collective-permute-start(bf16[256,384]{1,0:T(8,128)(2,1)S(1)} %get-tuple-element.40), channel_id=1, source_target_pairs={{0,3},{1,2},{2,1},{3,0},{4,7},{5,6},{6,5},{7,4},{8,11},{9,10},{10,... | collective-permute-start | bytes 589832 | tf_op jit(solution)/shard_map/ppermute | solution.py:33
  58.2 24.9 %conditional.1 = (bf16[1,128,1024]{2,1,0:T(8,128)(2,1)}, bf16[1,128,1024]{2,1,0:T(8,128)(2,1)}) conditional(s32[]{:T(128)} %bitcast.2, () %tuple.20, (bf16[4,128,1152]{2,1,0:T(8,128)(2,1)S(1)}, bf16[4,128,1152]{2,1,0:T(8,128)(2,1)S(1)}, s32[3]{0:T(128)S(1)}) %tuple.21), branch_computations={%region_0.1_spmd, %region_1.2_spmd} | conditional | bytes 26913072 | solution.py:419
  58.3 2.8 %collective-permute-done.refs_1_ = bf16[4,128,1152]{2,1,0:T(8,128)(2,1)S(1)} collective-permute-done((bf16[4,128,1152]{2,1,0:T(8,128)(2,1)S(1)}, bf16[4,128,1152]{2,1,0:T(8,128)(2,1)S(1)}, u32[]{:S(2)}, u32[]{:S(2)}) %collective-permute-start) | collective-permute-done | bytes 1179680 | tf_op jit(solution)/shard_map/cond/branch_1_fun/ppermute | solution.py:33
  61.4 1.7 %collective-permute-start.2 = (bf16[128,1280]{1,0:T(8,128)(2,1)S(1)}, bf16[128,1280]{1,0:T(8,128)(2,1)S(1)}, u32[]{:S(2)}, u32[]{:S(2)}) collective-permute-start(bf16[128,1280]{1,0:T(8,128)(2,1)S(1)} %get-tuple-element.14), channel_id=1, source_target_pairs={{0,8},{4,12},{8,0},{12,4},{1,9},{5,13},{9,1},{13,5},{2,10},{6,14},... | collective-permute-start | bytes 983048 | tf_op jit(solution)/shard_map/cond/branch_1_fun/ppermute | solution.py:33
  63.1 8.1 %collective-permute-done.2.refs_1_ = bf16[128,1280]{1,0:T(8,128)(2,1)S(1)} collective-permute-done((bf16[128,1280]{1,0:T(8,128)(2,1)S(1)}, bf16[128,1280]{1,0:T(8,128)(2,1)S(1)}, u32[]{:S(2)}, u32[]{:S(2)}) %collective-permute-start.2) | collective-permute-done | bytes 327712 | tf_op jit(solution)/shard_map/cond/branch_1_fun/ppermute | solution.py:33
  71.3 0.9 %collective-permute-start.3 = (bf16[128,1536]{1,0:T(8,128)(2,1)S(1)}, bf16[128,1536]{1,0:T(8,128)(2,1)S(1)}, u32[]{:S(2)}, u32[]{:S(2)}) collective-permute-start(bf16[128,1536]{1,0:T(8,128)(2,1)S(1)} %join.3), channel_id=1, source_target_pairs={{0,1},{1,0},{2,3},{3,2},{4,5},{5,4},{6,7},{7,6},{8,9},{9,8},{10,11... | collective-permute-start | bytes 1179656 | tf_op jit(solution)/shard_map/cond/branch_1_fun/ppermute | solution.py:33
  72.2 1.6 %collective-permute-start.1 = (bf16[128,1280]{1,0:T(8,128)(2,1)S(1)}, bf16[128,1280]{1,0:T(8,128)(2,1)S(1)}, u32[]{:S(2)}, u32[]{:S(2)}) collective-permute-start(bf16[128,1280]{1,0:T(8,128)(2,1)S(1)} %get-tuple-element.12), channel_id=1, source_target_pairs={{0,8},{4,12},{8,0},{12,4},{1,9},{5,13},{9,1},{13,5},{2,10},{6,14},... | collective-permute-start | bytes 983048 | tf_op jit(solution)/shard_map/cond/branch_1_fun/ppermute | solution.py:33
  73.8 7.0 %collective-permute-done.1.refs_1_ = bf16[128,1280]{1,0:T(8,128)(2,1)S(1)} collective-permute-done((bf16[128,1280]{1,0:T(8,128)(2,1)S(1)}, bf16[128,1280]{1,0:T(8,128)(2,1)S(1)}, u32[]{:S(2)}, u32[]{:S(2)}) %collective-permute-start.1) | collective-permute-done | bytes 327712 | tf_op jit(solution)/shard_map/cond/branch_1_fun/ppermute | solution.py:33
  81.7 1.4 %rows_out.1 = (bf16[128,1024]{1,0:T(8,128)(2,1)}, bf16[128,1024]{1,0:T(8,128)(2,1)}) custom-call(s32[3]{0:T(128)S(1)} %get-tuple-element.8.refs_0_, bf16[128,1536]{1,0:T(8,128)(2,1)S(1)} %join.2.refs_1_, bf16[128,1536]{1,0:T(8,128)(2,1)S(1)} %collective-permute-done.3.refs_2_), custom_call_target="tpu_custom_call" | custom-call | bytes 6000000 | tf_op jit(solution)/shard_map/cond/branch_1_fun/rows_out/pallas_call | solution.py:407
  83.1 1.5 %weights_out.1 = (f32[256,256]{1,0:T(8,128)}, f32[256,256]{1,0:T(8,128)}, f32[256,256]{1,0:T(8,128)}) custom-call(s32[3]{0:T(128)S(1)} %pad_add_fusion.refs_0_, bf16[256,384]{1,0:T(8,128)(2,1)S(1)} %get-tuple-element.37.refs_1_, bf16[256,384]{1,0:T(8,128)(2,1)S(1)} %collective-permute-done.15.refs_2_, bf16[256,384]{1,0:T(8,128)(2,1)S(1)} %collective-permute-done.16.refs_3_, ...), custom_call_target="tpu_custom_call" | custom-call | bytes 6000000 | tf_op jit(solution)/shard_map/weights_out/pallas_call | solution.py:427
  (48 shorter events, 8.0 us)
Async XLA Ops:
  0.6 8.1 %copy-start = (bf16[1,128,1024]{2,1,0:T(8,128)(2,1)S(1)}, bf16[1,128,1024]{2,1,0:T(8,128)(2,1)}, u32[]{:S(2)}) copy-start(bf16[1,128,1024]{2,1,0:T(8,128)(2,1)} %param.8) | copy-start | bytes 786436
  4.8 17.2 %collective-permute-start.8 = (bf16[128,1536]{1,0:T(8,128)(2,1)S(1)}, bf16[128,1536]{1,0:T(8,128)(2,1)S(1)}, u32[]{:S(2)}, u32[]{:S(2)}) collective-permute-start(bf16[128,1536]{1,0:T(8,128)(2,1)S(1)} %bitcast_dynamic-update-slice_fusion), channel_id=1, source_target_pairs={{0,1},{1,0},{2,3},{3,2},{4,5},{5,4},{6,7},{7,6},{8,9},{9,8},{10,11... | collective-permute-start | bytes 1179656 | tf_op jit(solution)/shard_map/ppermute | solution.py:33
  8.7 9.2 %copy-start.1 = (s32[1,2]{1,0:T(1,128)S(1)}, s32[1,2]{1,0:T(1,128)}, u32[]{:S(2)}) copy-start(s32[1,2]{1,0:T(1,128)} %param.9) | copy-start | bytes 28
  8.8 9.2 %collective-permute-start.6 = (bf16[128,1280]{1,0:T(8,128)(2,1)S(1)}, bf16[128,1280]{1,0:T(8,128)(2,1)S(1)}, u32[]{:S(2)}, u32[]{:S(2)}) collective-permute-start(bf16[128,1280]{1,0:T(8,128)(2,1)S(1)} %pad_maximum_fusion), channel_id=1, source_target_pairs={{0,8},{4,12},{8,0},{12,4},{1,9},{5,13},{9,1},{13,5},{2,10},{6,14},... | collective-permute-start | bytes 983048 | tf_op jit(solution)/shard_map/ppermute | solution.py:33
  12.2 18.7 %collective-permute-start.12 = (bf16[256,384]{1,0:T(8,128)(2,1)S(1)}, bf16[256,384]{1,0:T(8,128)(2,1)S(1)}, u32[]{:S(2)}, u32[]{:S(2)}) collective-permute-start(bf16[256,384]{1,0:T(8,128)(2,1)S(1)} %pad_maximum_fusion.7), channel_id=1, source_target_pairs={{0,1},{1,0},{2,3},{3,2},{4,5},{5,4},{6,7},{7,6},{8,9},{9,8},{10,11... | collective-permute-start | bytes 589832 | tf_op jit(solution)/shard_map/ppermute | solution.py:33
  12.7 18.2 %collective-permute-start.13 = (bf16[256,384]{1,0:T(8,128)(2,1)S(1)}, bf16[256,384]{1,0:T(8,128)(2,1)S(1)}, u32[]{:S(2)}, u32[]{:S(2)}) collective-permute-start(bf16[256,384]{1,0:T(8,128)(2,1)S(1)} %pad_maximum_fusion.6.refs_18_), channel_id=1, source_target_pairs={{0,2},{1,3},{2,0},{3,1},{4,6},{5,7},{6,4},{7,5},{8,10},{9,11},{10,... | collective-permute-start | bytes 589832 | tf_op jit(solution)/shard_map/ppermute | solution.py:33
  15.4 24.7 %collective-permute-start.5 = (bf16[128,1152]{1,0:T(8,128)(2,1)S(1)}, bf16[128,1152]{1,0:T(8,128)(2,1)S(1)}, u32[]{:S(2)}, u32[]{:S(2)}) collective-permute-start(bf16[128,1152]{1,0:T(8,128)(2,1)S(1)} %pad_maximum_fusion.2), channel_id=1, source_target_pairs={{0,4},{4,0},{8,12},{12,8},{1,5},{5,1},{9,13},{13,9},{2,6},{6,2},{1... | collective-permute-start | bytes 884744 | tf_op jit(solution)/shard_map/ppermute | solution.py:33
  18.0 12.3 %collective-permute-start.4 = (s32[1,2]{1,0:T(1,128)S(1)}, s32[1,2]{1,0:T(1,128)S(1)}, u32[]{:S(2)}, u32[]{:S(2)}) collective-permute-start(s32[1,2]{1,0:T(1,128)S(1)} %copy-done.1), channel_id=1, source_target_pairs={{0,1},{1,0},{2,3},{3,2},{4,5},{5,4},{6,7},{7,6},{8,9},{9,8},{10,11... | collective-permute-start | bytes 32 | tf_op jit(solution)/shard_map/ppermute | solution.py:33
  22.1 8.1 %collective-permute-start.10 = (bf16[128,1280]{1,0:T(8,128)(2,1)S(1)}, bf16[128,1280]{1,0:T(8,128)(2,1)S(1)}, u32[]{:S(2)}, u32[]{:S(2)}) collective-permute-start(bf16[128,1280]{1,0:T(8,128)(2,1)S(1)} %pad_maximum_fusion.1), channel_id=1, source_target_pairs={{0,8},{4,12},{8,0},{12,4},{1,9},{5,13},{9,1},{13,5},{2,10},{6,14},... | collective-permute-start | bytes 983048 | tf_op jit(solution)/shard_map/ppermute | solution.py:33
  30.2 9.9 %collective-permute-start.7 = (bf16[128,1152]{1,0:T(8,128)(2,1)S(1)}, bf16[128,1152]{1,0:T(8,128)(2,1)S(1)}, u32[]{:S(2)}, u32[]{:S(2)}) collective-permute-start(bf16[128,1152]{1,0:T(8,128)(2,1)S(1)} %pad_maximum_fusion.3), channel_id=1, source_target_pairs={{0,4},{4,0},{8,12},{12,8},{1,5},{5,1},{9,13},{13,9},{2,6},{6,2},{1... | collective-permute-start | bytes 884744 | tf_op jit(solution)/shard_map/ppermute | solution.py:33
  30.3 9.8 %collective-permute-start.9 = (bf16[128,1152]{1,0:T(8,128)(2,1)S(1)}, bf16[128,1152]{1,0:T(8,128)(2,1)S(1)}, u32[]{:S(2)}, u32[]{:S(2)}) collective-permute-start(bf16[128,1152]{1,0:T(8,128)(2,1)S(1)} %pad_maximum_fusion.4), channel_id=1, source_target_pairs={{0,4},{4,0},{8,12},{12,8},{1,5},{5,1},{9,13},{13,9},{2,6},{6,2},{1... | collective-permute-start | bytes 884744 | tf_op jit(solution)/shard_map/ppermute | solution.py:33
  30.9 9.3 %collective-permute-start.11 = (bf16[128,1152]{1,0:T(8,128)(2,1)S(1)}, bf16[128,1152]{1,0:T(8,128)(2,1)S(1)}, u32[]{:S(2)}, u32[]{:S(2)}) collective-permute-start(bf16[128,1152]{1,0:T(8,128)(2,1)S(1)} %pad_maximum_fusion.5), channel_id=1, source_target_pairs={{0,4},{4,0},{8,12},{12,8},{1,5},{5,1},{9,13},{13,9},{2,6},{6,2},{1... | collective-permute-start | bytes 884744 | tf_op jit(solution)/shard_map/ppermute | solution.py:33
  31.0 9.2 %collective-permute-start.14 = (bf16[256,384]{1,0:T(8,128)(2,1)S(1)}, bf16[256,384]{1,0:T(8,128)(2,1)S(1)}, u32[]{:S(2)}, u32[]{:S(2)}) collective-permute-start(bf16[256,384]{1,0:T(8,128)(2,1)S(1)} %pad_maximum_fusion.7), channel_id=1, source_target_pairs={{0,3},{1,2},{2,1},{3,0},{4,7},{5,6},{6,5},{7,4},{8,11},{9,10},{10,... | collective-permute-start | bytes 589832 | tf_op jit(solution)/shard_map/ppermute | solution.py:33
  52.9 30.1 %collective-permute-start.15 = (bf16[256,384]{1,0:T(8,128)(2,1)S(1)}, bf16[256,384]{1,0:T(8,128)(2,1)S(1)}, u32[]{:S(2)}, u32[]{:S(2)}) collective-permute-start(bf16[256,384]{1,0:T(8,128)(2,1)S(1)} %get-tuple-element.38), channel_id=1, source_target_pairs={{0,1},{1,0},{2,3},{3,2},{4,5},{5,4},{6,7},{7,6},{8,9},{9,8},{10,11... | collective-permute-start | bytes 589832 | tf_op jit(solution)/shard_map/ppermute | solution.py:33
  55.5 27.6 %collective-permute-start.16 = (bf16[256,384]{1,0:T(8,128)(2,1)S(1)}, bf16[256,384]{1,0:T(8,128)(2,1)S(1)}, u32[]{:S(2)}, u32[]{:S(2)}) collective-permute-start(bf16[256,384]{1,0:T(8,128)(2,1)S(1)} %get-tuple-element.39), channel_id=1, source_target_pairs={{0,2},{1,3},{2,0},{3,1},{4,6},{5,7},{6,4},{7,5},{8,10},{9,11},{10,... | collective-permute-start | bytes 589832 | tf_op jit(solution)/shard_map/ppermute | solution.py:33
  57.0 26.1 %collective-permute-start.17 = (bf16[256,384]{1,0:T(8,128)(2,1)S(1)}, bf16[256,384]{1,0:T(8,128)(2,1)S(1)}, u32[]{:S(2)}, u32[]{:S(2)}) collective-permute-start(bf16[256,384]{1,0:T(8,128)(2,1)S(1)} %get-tuple-element.40), channel_id=1, source_target_pairs={{0,3},{1,2},{2,1},{3,0},{4,7},{5,6},{6,5},{7,4},{8,11},{9,10},{10,... | collective-permute-start | bytes 589832 | tf_op jit(solution)/shard_map/ppermute | solution.py:33
  58.2 2.9 %collective-permute-start = (bf16[4,128,1152]{2,1,0:T(8,128)(2,1)S(1)}, bf16[4,128,1152]{2,1,0:T(8,128)(2,1)S(1)}, u32[]{:S(2)}, u32[]{:S(2)}) collective-permute-start(bf16[4,128,1152]{2,1,0:T(8,128)(2,1)S(1)} %get-tuple-element.10), channel_id=1, source_target_pairs={{0,4},{4,0},{8,12},{12,8},{1,5},{5,1},{9,13},{13,9},{2,6},{6,2},{1... | collective-permute-start | bytes 3538952 | tf_op jit(solution)/shard_map/cond/branch_1_fun/ppermute | solution.py:33
  61.4 9.8 %collective-permute-start.2 = (bf16[128,1280]{1,0:T(8,128)(2,1)S(1)}, bf16[128,1280]{1,0:T(8,128)(2,1)S(1)}, u32[]{:S(2)}, u32[]{:S(2)}) collective-permute-start(bf16[128,1280]{1,0:T(8,128)(2,1)S(1)} %get-tuple-element.14), channel_id=1, source_target_pairs={{0,8},{4,12},{8,0},{12,4},{1,9},{5,13},{9,1},{13,5},{2,10},{6,14},... | collective-permute-start | bytes 983048 | tf_op jit(solution)/shard_map/cond/branch_1_fun/ppermute | solution.py:33
  71.3 10.4 %collective-permute-start.3 = (bf16[128,1536]{1,0:T(8,128)(2,1)S(1)}, bf16[128,1536]{1,0:T(8,128)(2,1)S(1)}, u32[]{:S(2)}, u32[]{:S(2)}) collective-permute-start(bf16[128,1536]{1,0:T(8,128)(2,1)S(1)} %join.3), channel_id=1, source_target_pairs={{0,1},{1,0},{2,3},{3,2},{4,5},{5,4},{6,7},{7,6},{8,9},{9,8},{10,11... | collective-permute-start | bytes 1179656 | tf_op jit(solution)/shard_map/cond/branch_1_fun/ppermute | solution.py:33
  72.2 8.6 %collective-permute-start.1 = (bf16[128,1280]{1,0:T(8,128)(2,1)S(1)}, bf16[128,1280]{1,0:T(8,128)(2,1)S(1)}, u32[]{:S(2)}, u32[]{:S(2)}) collective-permute-start(bf16[128,1280]{1,0:T(8,128)(2,1)S(1)} %get-tuple-element.12), channel_id=1, source_target_pairs={{0,8},{4,12},{8,0},{12,4},{1,9},{5,13},{9,1},{13,5},{2,10},{6,14},... | collective-permute-start | bytes 983048 | tf_op jit(solution)/shard_map/cond/branch_1_fun/ppermute | solution.py:33

commit v4 on v3

--- a/solution.py
+++ b/solution.py
@@ -10,7 +10,6 @@
 HEADS = 16
 BLK = 64
 NEG = -1e30
-SPLIT = 2
 SPAN = 4
 
 NT = (((1,), (1,)), ((), ()))
@@ -19,6 +18,7 @@
 BF16 = jnp.bfloat16
 
 
+PACK_VMEM = 56 * 1024 * 1024
 SMALL = pltpu.CompilerParams(vmem_limit_bytes=8 * 1024 * 1024)
 
 
@@ -34,17 +34,19 @@
 
 
 def attention_kernel(
-    where_ref, chosen_ref, *refs, seqs, chunks, rows, heads, hdim, parts, scale, up_starts
+    where_ref, chosen_ref, *refs, seqs, chunks, rows, heads, hdim, parts, scale, sources, packed, ids_start
 ):
     pieces = seqs * chunks
     half = pieces // 2
-    token_refs = refs[:pieces]
-    up_refs = refs[pieces : 2 * pieces]
-    weight_refs = refs[2 * pieces : 2 * pieces + parts]
-    outs = refs[2 * pieces + parts :]
+    count = 1 + max(index for index, _, _ in sources)
+    token_refs = refs[:count]
+    ups = 1 if packed else count
+    up_refs = refs[count : count + ups]
+    weight_refs = refs[count + ups : count + ups + parts]
+    outs = refs[count + ups + parts :]
     grad_w_refs = outs[:parts]
     keep_ref, send_ref = outs[parts : parts + 2]
-    all_tokens, weight, up_all, kv_s, kvt_s, pair_s, dkv_s, grads, context_s, sems = outs[
+    all_tokens, weight, up_all, kv_s, kvt_s, pair_s, dkv_s, grads, context_s, far_ids, ids, sems = outs[
         parts + 2 :
     ]
     length = chunks * rows
@@ -58,12 +60,17 @@
     for j in range(parts):
         start = pl.multiple_of((line ^ j) * part_rows, part_rows)
         copies.append((weight_refs[j], weight.at[pl.ds(start, part_rows), :]))
-    for b in range(pieces):
-        copies.append((token_refs[b].at[:, :model], all_tokens.at[pl.ds(b * rows, rows), :]))
-    for b in range(pieces):
-        source = up_refs[b]
-        start = up_starts[b]
-        copies.append((source.at[:, start : start + width], up_all.at[pl.ds(b * rows, rows), :]))
+    for b, (index, first, start) in enumerate(sources):
+        held = pl.ds(first, rows)
+        target = pl.ds(b * rows, rows)
+        copies.append((token_refs[index].at[held, :model], all_tokens.at[target, :]))
+        if packed and b:
+            up = token_refs[index].at[held, start : start + width]
+        else:
+            up = up_refs[index].at[held, :]
+        copies.append((up, up_all.at[target, :]))
+    if seqs == 2:
+        copies.append((token_refs[1].at[:16, ids_start : ids_start + 128], far_ids))
     copies = [
         pltpu.make_async_copy(source, target, sems.at[index])
         for index, (source, target) in enumerate(copies)
@@ -72,6 +79,12 @@
         copy.start()
     for copy in copies:
         copy.wait()
+    for k in range(2):
+        ids[0, k] = jnp.full((1, rows), chosen_ref[k], jnp.int32)
+        if seqs == 2:
+            far = far_ids[:, k * 64 : k * 64 + 1].astype(F32).astype(jnp.int32)
+            ids[1, k] = jnp.broadcast_to(far[:1], (1, rows))
+
     pair_s[...] = jnp.zeros_like(pair_s)
     if SPAN < chunks:
         dkv_s[...] = jnp.zeros_like(dkv_s)
@@ -111,8 +124,8 @@
     def _(t):
         i = t // (chunks // span)
         keys_at = pl.ds(pl.multiple_of(i * length, length), length)
-        first = chosen_ref[2 * i]
-        second = chosen_ref[2 * i + 1]
+        first = ids[i, 0]
+        second = ids[i, 1]
         shape = (block_count, 1, rows)
         key = lax.broadcasted_iota(jnp.int32, shape, 0)
         key_block = (lax.shift_right_logical(key, log_blocks) ^ position) * blocks_per_chunk + (
@@ -229,9 +242,13 @@
         lo += value.shape[1]
 
 
-def final_kernel(where_ref, mine_ref, theirs_ref, grad_ref, context_ref, *, model, seqs, chunks):
-    total, mine, theirs = add_and_join(mine_ref[...], theirs_ref[...], model)
-    grad_ref[...] = total
+def final_kernel(
+    where_ref, mine_ref, near_ref, far_ref, grad_ref, context_ref, *, model, seqs, chunks
+):
+    total, mine, near = add_and_join(mine_ref[...], near_ref[...], model)
+    grad_ref[...] = (total.astype(F32) + far_ref[:, :model].astype(F32)).astype(BF16)
+    theirs = far_ref[:, model:]
+    mine = jnp.concatenate([mine, near], axis=1)
     groups = seqs * chunks
     width = model // groups
     values = [mine[:, k * width : (k + 1) * width] for k in range(groups // 2)]
@@ -264,6 +281,51 @@
             outs[m][:, width:] = jnp.where(flip, sums[0], sums[1])
 
 
+def pack_kernel(where_ref, chosen_ref, *refs, lefts, seqs, chunks, width, noted):
+    tokens, up = refs[:2]
+    weight_refs = refs[2:5]
+    hops = len(lefts)
+    sends = refs[5 : 5 + hops]
+    own_up = refs[5 + hops]
+    weight_sends = refs[6 + hops : 6 + hops + seqs]
+    sems = refs[6 + hops + seqs]
+    model = tokens.shape[1]
+
+    def columns(offset):
+        which = (where_ref[0] ^ (offset % chunks)) * seqs + (where_ref[2] ^ (offset // chunks))
+        return pl.ds(pl.multiple_of(which * width, width), width)
+
+    copies = []
+    for send, left in zip(sends, lefts):
+        copies.append((tokens, send.at[:, :model]))
+        for k in range(left):
+            lo = model + k * width
+            copies.append((up.at[:, columns(left + k)], send.at[:, lo : lo + width]))
+    copies.append((up.at[:, columns(0)], own_up))
+    for i in range(seqs):
+        for m in range(3):
+            copies.append(
+                (
+                    weight_refs[m].at[:, columns(i * chunks)],
+                    weight_sends[i].at[:, m * width : (m + 1) * width],
+                )
+            )
+    copies = [
+        pltpu.make_async_copy(source, target, sems.at[index])
+        for index, (source, target) in enumerate(copies)
+    ]
+    for copy in copies:
+        copy.start()
+    if noted:
+        lo = model + lefts[0] * width
+        shape = (tokens.shape[0], 128)
+        lane = lax.broadcasted_iota(jnp.int32, shape, 1)
+        both = jnp.where(lane < 64, chosen_ref[0], chosen_ref[1])
+        sends[0][:, lo : lo + 128] = both.astype(F32).astype(BF16)
+    for copy in copies:
+        copy.wait()
+
+
 def per_device(tokens, global_blocks, w_query, w_key, w_value, d_context):
     own_tokens = tokens[0]
     upstream = d_context[0]
@@ -271,7 +333,9 @@
     hdim = model // HEADS
     chunks = lax.axis_size("ctx")
     parts = lax.axis_size("dp")
-    seqs = SPLIT if HEADS % (SPLIT * chunks) == 0 and parts % SPLIT == 0 else 1
+    seqs = 1
+    if parts % 2 == 0 and model % (chunks * 2 * 128) == 0 and HEADS % (chunks * 2) == 0:
+        seqs = 2
     groups = chunks * seqs
     width = model // groups
     heads = width // hdim
@@ -286,45 +350,116 @@
         hops.append(("ctx", bit, bit))
         bit //= 2
 
-    def slice_of(value, offset):
-        which = (position ^ (offset % chunks)) * seqs + (side ^ (offset // chunks))
-        return lax.dynamic_slice_in_dim(value, which * width, width, 1)
-
-    sends = []
-    for i in range(seqs):
-        sends.append(
+    smem = pl.BlockSpec(memory_space=pltpu.SMEM)
+    vmem = pl.BlockSpec(memory_space=pltpu.VMEM)
+    hbm = pl.BlockSpec(memory_space=pltpu.HBM)
+    chosen = global_blocks[0]
+    lefts = [groups >> (k + 1) for k in range(len(hops))]
+    packed = width % 128 == 0
+    noted = 128 if seqs == 2 else 0
+    if packed:
+        sizes = [model + left * width + (noted if k == 0 else 0) for k, left in enumerate(lefts)]
+        outs = pl.pallas_call(
+            lambda *refs: pack_kernel(
+                *refs, lefts=lefts, seqs=seqs, chunks=chunks, width=width, noted=noted
+            ),
+            out_shape=tuple(jax.ShapeDtypeStruct((rows, size), BF16) for size in sizes + [width])
+            + (jax.ShapeDtypeStruct((model // parts, 3 * width), BF16),) * seqs,
+            in_specs=[smem, smem] + [hbm] * 5,
+            out_specs=(vmem,) * (len(hops) + 1 + seqs),
+            scratch_shapes=[
+                pltpu.SemaphoreType.DMA((len(hops) + sum(lefts) + 1 + 3 * seqs,)),
+            ],
+            compiler_params=pltpu.CompilerParams(vmem_limit_bytes=PACK_VMEM),
+            cost_estimate=cost(2),
+            name="pack",
+        )(where, chosen, own_tokens, upstream, w_query, w_key, w_value)
+        own_sends = outs[: len(hops)]
+        own_up = outs[len(hops)]
+        sends = outs[len(hops) + 1 :]
+    else:
+
+        def slice_of(value, offset):
+            which = (position ^ (offset % chunks)) * seqs + (side ^ (offset // chunks))
+            return lax.dynamic_slice_in_dim(value, which * width, width, 1)
+
+        ups = [slice_of(upstream, o) for o in range(groups)]
+        own_up = ups[0]
+        own_sends = [
+            jnp.concatenate([own_tokens] + ups[left : 2 * left], axis=1) for left in lefts
+        ]
+        sends = [
             jnp.concatenate(
                 [slice_of(w, i * chunks) for w in (w_query, w_key, w_value)], axis=1
             )
-        )
+            for i in range(seqs)
+        ]
+
+    arrived = [xor_permute(own_sends[k], *hops[k][:2]) for k in range(2)]
     weights = [sends[0]]
     for j in range(1, parts):
         weights.append(xor_permute(sends[j % seqs], "dp", j))
 
-    ups = [slice_of(upstream, o) for o in range(groups)]
-    pieces = {0: None}
-    chosen = [global_blocks[0]]
-    left = groups
-    for axis, bit, offset in hops:
-        left //= 2
-        for key in list(pieces):
-            held = pieces[key]
-            if held is None:
-                send = [own_tokens] + ups[left : 2 * left]
-            else:
-                lo = model + left * width
-                send = [held[:, :model], held[:, lo : lo + left * width]]
-            pieces[key + offset] = xor_permute(jnp.concatenate(send, axis=1), axis, bit)
-        if axis == "dp":
-            chosen.append(xor_permute(global_blocks, axis, bit)[0])
-    token_pieces = [own_tokens] + [pieces[o] for o in range(1, groups)]
-    if width % 128 == 0:
-        up_pieces = [ups[0]] + token_pieces[1:]
-        up_starts = [0] + [model] * (groups - 1)
+    def by_age(keys):
+        return sorted(keys, key=lambda o: (o.bit_count(), o & hops[0][2]))
+
+    inner = [o for o in range(2, groups, 2) if o not in (hops[0][2], hops[1][2])]
+
+    def spread(near, far, *own):
+        pieces = {hops[0][2]: near}
+        for k in range(1, len(hops)):
+            axis, bit, offset = hops[k]
+            lo = model + lefts[k] * width
+            keys = by_age(pieces)
+            sends = [
+                jnp.concatenate(
+                    [pieces[key][:, :model], pieces[key][:, lo : lo + lefts[k] * width]], axis=1
+                )
+                for key in keys
+            ]
+            if k > 1:
+                keys = [0] + keys
+                sends = [own[k - 2]] + sends
+            if len(sends) > 1:
+                first = jnp.concatenate(sends[:-1], axis=0)
+                if k + 1 == len(hops):
+                    first, _ = lax.optimization_barrier((first, pieces[keys[-1]]))
+                first = xor_permute(first, axis, bit)
+                if k + 1 == len(hops):
+                    last = xor_permute(pieces[keys[-1]], axis, bit)
+                    return tuple(pieces[o] for o in inner) + (first, last)
+                for n, key in enumerate(keys[:-1]):
+                    pieces[key + offset] = first[n * rows : (n + 1) * rows]
+            pieces[keys[-1] + offset] = xor_permute(sends[-1], axis, bit)
+            if k == 1:
+                pieces[offset] = far
+
+    operands = (*arrived, *own_sends[2:])
+    live = global_blocks[0, 0] >= 0
+    spread_out = lax.cond(
+        live,
+        spread,
+        lambda *values: jax.tree.map(
+            lambda v: jnp.zeros(v.shape, v.dtype), jax.eval_shape(spread, *values)
+        ),
+        *operands,
+    )
+    buffers = [own_tokens, *arrived, *spread_out]
+    where_is = {0: (0, 0), hops[0][2]: (1, 0), hops[1][2]: (2, 0)}
+    for n, o in enumerate(inner):
+        where_is[o] = (3 + n, 0)
+    ordered = by_age(range(0, groups, 2))
+    for n, o in enumerate(ordered[:-1]):
+        where_is[o + 1] = (3 + len(inner), n * rows)
+    where_is[ordered[-1] + 1] = (4 + len(inner), 0)
+    late = ordered[-1] + 1
+    if packed:
+        up_buffers = [own_up]
     else:
-        up_pieces = [ups[0]] + [v[:, model : model + width] for v in token_pieces[1:]]
-        token_pieces = [v[:, :model] for v in token_pieces]
-        up_starts = [0] * groups
+        up_buffers = [own_up] + [v[:, model : model + width] for v in buffers[1:-1]]
+        up_buffers.append(buffers[-1][:, model + width : model + 2 * width])
+        buffers = [v[:, :model] for v in buffers]
+    sources = [where_is[o] + (model + (width if o == late else 0),) for o in range(groups)]
 
     length = chunks * rows
     total = seqs * length
@@ -338,12 +473,14 @@
             hdim=hdim,
             parts=parts,
             scale=1.0 / math.sqrt(hdim),
-            up_starts=up_starts,
+            sources=sources,
+            packed=packed,
+            ids_start=model + lefts[0] * width,
         ),
         out_shape=(jax.ShapeDtypeStruct((model // parts, 3 * width), BF16),) * parts
         + (jax.ShapeDtypeStruct((groups // 2, rows, model + width), BF16),) * 2,
         in_specs=[pl.BlockSpec(memory_space=pltpu.SMEM)] * 2
-        + [pl.BlockSpec(memory_space=pl.ANY)] * (2 * groups + parts),
+        + [pl.BlockSpec(memory_space=pl.ANY)] * (len(buffers) + len(up_buffers) + parts),
         out_specs=(pl.BlockSpec(memory_space=pltpu.VMEM),) * (parts + 2),
         scratch_shapes=[
             pltpu.VMEM((total, model), BF16),
@@ -355,26 +492,38 @@
             pltpu.VMEM((heads, total, 2 * hdim), F32),
             pltpu.VMEM((total, 3 * width), BF16),
             pltpu.VMEM((total, width), BF16),
-            pltpu.SemaphoreType.DMA((2 * groups + parts,)),
+            pltpu.VMEM((16, 128), BF16),
+            pltpu.VMEM((seqs, 2, 1, rows), jnp.int32),
+            pltpu.SemaphoreType.DMA((2 * groups + parts + 1,)),
         ],
         compiler_params=pltpu.CompilerParams(vmem_limit_bytes=24 * 1024 * 1024),
         cost_estimate=cost(13),
         name="attention",
     )(
         where,
-        jnp.concatenate(chosen),
-        *token_pieces,
-        *up_pieces,
+        chosen,
+        *buffers,
+        *up_buffers,
         *weights,
     )
     grad_w = results[:parts]
     keep, send = results[parts:]
-    smem = pl.BlockSpec(memory_space=pltpu.SMEM)
-    vmem = pl.BlockSpec(memory_space=pltpu.VMEM)
-
-    def send_rows(keep, send):
-        axis, bit, _ = hops[-1]
-        got = xor_permute(send, axis, bit)
+    moved = [grad_w[0]] + [xor_permute(grad_w[j], "dp", j) for j in range(1, parts)]
+
+    def join(mine, theirs):
+        columns = 2 * mine.shape[1] - model
+        return pl.pallas_call(
+            lambda *refs: join_kernel(*refs, model=model),
+            out_shape=jax.ShapeDtypeStruct((rows, columns), BF16),
+            in_specs=[vmem] * 2,
+            out_specs=vmem,
+            compiler_params=SMALL,
+            cost_estimate=cost(1),
+            name="join",
+        )(mine, theirs)
+
+    def collect(keep, send):
+        got = xor_permute(send, *hops[-1][:2])
         columns = model + 2 * width
         held = pl.pallas_call(
             lambda *refs: combine_kernel(*refs, model=model),
@@ -385,41 +534,25 @@
             cost_estimate=cost(2),
             name="combine",
         )(keep, got)
-        held = list(held)
-        for axis, bit, offset in reversed(hops[:-1]):
-            arrived = [xor_permute(value, axis, bit) for value in reversed(held[1::2])][::-1]
-            held = held[::2]
-            if len(held) == 1:
-                break
-            columns = 2 * columns - model
-            held = [
-                pl.pallas_call(
-                    lambda *refs: join_kernel(*refs, model=model),
-                    out_shape=jax.ShapeDtypeStruct((rows, columns), BF16),
-                    in_specs=[vmem] * 2,
-                    out_specs=vmem,
-                    compiler_params=SMALL,
-                    cost_estimate=cost(1),
-                    name="join",
-                )(mine, theirs)
-                for mine, theirs in zip(held, arrived)
-            ]
-        grad_tokens, context = pl.pallas_call(
+        for axis, bit, _ in reversed(hops[2:-1]):
+            theirs = [xor_permute(value, axis, bit) for value in held[1::2]]
+            held = [join(*pair) for pair in zip(held[::2], theirs)]
+        far = join(held[2], xor_permute(held[3], *hops[1][:2]))
+        far = xor_permute(far, *hops[0][:2])
+        near = xor_permute(held[1], *hops[1][:2])
+        return pl.pallas_call(
             lambda *refs: final_kernel(*refs, model=model, seqs=seqs, chunks=chunks),
             out_shape=(jax.ShapeDtypeStruct((rows, model), BF16),) * 2,
-            in_specs=[smem, vmem, vmem],
+            in_specs=[smem, vmem, vmem, vmem],
             compiler_params=SMALL,
             cost_estimate=cost(2),
             name="rows_out",
-        )(where, held[0], arrived[0])
-
-        return context, grad_tokens
-
-    moved = [grad_w[0]] + [xor_permute(grad_w[j], "dp", j) for j in range(1, parts)]
-    context, grad_tokens = lax.cond(
-        global_blocks[0, 0] >= 0,
-        send_rows,
-        lambda keep, send: (jnp.zeros((rows, model), BF16),) * 2,
+        )(where, held[0], near, far)
+
+    grad_tokens, context = lax.cond(
+        live,
+        collect,
+        lambda *values: (jnp.zeros((rows, model), BF16),) * 2,
         keep,
         send,
     )

time: 85.1 us -> 81.8 us (0.961)
  local copies, waits for them, and re-layouts: 6.85 us -> 0.07 us
  Pallas kernels: 16 us -> 20.3 us
  starting transfers between devices: 23.9 us -> 22.5 us
  waiting for transfers between devices: 36.5 us -> 37.8 us
    unnamed x8, local copies, waits for them, and re-layouts: 3.33 us -> 0.02 us
    pallas_call x4, Pallas kernels: 1.78 us -> 4.95 us  [the longest x1 3.18 us: per_device(): pl.pallas_call(lambda *refs: pack_kernel(*refs, lefts=lefts, seqs=seqs, c...]
    dynamic_slice x3 -> x0, local copies, waits for them, and re-layouts: 2.68 us -> none  [slice_of(): return lax.dynamic_slice_in_dim(value, which * width, width, 1)]
    ppermute x18 -> x15, starting transfers between devices: 23.9 us -> 22.5 us  [xor_permute(): return lax.ppermute(value, axis, [(i, i ^ bit) for i in range(count)])]
    ppermute x18 -> x15, waiting for transfers between devices: 36.5 us -> 37.8 us  [xor_permute(): return lax.ppermute(value, axis, [(i, i ^ bit) for i in range(count)])]
    pallas_call x1, Pallas kernels: 12.8 us -> 13.9 us  [per_device(): pl.pallas_call(lambda *refs: attention_kernel(*refs, seqs=seqs, chunks=ch...]
  transfers between devices with their start and end apart: 18 -> 15, of which waited for: 8 -> 9; matrix products, arithmetic and copies ran while one was open for 4% -> 0% of each run, Pallas kernels for 2% -> 2%
where the time goes in v4:
time: 81.8 us; the launch traced here: 81.6 us
  waiting for transfers between devices  37.8 us (46%)
  starting transfers between devices  22.5 us (28%)
  Pallas kernels  20.3 us (25%)
    ppermute x15, waiting for transfers between devices, xor_permute(): return lax.ppermute(value, axis, [(i, i ^ bit) for i in range(count)])  37.8 us
    ppermute x15, starting transfers between devices, xor_permute(): return lax.ppermute(value, axis, [(i, i ^ bit) for i in range(count)])  22.5 us
    pallas_call x1, Pallas kernels, per_device(): pl.pallas_call(lambda *refs: attention_kernel(*refs, seqs=seqs, chunks=ch...  13.9 us
    pallas_call x1, Pallas kernels, per_device(): pl.pallas_call(lambda *refs: pack_kernel(*refs, lefts=lefts, seqs=seqs, c...  3.18 us
  transfers between devices with their start and end apart: 15, of which 9 were waited for; matrix products, arithmetic and copies ran while one was open for 0% of the time, Pallas kernels for 2%

profile of v4, /device:TPU:0, one launch (start us, length us, event | category | flops | bytes accessed | tf_op | source)
XLA Modules:
  0.0 81.6 jit_solution(5404547832870636776)
XLA Ops:
  0.7 3.2 %pack.1 = (bf16[128,1664]{1,0:T(8,128)(2,1)}, bf16[128,1280]{1,0:T(8,128)(2,1)}, bf16[128,1152]{1,0:T(8,128)(2,1)S(1)}, bf16[128,128]{1,0:T(8,128)(2,1)}, bf16[2...) custom-call(s32[3]{0:T(128)S(1)} %pad_add_fusion.refs_0_, s32[2]{0:T(128)} %bitcast.12, bf16[128,1024]{1,0:T(8,128)(2,1)} %bitcast.10, ...), custom_call_target="tpu_custom_call" | custom-call | bytes 6000000 | tf_op jit(solution)/shard_map/pack/pallas_call | solution.py:362
  3.9 3.1 %collective-permute-start.7 = (bf16[128,1664]{1,0:T(8,128)(2,1)}, bf16[128,1664]{1,0:T(8,128)(2,1)S(1)}, u32[]{:S(2)}, u32[]{:S(2)}) collective-permute-start(bf16[128,1664]{1,0:T(8,128)(2,1)} %get-tuple-element.54), channel_id=1, source_target_pairs={{0,1},{1,0},{2,3},{3,2},{4,5},{5,4},{6,7},{7,6},{8,9},{9,8},{10,11... | collective-permute-start | bytes 1277960 | tf_op jit(solution)/shard_map/ppermute | solution.py:33
  7.0 1.5 %collective-permute-start.8 = (bf16[128,1280]{1,0:T(8,128)(2,1)}, bf16[128,1280]{1,0:T(8,128)(2,1)S(1)}, u32[]{:S(2)}, u32[]{:S(2)}) collective-permute-start(bf16[128,1280]{1,0:T(8,128)(2,1)} %get-tuple-element.55), channel_id=1, source_target_pairs={{0,8},{4,12},{8,0},{12,4},{1,9},{5,13},{9,1},{13,5},{2,10},{6,14},... | collective-permute-start | bytes 983048 | tf_op jit(solution)/shard_map/ppermute | solution.py:33
  8.5 2.6 %collective-permute-start.10 = (bf16[256,384]{1,0:T(8,128)(2,1)}, bf16[256,384]{1,0:T(8,128)(2,1)S(1)}, u32[]{:S(2)}, u32[]{:S(2)}) collective-permute-start(bf16[256,384]{1,0:T(8,128)(2,1)} %get-tuple-element.61.refs_9_), channel_id=1, source_target_pairs={{0,2},{1,3},{2,0},{3,1},{4,6},{5,7},{6,4},{7,5},{8,10},{9,11},{10,... | collective-permute-start | bytes 589832 | tf_op jit(solution)/shard_map/ppermute | solution.py:33
  11.4 0.7 collective-permute-start.9
  12.1 4.4 %collective-permute-done.8.refs_4_ = bf16[128,1280]{1,0:T(8,128)(2,1)S(1)} collective-permute-done((bf16[128,1280]{1,0:T(8,128)(2,1)}, bf16[128,1280]{1,0:T(8,128)(2,1)S(1)}, u32[]{:S(2)}, u32[]{:S(2)}) %collective-permute-start.8) | collective-permute-done | bytes 327712 | tf_op jit(solution)/shard_map/ppermute | solution.py:33
  16.4 5.7 %collective-permute-done.7.refs_3_ = bf16[128,1664]{1,0:T(8,128)(2,1)S(1)} collective-permute-done((bf16[128,1664]{1,0:T(8,128)(2,1)}, bf16[128,1664]{1,0:T(8,128)(2,1)S(1)}, u32[]{:S(2)}, u32[]{:S(2)}) %collective-permute-start.7) | collective-permute-done | bytes 426016 | tf_op jit(solution)/shard_map/ppermute | solution.py:33
  22.1 11.4 %conditional.2 = (bf16[128,1280]{1,0:T(8,128)(2,1)}, bf16[384,1152]{1,0:T(8,128)(2,1)}, bf16[128,1280]{1,0:T(8,128)(2,1)}) conditional(s32[]{:T(128)} %bitcast.2, () %tuple.30, (bf16[128,1664]{1,0:T(8,128)(2,1)S(1)}, bf16[128,1280]{1,0:T(8,128)(2,1)S(1)}, bf16[128,1152]{1,0:T(8,128)(2,1)S(1)}) %tuple.31), branch_computations={%region_0.1_spmd, %region_1.2_spmd} | conditional | flops 5079040 | bytes 9896080 | solution.py:439
  22.2 2.3 %collective-permute-start.4 = (bf16[128,1280]{1,0:T(8,128)(2,1)S(1)}, bf16[128,1280]{1,0:T(8,128)(2,1)}, u32[]{:S(2)}, u32[]{:S(2)}) collective-permute-start(bf16[128,1280]{1,0:T(8,128)(2,1)S(1)} %pad_maximum_fusion), channel_id=1, source_target_pairs={{0,8},{4,12},{8,0},{12,4},{1,9},{5,13},{9,1},{13,5},{2,10},{6,14},... | collective-permute-start | bytes 983048 | tf_op jit(solution)/shard_map/cond/branch_1_fun/ppermute | solution.py:33
  24.6 5.8 %collective-permute-done.4 = bf16[128,1280]{1,0:T(8,128)(2,1)} collective-permute-done((bf16[128,1280]{1,0:T(8,128)(2,1)S(1)}, bf16[128,1280]{1,0:T(8,128)(2,1)}, u32[]{:S(2)}, u32[]{:S(2)}) %collective-permute-start.4) | collective-permute-done | bytes 327712 | tf_op jit(solution)/shard_map/cond/branch_1_fun/ppermute | solution.py:33
  30.5 0.5 collective-permute-start.6
  31.0 2.4 %collective-permute-done.6 = bf16[128,1280]{1,0:T(8,128)(2,1)} collective-permute-done((bf16[128,1280]{1,0:T(8,128)(2,1)}, bf16[128,1280]{1,0:T(8,128)(2,1)}, u32[]{:S(2)}, u32[]{:S(2)}) %collective-permute-start.6) | collective-permute-done | bytes 327712 | tf_op jit(solution)/shard_map/cond/branch_1_fun/ppermute | solution.py:33
  33.5 13.9 %attention.1 = (bf16[256,384]{1,0:T(8,128)(2,1)S(1)}, bf16[256,384]{1,0:T(8,128)(2,1)S(1)}, bf16[256,384]{1,0:T(8,128)(2,1)S(1)}, bf16[256,384]{1,0:T(8,128)(2,1...) custom-call(s32[3]{0:T(128)S(1)} %pad_add_fusion.refs_0_, s32[2]{0:T(128)S(1)} %bitcast.14, ...), custom_call_target="tpu_custom_call" | custom-call | bytes 39000000 | tf_op jit(solution)/shard_map/attention/pallas_call | solution.py:466
  47.5 7.8 %collective-permute-start.13 = (bf16[256,384]{1,0:T(8,128)(2,1)S(1)}, bf16[256,384]{1,0:T(8,128)(2,1)S(1)}, u32[]{:S(2)}, u32[]{:S(2)}) collective-permute-start(bf16[256,384]{1,0:T(8,128)(2,1)S(1)} %get-tuple-element.69), channel_id=1, source_target_pairs={{0,2},{1,3},{2,0},{3,1},{4,6},{5,7},{6,4},{7,5},{8,10},{9,11},{10,... | collective-permute-start | bytes 589832 | tf_op jit(solution)/shard_map/ppermute | solution.py:33
  55.3 24.8 %conditional.3 = (bf16[1,128,1024]{2,1,0:T(8,128)(2,1)}, bf16[1,128,1024]{2,1,0:T(8,128)(2,1)}) conditional(s32[]{:T(128)} %bitcast.2, () %tuple.29, (bf16[4,128,1152]{2,1,0:T(8,128)(2,1)S(1)}, bf16[4,128,1152]{2,1,0:T(8,128)(2,1)S(1)}, s32[3]{0:T(128)S(1)}) %tuple.32), branch_computations={%region_2.3_spmd, %region_3.4_spmd} | conditional | bytes 23913072 | solution.py:552
  55.3 2.8 %collective-permute-done.refs_1_ = bf16[4,128,1152]{2,1,0:T(8,128)(2,1)S(1)} collective-permute-done((bf16[4,128,1152]{2,1,0:T(8,128)(2,1)S(1)}, bf16[4,128,1152]{2,1,0:T(8,128)(2,1)S(1)}, u32[]{:S(2)}, u32[]{:S(2)}) %collective-permute-start) | collective-permute-done | bytes 1179680 | tf_op jit(solution)/shard_map/cond/branch_1_fun/ppermute | solution.py:33
  58.4 1.6 %collective-permute-start.2 = (bf16[128,1280]{1,0:T(8,128)(2,1)S(1)}, bf16[128,1280]{1,0:T(8,128)(2,1)S(1)}, u32[]{:S(2)}, u32[]{:S(2)}) collective-permute-start(bf16[128,1280]{1,0:T(8,128)(2,1)S(1)} %get-tuple-element.26), channel_id=1, source_target_pairs={{0,8},{4,12},{8,0},{12,4},{1,9},{5,13},{9,1},{13,5},{2,10},{6,14},... | collective-permute-start | bytes 983048 | tf_op jit(solution)/shard_map/cond/branch_1_fun/ppermute | solution.py:33
  60.0 8.3 %collective-permute-done.2.refs_1_ = bf16[128,1280]{1,0:T(8,128)(2,1)S(1)} collective-permute-done((bf16[128,1280]{1,0:T(8,128)(2,1)S(1)}, bf16[128,1280]{1,0:T(8,128)(2,1)S(1)}, u32[]{:S(2)}, u32[]{:S(2)}) %collective-permute-start.2) | collective-permute-done | bytes 327712 | tf_op jit(solution)/shard_map/cond/branch_1_fun/ppermute | solution.py:33
  68.3 0.6 collective-permute-start.3
  68.9 1.5 %collective-permute-start.1 = (bf16[128,1280]{1,0:T(8,128)(2,1)S(1)}, bf16[128,1280]{1,0:T(8,128)(2,1)S(1)}, u32[]{:S(2)}, u32[]{:S(2)}) collective-permute-start(bf16[128,1280]{1,0:T(8,128)(2,1)S(1)} %get-tuple-element.24), channel_id=1, source_target_pairs={{0,8},{4,12},{8,0},{12,4},{1,9},{5,13},{9,1},{13,5},{2,10},{6,14},... | collective-permute-start | bytes 983048 | tf_op jit(solution)/shard_map/cond/branch_1_fun/ppermute | solution.py:33
  70.4 7.1 %collective-permute-done.1.refs_2_ = bf16[128,1280]{1,0:T(8,128)(2,1)S(1)} collective-permute-done((bf16[128,1280]{1,0:T(8,128)(2,1)S(1)}, bf16[128,1280]{1,0:T(8,128)(2,1)S(1)}, u32[]{:S(2)}, u32[]{:S(2)}) %collective-permute-start.1) | collective-permute-done | bytes 327712 | tf_op jit(solution)/shard_map/cond/branch_1_fun/ppermute | solution.py:33
  77.6 1.1 %collective-permute-done.3.refs_3_ = bf16[128,1536]{1,0:T(8,128)(2,1)S(1)} collective-permute-done((bf16[128,1536]{1,0:T(8,128)(2,1)S(1)}, bf16[128,1536]{1,0:T(8,128)(2,1)S(1)}, u32[]{:S(2)}, u32[]{:S(2)}) %collective-permute-start.3) | collective-permute-done | bytes 393248 | tf_op jit(solution)/shard_map/cond/branch_1_fun/ppermute | solution.py:33
  78.7 1.5 %rows_out.1 = (bf16[128,1024]{1,0:T(8,128)(2,1)}, bf16[128,1024]{1,0:T(8,128)(2,1)}) custom-call(s32[3]{0:T(128)S(1)} %get-tuple-element.20.refs_0_, bf16[128,1280]{1,0:T(8,128)(2,1)S(1)} %get-tuple-element.23.refs_1_, bf16[128,1280]{1,0:T(8,128)(2,1)S(1)} %collective-permute-done.1.refs_2_, bf16[128,1536]{1,0:T(8,128)(2,1)S(1)} %collective-permute-done.3.refs_3_), custom_call_target="tpu_custom_call" | custom-call | bytes 6000000 | tf_op jit(solution)/shard_map/cond/branch_1_fun/rows_out/pallas_call | solution.py:543
  80.2 1.5 %weights_out.1 = (f32[256,256]{1,0:T(8,128)}, f32[256,256]{1,0:T(8,128)}, f32[256,256]{1,0:T(8,128)}) custom-call(s32[3]{0:T(128)S(1)} %pad_add_fusion.refs_0_, bf16[256,384]{1,0:T(8,128)(2,1)S(1)} %get-tuple-element.67.refs_1_, bf16[256,384]{1,0:T(8,128)(2,1)S(1)} %collective-permute-done.12.refs_2_, bf16[256,384]{1,0:T(8,128)(2,1)S(1)} %collective-permute-done.13.refs_3_, ...), custom_call_target="tpu_custom_call" | custom-call | bytes 6000000 | tf_op jit(solution)/shard_map/weights_out/pallas_call | solution.py:560
  (30 shorter events, 1.0 us)
Async XLA Ops:
  0.6 11.4 %copy-start.3 = (s32[1,2]{1,0:T(1,128)S(1)}, s32[1,2]{1,0:T(1,128)}, u32[]{:S(2)}) copy-start(s32[1,2]{1,0:T(1,128)} %param.11) | copy-start | bytes 28
  3.9 18.2 %collective-permute-start.7 = (bf16[128,1664]{1,0:T(8,128)(2,1)}, bf16[128,1664]{1,0:T(8,128)(2,1)S(1)}, u32[]{:S(2)}, u32[]{:S(2)}) collective-permute-start(bf16[128,1664]{1,0:T(8,128)(2,1)} %get-tuple-element.54), channel_id=1, source_target_pairs={{0,1},{1,0},{2,3},{3,2},{4,5},{5,4},{6,7},{7,6},{8,9},{9,8},{10,11... | collective-permute-start | bytes 1277960 | tf_op jit(solution)/shard_map/ppermute | solution.py:33
  7.0 9.4 %collective-permute-start.8 = (bf16[128,1280]{1,0:T(8,128)(2,1)}, bf16[128,1280]{1,0:T(8,128)(2,1)S(1)}, u32[]{:S(2)}, u32[]{:S(2)}) collective-permute-start(bf16[128,1280]{1,0:T(8,128)(2,1)} %get-tuple-element.55), channel_id=1, source_target_pairs={{0,8},{4,12},{8,0},{12,4},{1,9},{5,13},{9,1},{13,5},{2,10},{6,14},... | collective-permute-start | bytes 983048 | tf_op jit(solution)/shard_map/ppermute | solution.py:33
  8.5 25.0 %collective-permute-start.10 = (bf16[256,384]{1,0:T(8,128)(2,1)}, bf16[256,384]{1,0:T(8,128)(2,1)S(1)}, u32[]{:S(2)}, u32[]{:S(2)}) collective-permute-start(bf16[256,384]{1,0:T(8,128)(2,1)} %get-tuple-element.61.refs_9_), channel_id=1, source_target_pairs={{0,2},{1,3},{2,0},{3,1},{4,6},{5,7},{6,4},{7,5},{8,10},{9,11},{10,... | collective-permute-start | bytes 589832 | tf_op jit(solution)/shard_map/ppermute | solution.py:33
  11.1 22.4 %collective-permute-start.11 = (bf16[256,384]{1,0:T(8,128)(2,1)}, bf16[256,384]{1,0:T(8,128)(2,1)S(1)}, u32[]{:S(2)}, u32[]{:S(2)}) collective-permute-start(bf16[256,384]{1,0:T(8,128)(2,1)} %get-tuple-element.62), channel_id=1, source_target_pairs={{0,3},{1,2},{2,1},{3,0},{4,7},{5,6},{6,5},{7,4},{8,11},{9,10},{10,... | collective-permute-start | bytes 589832 | tf_op jit(solution)/shard_map/ppermute | solution.py:33
  11.4 22.2 %collective-permute-start.9 = (bf16[256,384]{1,0:T(8,128)(2,1)}, bf16[256,384]{1,0:T(8,128)(2,1)S(1)}, u32[]{:S(2)}, u32[]{:S(2)}) collective-permute-start(bf16[256,384]{1,0:T(8,128)(2,1)} %get-tuple-element.62), channel_id=1, source_target_pairs={{0,1},{1,0},{2,3},{3,2},{4,5},{5,4},{6,7},{7,6},{8,9},{9,8},{10,11... | collective-permute-start | bytes 589832 | tf_op jit(solution)/shard_map/ppermute | solution.py:33
  22.1 11.4 %copy-start = (bf16[1,128,1024]{2,1,0:T(8,128)(2,1)S(1)}, bf16[1,128,1024]{2,1,0:T(8,128)(2,1)}, u32[]{:S(2)}) copy-start(bf16[1,128,1024]{2,1,0:T(8,128)(2,1)} %param.10) | copy-start | bytes 786436
  22.1 11.4 %copy-start.1 = (bf16[256,384]{1,0:T(8,128)(2,1)S(1)}, bf16[256,384]{1,0:T(8,128)(2,1)}, u32[]{:S(2)}) copy-start(bf16[256,384]{1,0:T(8,128)(2,1)} %get-tuple-element.61.refs_9_) | copy-start | bytes 589828
  22.1 11.4 %copy-start.2 = (bf16[128,128]{1,0:T(8,128)(2,1)S(1)}, bf16[128,128]{1,0:T(8,128)(2,1)}, u32[]{:S(2)}) copy-start(bf16[128,128]{1,0:T(8,128)(2,1)} %get-tuple-element.60.refs_8_) | copy-start | bytes 98308
  22.2 8.3 %collective-permute-start.4 = (bf16[128,1280]{1,0:T(8,128)(2,1)S(1)}, bf16[128,1280]{1,0:T(8,128)(2,1)}, u32[]{:S(2)}, u32[]{:S(2)}) collective-permute-start(bf16[128,1280]{1,0:T(8,128)(2,1)S(1)} %pad_maximum_fusion), channel_id=1, source_target_pairs={{0,8},{4,12},{8,0},{12,4},{1,9},{5,13},{9,1},{13,5},{2,10},{6,14},... | collective-permute-start | bytes 983048 | tf_op jit(solution)/shard_map/cond/branch_1_fun/ppermute | solution.py:33
  30.5 3.0 %collective-permute-start.5 = (bf16[384,1152]{1,0:T(8,128)(2,1)S(1)}, bf16[384,1152]{1,0:T(8,128)(2,1)}, u32[]{:S(2)}, u32[]{:S(2)}) collective-permute-start(bf16[384,1152]{1,0:T(8,128)(2,1)S(1)} %maximum_maximum_fusion), channel_id=1, source_target_pairs={{0,4},{4,0},{8,12},{12,8},{1,5},{5,1},{9,13},{13,9},{2,6},{6,2},{1... | collective-permute-start | bytes 2654216 | tf_op jit(solution)/shard_map/cond/branch_1_fun/ppermute | solution.py:33
  30.5 2.9 %collective-permute-start.6 = (bf16[128,1280]{1,0:T(8,128)(2,1)}, bf16[128,1280]{1,0:T(8,128)(2,1)}, u32[]{:S(2)}, u32[]{:S(2)}) collective-permute-start(bf16[128,1280]{1,0:T(8,128)(2,1)} %collective-permute-done.4), channel_id=1, source_target_pairs={{0,4},{4,0},{8,12},{12,8},{1,5},{5,1},{9,13},{13,9},{2,6},{6,2},{1... | collective-permute-start | bytes 983048 | tf_op jit(solution)/shard_map/cond/branch_1_fun/ppermute | solution.py:33
  47.4 32.7 %collective-permute-start.12 = (bf16[256,384]{1,0:T(8,128)(2,1)S(1)}, bf16[256,384]{1,0:T(8,128)(2,1)S(1)}, u32[]{:S(2)}, u32[]{:S(2)}) collective-permute-start(bf16[256,384]{1,0:T(8,128)(2,1)S(1)} %get-tuple-element.68), channel_id=1, source_target_pairs={{0,1},{1,0},{2,3},{3,2},{4,5},{5,4},{6,7},{7,6},{8,9},{9,8},{10,11... | collective-permute-start | bytes 589832 | tf_op jit(solution)/shard_map/ppermute | solution.py:33
  47.5 32.6 %collective-permute-start.13 = (bf16[256,384]{1,0:T(8,128)(2,1)S(1)}, bf16[256,384]{1,0:T(8,128)(2,1)S(1)}, u32[]{:S(2)}, u32[]{:S(2)}) collective-permute-start(bf16[256,384]{1,0:T(8,128)(2,1)S(1)} %get-tuple-element.69), channel_id=1, source_target_pairs={{0,2},{1,3},{2,0},{3,1},{4,6},{5,7},{6,4},{7,5},{8,10},{9,11},{10,... | collective-permute-start | bytes 589832 | tf_op jit(solution)/shard_map/ppermute | solution.py:33
  55.3 24.8 %collective-permute-start.14 = (bf16[256,384]{1,0:T(8,128)(2,1)S(1)}, bf16[256,384]{1,0:T(8,128)(2,1)S(1)}, u32[]{:S(2)}, u32[]{:S(2)}) collective-permute-start(bf16[256,384]{1,0:T(8,128)(2,1)S(1)} %get-tuple-element.70), channel_id=1, source_target_pairs={{0,3},{1,2},{2,1},{3,0},{4,7},{5,6},{6,5},{7,4},{8,11},{9,10},{10,... | collective-permute-start | bytes 589832 | tf_op jit(solution)/shard_map/ppermute | solution.py:33
  55.3 2.8 %collective-permute-start = (bf16[4,128,1152]{2,1,0:T(8,128)(2,1)S(1)}, bf16[4,128,1152]{2,1,0:T(8,128)(2,1)S(1)}, u32[]{:S(2)}, u32[]{:S(2)}) collective-permute-start(bf16[4,128,1152]{2,1,0:T(8,128)(2,1)S(1)} %get-tuple-element.22), channel_id=1, source_target_pairs={{0,4},{4,0},{8,12},{12,8},{1,5},{5,1},{9,13},{13,9},{2,6},{6,2},{1... | collective-permute-start | bytes 3538952 | tf_op jit(solution)/shard_map/cond/branch_1_fun/ppermute | solution.py:33
  58.4 9.8 %collective-permute-start.2 = (bf16[128,1280]{1,0:T(8,128)(2,1)S(1)}, bf16[128,1280]{1,0:T(8,128)(2,1)S(1)}, u32[]{:S(2)}, u32[]{:S(2)}) collective-permute-start(bf16[128,1280]{1,0:T(8,128)(2,1)S(1)} %get-tuple-element.26), channel_id=1, source_target_pairs={{0,8},{4,12},{8,0},{12,4},{1,9},{5,13},{9,1},{13,5},{2,10},{6,14},... | collective-permute-start | bytes 983048 | tf_op jit(solution)/shard_map/cond/branch_1_fun/ppermute | solution.py:33
  68.3 10.4 %collective-permute-start.3 = (bf16[128,1536]{1,0:T(8,128)(2,1)S(1)}, bf16[128,1536]{1,0:T(8,128)(2,1)S(1)}, u32[]{:S(2)}, u32[]{:S(2)}) collective-permute-start(bf16[128,1536]{1,0:T(8,128)(2,1)S(1)} %join.1), channel_id=1, source_target_pairs={{0,1},{1,0},{2,3},{3,2},{4,5},{5,4},{6,7},{7,6},{8,9},{9,8},{10,11... | collective-permute-start | bytes 1179656 | tf_op jit(solution)/shard_map/cond/branch_1_fun/ppermute | solution.py:33
  68.9 8.6 %collective-permute-start.1 = (bf16[128,1280]{1,0:T(8,128)(2,1)S(1)}, bf16[128,1280]{1,0:T(8,128)(2,1)S(1)}, u32[]{:S(2)}, u32[]{:S(2)}) collective-permute-start(bf16[128,1280]{1,0:T(8,128)(2,1)S(1)} %get-tuple-element.24), channel_id=1, source_target_pairs={{0,8},{4,12},{8,0},{12,4},{1,9},{5,13},{9,1},{13,5},{2,10},{6,14},... | collective-permute-start | bytes 983048 | tf_op jit(solution)/shard_map/cond/branch_1_fun/ppermute | solution.py:33

commit v5 on v4

--- a/solution.py
+++ b/solution.py
@@ -34,21 +34,19 @@
 
 
 def attention_kernel(
-    where_ref, chosen_ref, *refs, seqs, chunks, rows, heads, hdim, parts, scale, sources, packed, ids_start
+    where_ref, chosen_ref, *refs, sources, chunks, far_ids, carry, rows, heads, hdim, parts, scale
 ):
-    pieces = seqs * chunks
-    half = pieces // 2
-    count = 1 + max(index for index, _, _ in sources)
-    token_refs = refs[:count]
-    ups = 1 if packed else count
-    up_refs = refs[count : count + ups]
-    weight_refs = refs[count + ups : count + ups + parts]
-    outs = refs[count + ups + parts :]
+    half = chunks // 2
+    count = 1 + max(max(source[0], source[3]) for source in sources)
+    buffers = refs[:count]
+    weight_refs = refs[count : count + parts]
+    carried = refs[count + parts : count + 2 * parts] if carry == "in" else None
+    outs = refs[count + (2 if carry == "in" else 1) * parts :]
     grad_w_refs = outs[:parts]
     keep_ref, send_ref = outs[parts : parts + 2]
-    all_tokens, weight, up_all, kv_s, kvt_s, pair_s, dkv_s, grads, context_s, far_ids, ids, sems = outs[
-        parts + 2 :
-    ]
+    (
+        all_tokens, weight, up_all, kv_s, kvt_s, pair_s, dkv_s, grads, context_s, noted, sems
+    ) = outs[parts + 2 :]
     length = chunks * rows
     width = heads * hdim
     model = all_tokens.shape[1]
@@ -60,17 +58,17 @@
     for j in range(parts):
         start = pl.multiple_of((line ^ j) * part_rows, part_rows)
         copies.append((weight_refs[j], weight.at[pl.ds(start, part_rows), :]))
-    for b, (index, first, start) in enumerate(sources):
-        held = pl.ds(first, rows)
-        target = pl.ds(b * rows, rows)
-        copies.append((token_refs[index].at[held, :model], all_tokens.at[target, :]))
-        if packed and b:
-            up = token_refs[index].at[held, start : start + width]
-        else:
-            up = up_refs[index].at[held, :]
-        copies.append((up, up_all.at[target, :]))
-    if seqs == 2:
-        copies.append((token_refs[1].at[:16, ids_start : ids_start + 128], far_ids))
+    at = 0
+    for index, first, size, up, start in sources:
+        target = pl.ds(at, size)
+        held = pl.ds(first, size)
+        copies.append((buffers[index].at[held, :model], all_tokens.at[target, :]))
+        if up != index:
+            held = pl.ds(0, size)
+        copies.append((buffers[up].at[held, start : start + width], up_all.at[target, :]))
+        at += size
+    if far_ids is not None:
+        copies.append((buffers[0].at[:16, far_ids : far_ids + 128], noted))
     copies = [
         pltpu.make_async_copy(source, target, sems.at[index])
         for index, (source, target) in enumerate(copies)
@@ -79,18 +77,18 @@
         copy.start()
     for copy in copies:
         copy.wait()
-    for k in range(2):
-        ids[0, k] = jnp.full((1, rows), chosen_ref[k], jnp.int32)
-        if seqs == 2:
-            far = far_ids[:, k * 64 : k * 64 + 1].astype(F32).astype(jnp.int32)
-            ids[1, k] = jnp.broadcast_to(far[:1], (1, rows))
+    if far_ids is None:
+        chosen = [chosen_ref[k] for k in range(2)]
+    else:
+        chosen = [noted[:1, 64 * k : 64 * k + 1].astype(F32).astype(jnp.int32) for k in range(2)]
+        chosen = [jnp.broadcast_to(value, (1, rows)) for value in chosen]
 
     pair_s[...] = jnp.zeros_like(pair_s)
     if SPAN < chunks:
         dkv_s[...] = jnp.zeros_like(dkv_s)
     tile = min(512, length)
 
-    @pl.loop(0, seqs * length // tile)
+    @pl.loop(0, length // tile)
     def _(t):
         at = pl.ds(pl.multiple_of(t * tile, tile), tile)
         out = jnp.dot(all_tokens[at, :], weight[...], preferred_element_type=F32)
@@ -109,7 +107,7 @@
             for p in range(tile // rows):
                 pair_s[h, t * (tile // rows) + p, :rows, :hdim] = q[p * rows : (p + 1) * rows]
     for h in range(heads):
-        for b in range(pieces):
+        for b in range(chunks):
             pair_s[h, b, rows:, hdim:] = up_all[
                 b * rows : (b + 1) * rows, h * hdim : (h + 1) * hdim
             ]
@@ -120,12 +118,9 @@
 
     span = min(SPAN, chunks)
 
-    @pl.loop(0, pieces // span)
+    @pl.loop(0, chunks // span)
     def _(t):
-        i = t // (chunks // span)
-        keys_at = pl.ds(pl.multiple_of(i * length, length), length)
-        first = ids[i, 0]
-        second = ids[i, 1]
+        first, second = chosen
         shape = (block_count, 1, rows)
         key = lax.broadcasted_iota(jnp.int32, shape, 0)
         key_block = (lax.shift_right_logical(key, log_blocks) ^ position) * blocks_per_chunk + (
@@ -136,7 +131,7 @@
         )
         biases = []
         for p in range(span):
-            j = t * span + p - i * chunks
+            j = t * span + p
             query_block = (position ^ j) * blocks_per_chunk + offset
             keep = (
                 (jnp.abs(key_block - query_block) <= 1)
@@ -148,7 +143,7 @@
             biases.append(jnp.where(keep, 0.0, NEG))
         for h in range(heads):
             pair = pair_s[h, pl.ds(t * span, span)].reshape(span * 2 * rows, 2 * hdim)
-            both = lax.dot_general(kv_s[h, keys_at, :], pair, NT, preferred_element_type=F32)
+            both = lax.dot_general(kv_s[h], pair, NT, preferred_element_type=F32)
             parts_of = [both[:, p * rows : (p + 1) * rows] for p in range(2 * span)]
             forward = []
             backward = []
@@ -169,7 +164,7 @@
                 backward += [low, probs.astype(BF16)]
                 inverses.append(inverse)
             sums = jnp.dot(
-                kvt_s[h, :, keys_at],
+                kvt_s[h],
                 jnp.concatenate(forward, axis=1),
                 preferred_element_type=F32,
             )
@@ -177,9 +172,9 @@
                 jnp.concatenate(backward, axis=1), pair, preferred_element_type=F32
             )
             if span == chunks:
-                dkv_s[h, keys_at, :] = dkv
+                dkv_s[h] = dkv
             else:
-                dkv_s[h, keys_at, :] += dkv
+                dkv_s[h] += dkv
             lo = h * hdim
             for p in range(span):
                 at = pl.ds(pl.multiple_of((t * span + p) * rows, rows), rows)
@@ -203,9 +198,10 @@
 
     for j in range(parts):
         cols = pl.ds(pl.multiple_of((line ^ j) * part_rows, part_rows), part_rows)
-        grad_w_refs[j][...] = lax.dot_general(
-            all_tokens[:, cols], grads[...], TN, preferred_element_type=F32
-        ).astype(BF16)
+        out = lax.dot_general(all_tokens[:, cols], grads[...], TN, preferred_element_type=F32)
+        if carry == "in":
+            out = out + carried[j][...]
+        grad_w_refs[j][...] = out.astype(grad_w_refs[j].dtype)
 
     @pl.loop(0, half)
     def _(t):
@@ -242,13 +238,16 @@
         lo += value.shape[1]
 
 
-def final_kernel(
-    where_ref, mine_ref, near_ref, far_ref, grad_ref, context_ref, *, model, seqs, chunks
-):
-    total, mine, near = add_and_join(mine_ref[...], near_ref[...], model)
+def final_kernel(where_ref, *refs, model, seqs, chunks):
+    far_ref, grad_ref, context_ref = refs[-3:]
+    if len(refs) == 5:
+        total, mine, near = add_and_join(refs[0][...], refs[1][...], model)
+        mine = jnp.concatenate([mine, near], axis=1)
+    else:
+        total = refs[0][:, :model]
+        mine = refs[0][:, model:]
     grad_ref[...] = (total.astype(F32) + far_ref[:, :model].astype(F32)).astype(BF16)
     theirs = far_ref[:, model:]
-    mine = jnp.concatenate([mine, near], axis=1)
     groups = seqs * chunks
     width = model // groups
     values = [mine[:, k * width : (k + 1) * width] for k in range(groups // 2)]
@@ -334,7 +333,7 @@
     chunks = lax.axis_size("ctx")
     parts = lax.axis_size("dp")
     seqs = 1
-    if parts % 2 == 0 and model % (chunks * 2 * 128) == 0 and HEADS % (chunks * 2) == 0:
+    if chunks == 4 and parts % 2 == 0 and model % 1024 == 0 and HEADS % 8 == 0:
         seqs = 2
     groups = chunks * seqs
     width = model // groups
@@ -395,126 +394,80 @@
             for i in range(seqs)
         ]
 
-    arrived = [xor_permute(own_sends[k], *hops[k][:2]) for k in range(2)]
+    arrived = [xor_permute(own_sends[k], *hops[k][:2]) for k in range(seqs)]
     weights = [sends[0]]
     for j in range(1, parts):
         weights.append(xor_permute(sends[j % seqs], "dp", j))
 
-    def by_age(keys):
-        return sorted(keys, key=lambda o: (o.bit_count(), o & hops[0][2]))
-
-    inner = [o for o in range(2, groups, 2) if o not in (hops[0][2], hops[1][2])]
-
-    def spread(near, far, *own):
-        pieces = {hops[0][2]: near}
-        for k in range(1, len(hops)):
-            axis, bit, offset = hops[k]
-            lo = model + lefts[k] * width
-            keys = by_age(pieces)
-            sends = [
-                jnp.concatenate(
-                    [pieces[key][:, :model], pieces[key][:, lo : lo + lefts[k] * width]], axis=1
-                )
-                for key in keys
-            ]
-            if k > 1:
-                keys = [0] + keys
-                sends = [own[k - 2]] + sends
-            if len(sends) > 1:
-                first = jnp.concatenate(sends[:-1], axis=0)
-                if k + 1 == len(hops):
-                    first, _ = lax.optimization_barrier((first, pieces[keys[-1]]))
-                first = xor_permute(first, axis, bit)
-                if k + 1 == len(hops):
-                    last = xor_permute(pieces[keys[-1]], axis, bit)
-                    return tuple(pieces[o] for o in inner) + (first, last)
-                for n, key in enumerate(keys[:-1]):
-                    pieces[key + offset] = first[n * rows : (n + 1) * rows]
-            pieces[keys[-1] + offset] = xor_permute(sends[-1], axis, bit)
-            if k == 1:
-                pieces[offset] = far
-
-    operands = (*arrived, *own_sends[2:])
+    length = chunks * rows
     live = global_blocks[0, 0] >= 0
-    spread_out = lax.cond(
-        live,
-        spread,
-        lambda *values: jax.tree.map(
-            lambda v: jnp.zeros(v.shape, v.dtype), jax.eval_shape(spread, *values)
-        ),
-        *operands,
-    )
-    buffers = [own_tokens, *arrived, *spread_out]
-    where_is = {0: (0, 0), hops[0][2]: (1, 0), hops[1][2]: (2, 0)}
-    for n, o in enumerate(inner):
-        where_is[o] = (3 + n, 0)
-    ordered = by_age(range(0, groups, 2))
-    for n, o in enumerate(ordered[:-1]):
-        where_is[o + 1] = (3 + len(inner), n * rows)
-    where_is[ordered[-1] + 1] = (4 + len(inner), 0)
-    late = ordered[-1] + 1
-    if packed:
-        up_buffers = [own_up]
-    else:
-        up_buffers = [own_up] + [v[:, model : model + width] for v in buffers[1:-1]]
-        up_buffers.append(buffers[-1][:, model + width : model + 2 * width])
-        buffers = [v[:, :model] for v in buffers]
-    sources = [where_is[o] + (model + (width if o == late else 0),) for o in range(groups)]
-
-    length = chunks * rows
-    total = seqs * length
-    results = pl.pallas_call(
-        lambda *refs: attention_kernel(
-            *refs,
-            seqs=seqs,
-            chunks=chunks,
-            rows=rows,
-            heads=heads,
-            hdim=hdim,
-            parts=parts,
-            scale=1.0 / math.sqrt(hdim),
-            sources=sources,
-            packed=packed,
-            ids_start=model + lefts[0] * width,
-        ),
-        out_shape=(jax.ShapeDtypeStruct((model // parts, 3 * width), BF16),) * parts
-        + (jax.ShapeDtypeStruct((groups // 2, rows, model + width), BF16),) * 2,
-        in_specs=[pl.BlockSpec(memory_space=pltpu.SMEM)] * 2
-        + [pl.BlockSpec(memory_space=pl.ANY)] * (len(buffers) + len(up_buffers) + parts),
-        out_specs=(pl.BlockSpec(memory_space=pltpu.VMEM),) * (parts + 2),
-        scratch_shapes=[
-            pltpu.VMEM((total, model), BF16),
-            pltpu.VMEM((model, 3 * width), BF16),
-            pltpu.VMEM((total, width), BF16),
-            pltpu.VMEM((heads, total, 2 * hdim), BF16),
-            pltpu.VMEM((heads, 2 * hdim, total), BF16),
-            pltpu.VMEM((heads, groups, 2 * rows, 2 * hdim), BF16),
-            pltpu.VMEM((heads, total, 2 * hdim), F32),
-            pltpu.VMEM((total, 3 * width), BF16),
-            pltpu.VMEM((total, width), BF16),
-            pltpu.VMEM((16, 128), BF16),
-            pltpu.VMEM((seqs, 2, 1, rows), jnp.int32),
-            pltpu.SemaphoreType.DMA((2 * groups + parts + 1,)),
-        ],
-        compiler_params=pltpu.CompilerParams(vmem_limit_bytes=24 * 1024 * 1024),
-        cost_estimate=cost(13),
-        name="attention",
-    )(
-        where,
-        chosen,
-        *buffers,
-        *up_buffers,
-        *weights,
-    )
-    grad_w = results[:parts]
-    keep, send = results[parts:]
-    moved = [grad_w[0]] + [xor_permute(grad_w[j], "dp", j) for j in range(1, parts)]
+
+    def guarded(function, *operands):
+        return lax.cond(
+            live,
+            function,
+            lambda *values: jax.tree.map(
+                lambda v: jnp.zeros(v.shape, v.dtype), jax.eval_shape(function, *values)
+            ),
+            *operands,
+        )
+
+    def attend(buffers, sources, weights, carry=None, carried=(), far_ids=None):
+        kind = F32 if carry == "out" else BF16
+        results = pl.pallas_call(
+            lambda *refs: attention_kernel(
+                *refs,
+                sources=sources,
+                chunks=chunks,
+                far_ids=far_ids,
+                carry=carry,
+                rows=rows,
+                heads=heads,
+                hdim=hdim,
+                parts=parts,
+                scale=1.0 / math.sqrt(hdim),
+            ),
+            out_shape=(jax.ShapeDtypeStruct((model // parts, 3 * width), kind),) * parts
+            + (jax.ShapeDtypeStruct((chunks // 2, rows, model + width), BF16),) * 2,
+            in_specs=[smem] * 2
+            + [pl.BlockSpec(memory_space=pl.ANY)] * (len(buffers) + parts)
+            + [vmem] * len(carried),
+            out_specs=(vmem,) * (parts + 2),
+            scratch_shapes=[
+                pltpu.VMEM((length, model), BF16),
+                pltpu.VMEM((model, 3 * width), BF16),
+                pltpu.VMEM((length, width), BF16),
+                pltpu.VMEM((heads, length, 2 * hdim), BF16),
+                pltpu.VMEM((heads, 2 * hdim, length), BF16),
+                pltpu.VMEM((heads, chunks, 2 * rows, 2 * hdim), BF16),
+                pltpu.VMEM((heads, length, 2 * hdim), F32),
+                pltpu.VMEM((length, 3 * width), BF16),
+                pltpu.VMEM((length, width), BF16),
+                pltpu.VMEM((16, 128), BF16),
+                pltpu.SemaphoreType.DMA((2 * len(sources) + parts + 1,)),
+            ],
+            compiler_params=pltpu.CompilerParams(vmem_limit_bytes=24 * 1024 * 1024),
+            cost_estimate=cost(14 // seqs),
+            name="attention",
+        )(where, chosen, *buffers, *weights, *carried)
+        return results[:parts], results[parts], results[parts + 1]
+
+    def combine(keep, got):
+        count = keep.shape[0]
+        return pl.pallas_call(
+            lambda *refs: combine_kernel(*refs, model=model),
+            out_shape=(jax.ShapeDtypeStruct((rows, model + 2 * width), BF16),) * count,
+            in_specs=[vmem] * 2,
+            out_specs=(vmem,) * count,
+            compiler_params=SMALL,
+            cost_estimate=cost(1),
+            name="combine",
+        )(keep, got)
 
     def join(mine, theirs):
-        columns = 2 * mine.shape[1] - model
         return pl.pallas_call(
             lambda *refs: join_kernel(*refs, model=model),
-            out_shape=jax.ShapeDtypeStruct((rows, columns), BF16),
+            out_shape=jax.ShapeDtypeStruct((rows, 2 * mine.shape[1] - model), BF16),
             in_specs=[vmem] * 2,
             out_specs=vmem,
             compiler_params=SMALL,
@@ -522,40 +475,112 @@
             name="join",
         )(mine, theirs)
 
-    def collect(keep, send):
-        got = xor_permute(send, *hops[-1][:2])
-        columns = model + 2 * width
-        held = pl.pallas_call(
-            lambda *refs: combine_kernel(*refs, model=model),
-            out_shape=(jax.ShapeDtypeStruct((rows, columns), BF16),) * (groups // 2),
-            in_specs=[vmem] * 2,
-            out_specs=(vmem,) * (groups // 2),
-            compiler_params=SMALL,
-            cost_estimate=cost(2),
-            name="combine",
-        )(keep, got)
-        for axis, bit, _ in reversed(hops[2:-1]):
-            theirs = [xor_permute(value, axis, bit) for value in held[1::2]]
-            held = [join(*pair) for pair in zip(held[::2], theirs)]
-        far = join(held[2], xor_permute(held[3], *hops[1][:2]))
-        far = xor_permute(far, *hops[0][:2])
-        near = xor_permute(held[1], *hops[1][:2])
+    def finish(*values):
         return pl.pallas_call(
             lambda *refs: final_kernel(*refs, model=model, seqs=seqs, chunks=chunks),
             out_shape=(jax.ShapeDtypeStruct((rows, model), BF16),) * 2,
-            in_specs=[smem, vmem, vmem, vmem],
+            in_specs=[smem] + [vmem] * len(values),
             compiler_params=SMALL,
             cost_estimate=cost(2),
             name="rows_out",
-        )(where, held[0], near, far)
-
-    grad_tokens, context = lax.cond(
-        live,
-        collect,
-        lambda *values: (jnp.zeros((rows, model), BF16),) * 2,
-        keep,
-        send,
-    )
+        )(where, *values)
+
+    if seqs == 2:
+        line_hop, far_hop, near_hop = [hop[:2] for hop in hops]
+        tz, tx = arrived
+
+        def share(own, tx):
+            rest = jnp.concatenate([tx[:, :model], tx[:, model + width :]], axis=1)
+            return xor_permute(jnp.concatenate([own, rest], axis=0), *near_hop)
+
+        shared = guarded(share, own_sends[2], tx)
+
+        def both(tz, tx, shared, own_tokens, own_up, *weights):
+            lo = model + 2 * width
+            part = rows // 2
+            txz = [
+                xor_permute(
+                    jnp.concatenate([piece[:, :model], piece[:, lo : lo + 2 * width]], axis=1),
+                    *far_hop,
+                )
+                for piece in (tz[:part], tz[part:])
+            ]
+            first, keep, send = attend(
+                (own_tokens, shared, tx, own_up),
+                (
+                    (0, 0, rows, 3, 0),
+                    (1, 0, rows, 1, model),
+                    (2, 0, rows, 2, model),
+                    (1, rows, rows, 1, model),
+                ),
+                weights,
+                carry="out",
+            )
+            first = list(first)
+            txz, first[0] = lax.optimization_barrier((txz, first[0]))
+            ctz = xor_permute(tz, *near_hop)
+            ctxz = [xor_permute(piece, *near_hop) for piece in txz]
+            up = model + width
+            grad_w, keep_other, send_other = attend(
+                (tz, ctz, *txz, *ctxz),
+                (
+                    (0, 0, rows, 0, model),
+                    (1, 0, rows, 1, up),
+                    (2, 0, part, 2, model),
+                    (3, 0, part, 3, model),
+                    (4, 0, part, 4, up),
+                    (5, 0, part, 5, up),
+                ),
+                weights,
+                carry="in",
+                carried=first,
+                far_ids=model + 4 * width,
+            )
+            return grad_w, keep, send, keep_other, send_other
+
+        grad_w, *rest = both(tz, tx, shared, own_tokens, own_up, *weights)
+
+        def collect(keep, send, keep_other, send_other):
+            held, far = combine(keep_other, xor_permute(send_other, *near_hop))
+            mine, near = combine(keep, xor_permute(send, *near_hop))
+            held = join(held, xor_permute(far, *far_hop))
+            far = xor_permute(held, *line_hop)
+            return finish(mine, xor_permute(near, *far_hop), far)
+
+        moved = [grad_w[0]] + [xor_permute(grad_w[j], "dp", j) for j in range(1, parts)]
+        grad_tokens, context = guarded(collect, *rest)
+    else:
+
+        def spread(first, *own):
+            pieces = {hops[0][2]: first}
+            for k in range(1, len(hops)):
+                axis, bit, offset = hops[k]
+                lo = model + lefts[k] * width
+                for key in list(pieces):
+                    value = pieces[key]
+                    value = jnp.concatenate(
+                        [value[:, :model], value[:, lo : lo + lefts[k] * width]], axis=1
+                    )
+                    pieces[key + offset] = xor_permute(value, axis, bit)
+                pieces[offset] = xor_permute(own[k - 1], axis, bit)
+            return tuple(pieces[o] for o in range(1, groups))
+
+        pieces = guarded(spread, arrived[0], *own_sends[1:])
+        ups = [own_up] + [value[:, model : model + width] for value in pieces]
+        buffers = [own_tokens] + [value[:, :model] for value in pieces] + ups
+        grad_w, keep, send = attend(
+            buffers, [(o, 0, rows, groups + o, 0) for o in range(groups)], weights
+        )
+
+        def collect(keep, send):
+            held = combine(keep, xor_permute(send, *hops[-1][:2]))
+            for axis, bit, _ in reversed(hops[1:-1]):
+                theirs = [xor_permute(value, axis, bit) for value in held[1::2]]
+                held = [join(*pair) for pair in zip(held[::2], theirs)]
+            return finish(held[0], xor_permute(held[1], *hops[0][:2]))
+
+        moved = [grad_w[0]] + [xor_permute(grad_w[j], "dp", j) for j in range(1, parts)]
+        grad_tokens, context = guarded(collect, keep, send)
 
     final = pl.pallas_call(
         lambda *refs: sum_kernel(*refs, parts=parts, seqs=seqs, width=width),

time: 81.8 us -> 77.9 us (0.952)
  waiting for transfers between devices: 37.8 us -> 33.2 us
  Pallas kernels: 20.3 us -> 21.6 us
    ppermute x15 -> x19, waiting for transfers between devices: 37.8 us -> 33.2 us  [xor_permute(): return lax.ppermute(value, axis, [(i, i ^ bit) for i in range(count)])]
    pallas_call x3 -> x5, Pallas kernels: 15.6 us -> 16.8 us  [the longest x2 15.1 us: attend(): pl.pallas_call(lambda *refs: attention_kernel(*refs, sources=sources, chu...]
    ppermute x15 -> x19, starting transfers between devices: 22.5 us -> 21.8 us  [xor_permute(): return lax.ppermute(value, axis, [(i, i ^ bit) for i in range(count)])]
  transfers between devices with their start and end apart: 15 -> 19, of which waited for: 9 -> 10; matrix products, arithmetic and copies ran while one was open for 0% -> 0% of each run, Pallas kernels for 2% -> 13%
where the time goes in v5:
time: 77.9 us; the launch traced here: 77.7 us
  waiting for transfers between devices  33.2 us (43%)
  starting transfers between devices  21.8 us (28%)
  Pallas kernels  21.6 us (28%)
  between operations  0.81 us (1%)
    ppermute x19, waiting for transfers between devices, xor_permute(): return lax.ppermute(value, axis, [(i, i ^ bit) for i in range(count)])  33.2 us
    ppermute x19, starting transfers between devices, xor_permute(): return lax.ppermute(value, axis, [(i, i ^ bit) for i in range(count)])  21.8 us
    pallas_call x2, Pallas kernels, attend(): pl.pallas_call(lambda *refs: attention_kernel(*refs, sources=sources, chu...  15.1 us
    pallas_call x1, Pallas kernels, per_device(): pl.pallas_call(lambda *refs: pack_kernel(*refs, lefts=lefts, seqs=seqs, c...  3.31 us
  transfers between devices with their start and end apart: 19, of which 10 were waited for; matrix products, arithmetic and copies ran while one was open for 0% of the time, Pallas kernels for 13%

profile of v5, /device:TPU:0, one launch (start us, length us, event | category | flops | bytes accessed | tf_op | source)
XLA Modules:
  0.0 77.7 jit_solution(6857339141390906822)
XLA Ops:
  0.7 3.3 %pack.1 = (bf16[128,1664]{1,0:T(8,128)(2,1)}, bf16[128,1280]{1,0:T(8,128)(2,1)}, bf16[128,1152]{1,0:T(8,128)(2,1)S(1)}, bf16[128,128]{1,0:T(8,128)(2,1)}, bf16[2...) custom-call(s32[3]{0:T(128)S(1)} %pad_add_fusion.refs_0_, s32[2]{0:T(128)} %bitcast.12, bf16[128,1024]{1,0:T(8,128)(2,1)} %bitcast.10, ...), custom_call_target="tpu_custom_call" | custom-call | bytes 6000000 | tf_op jit(solution)/shard_map/pack/pallas_call | solution.py:361
  4.0 3.1 %collective-permute-start.10 = (bf16[128,1664]{1,0:T(8,128)(2,1)}, bf16[128,1664]{1,0:T(8,128)(2,1)S(1)}, u32[]{:S(2)}, u32[]{:S(2)}) collective-permute-start(bf16[128,1664]{1,0:T(8,128)(2,1)} %get-tuple-element.72), channel_id=1, source_target_pairs={{0,1},{1,0},{2,3},{3,2},{4,5},{5,4},{6,7},{7,6},{8,9},{9,8},{10,11... | collective-permute-start | bytes 1277960 | tf_op jit(solution)/shard_map/ppermute | solution.py:33
  7.2 1.5 %collective-permute-start.6 = (bf16[128,1280]{1,0:T(8,128)(2,1)}, bf16[128,1280]{1,0:T(8,128)(2,1)S(1)}, u32[]{:S(2)}, u32[]{:S(2)}) collective-permute-start(bf16[128,1280]{1,0:T(8,128)(2,1)} %get-tuple-element.65), channel_id=1, source_target_pairs={{0,8},{4,12},{8,0},{12,4},{1,9},{5,13},{9,1},{13,5},{2,10},{6,14},... | collective-permute-start | bytes 983048 | tf_op jit(solution)/shard_map/ppermute | solution.py:33
  8.6 2.5 %collective-permute-start.9 = (bf16[256,384]{1,0:T(8,128)(2,1)}, bf16[256,384]{1,0:T(8,128)(2,1)S(1)}, u32[]{:S(2)}, u32[]{:S(2)}) collective-permute-start(bf16[256,384]{1,0:T(8,128)(2,1)} %get-tuple-element.69), channel_id=1, source_target_pairs={{0,3},{1,2},{2,1},{3,0},{4,7},{5,6},{6,5},{7,4},{8,11},{9,10},{10,... | collective-permute-start | bytes 589832 | tf_op jit(solution)/shard_map/ppermute | solution.py:33
  11.8 1.2 %collective-permute-start.8 = (bf16[256,384]{1,0:T(8,128)(2,1)}, bf16[256,384]{1,0:T(8,128)(2,1)S(1)}, u32[]{:S(2)}, u32[]{:S(2)}) collective-permute-start(bf16[256,384]{1,0:T(8,128)(2,1)} %get-tuple-element.68.refs_6_.refs_8_), channel_id=1, source_target_pairs={{0,2},{1,3},{2,0},{3,1},{4,6},{5,7},{6,4},{7,5},{8,10},{9,11},{10,... | collective-permute-start | bytes 589832 | tf_op jit(solution)/shard_map/ppermute | solution.py:33
  13.1 3.5 %collective-permute-done.6.refs_4_ = bf16[128,1280]{1,0:T(8,128)(2,1)S(1)} collective-permute-done((bf16[128,1280]{1,0:T(8,128)(2,1)}, bf16[128,1280]{1,0:T(8,128)(2,1)S(1)}, u32[]{:S(2)}, u32[]{:S(2)}) %collective-permute-start.6) | collective-permute-done | bytes 327712 | tf_op jit(solution)/shard_map/ppermute | solution.py:33
  16.6 2.3 %conditional.2 = (bf16[256,1152]{1,0:T(8,128)(2,1)}) conditional(s32[]{:T(128)} %bitcast.2, () %tuple.28, (bf16[128,1280]{1,0:T(8,128)(2,1)S(1)}, bf16[128,1152]{1,0:T(8,128)(2,1)S(1)}) %tuple.29), branch_computations={%region_0.1_spmd, %region_1.2_spmd} | conditional | flops 1769472 | bytes 4128816 | solution.py:406
  16.7 2.1 %collective-permute-done.5 = bf16[256,1152]{1,0:T(8,128)(2,1)} collective-permute-done((bf16[256,1152]{1,0:T(8,128)(2,1)S(1)}, bf16[256,1152]{1,0:T(8,128)(2,1)}, u32[]{:S(2)}, u32[]{:S(2)}) %collective-permute-start.5) | collective-permute-done | bytes 589856 | tf_op jit(solution)/shard_map/cond/branch_1_fun/ppermute | solution.py:33
  18.9 7.6 %collective-permute-done.10.refs_2_ = bf16[128,1664]{1,0:T(8,128)(2,1)S(1)} collective-permute-done((bf16[128,1664]{1,0:T(8,128)(2,1)}, bf16[128,1664]{1,0:T(8,128)(2,1)S(1)}, u32[]{:S(2)}, u32[]{:S(2)}) %collective-permute-start.10) | collective-permute-done | bytes 426016 | tf_op jit(solution)/shard_map/ppermute | solution.py:33
  26.5 2.1 %collective-permute-start.12 = (bf16[64,1280]{1,0:T(8,128)(2,1)S(1)}, bf16[64,1280]{1,0:T(8,128)(2,1)S(1)}, u32[]{:S(2)}, u32[]{:S(2)}) collective-permute-start(bf16[64,1280]{1,0:T(8,128)(2,1)S(1)} %pad_maximum_fusion), channel_id=1, source_target_pairs={{0,8},{4,12},{8,0},{12,4},{1,9},{5,13},{9,1},{13,5},{2,10},{6,14},... | collective-permute-start | bytes 491528 | tf_op jit(solution)/shard_map/ppermute | solution.py:33
  28.8 1.1 %collective-permute-done.7.refs_7_.refs_9_ = bf16[256,384]{1,0:T(8,128)(2,1)S(1)} collective-permute-done((bf16[256,384]{1,0:T(8,128)(2,1)}, bf16[256,384]{1,0:T(8,128)(2,1)S(1)}, u32[]{:S(2)}, u32[]{:S(2)}) %collective-permute-start.7) | collective-permute-done | bytes 196640 | tf_op jit(solution)/shard_map/ppermute | solution.py:33
  29.9 8.0 %attention.2 = (f32[256,384]{1,0:T(8,128)S(1)}, f32[256,384]{1,0:T(8,128)S(1)}, f32[256,384]{1,0:T(8,128)S(1)}, f32[256,384]{1,0:T(8,128)S(1)}, bf16[2,128,1152]...) custom-call(s32[3]{0:T(128)S(1)} %pad_add_fusion.refs_0_, s32[2]{0:T(128)S(1)} %bitcast.14, ...), custom_call_target="tpu_custom_call" | custom-call | bytes 21000000 | tf_op jit(solution)/shard_map/attention/pallas_call | solution.py:417
  39.6 7.1 %attention.3 = (bf16[256,384]{1,0:T(8,128)(2,1)S(1)}, bf16[256,384]{1,0:T(8,128)(2,1)S(1)}, bf16[256,384]{1,0:T(8,128)(2,1)S(1)}, bf16[256,384]{1,0:T(8,128)(2,1...) custom-call(s32[3]{0:T(128)S(1)} %pad_add_fusion.refs_0_, s32[2]{0:T(128)S(1)} %bitcast.15, ...), custom_call_target="tpu_custom_call" | custom-call | bytes 21000000 | tf_op jit(solution)/shard_map/attention/pallas_call | solution.py:417
  46.7 2.9 %collective-permute-start.16 = (bf16[256,384]{1,0:T(8,128)(2,1)S(1)}, bf16[256,384]{1,0:T(8,128)(2,1)S(1)}, u32[]{:S(2)}, u32[]{:S(2)}) collective-permute-start(bf16[256,384]{1,0:T(8,128)(2,1)S(1)} %get-tuple-element.85), channel_id=1, source_target_pairs={{0,1},{1,0},{2,3},{3,2},{4,5},{5,4},{6,7},{7,6},{8,9},{9,8},{10,11... | collective-permute-start | bytes 589832 | tf_op jit(solution)/shard_map/ppermute | solution.py:33
  49.6 1.5 %collective-permute-start.17 = (bf16[256,384]{1,0:T(8,128)(2,1)S(1)}, bf16[256,384]{1,0:T(8,128)(2,1)S(1)}, u32[]{:S(2)}, u32[]{:S(2)}) collective-permute-start(bf16[256,384]{1,0:T(8,128)(2,1)S(1)} %get-tuple-element.86), channel_id=1, source_target_pairs={{0,2},{1,3},{2,0},{3,1},{4,6},{5,7},{6,4},{7,5},{8,10},{9,11},{10,... | collective-permute-start | bytes 589832 | tf_op jit(solution)/shard_map/ppermute | solution.py:33
  52.0 24.2 %conditional.3 = (bf16[1,128,1024]{2,1,0:T(8,128)(2,1)}, bf16[1,128,1024]{2,1,0:T(8,128)(2,1)}) conditional(s32[]{:T(128)} %bitcast.2, () %tuple.27, (bf16[2,128,1152]{2,1,0:T(8,128)(2,1)S(1)}, bf16[2,128,1152]{2,1,0:T(8,128)(2,1)S(1)}, bf16[2,128,1152]{2,1,0:T(8,128)(2,1)S(1)}, bf16[2,128,1152]{2,1,0:T(8,128)(2,1)S(1)}, s32[3]{0:T(128)S(1)}) %tuple.31), branch_computations={%region_2.3_spmd, %region_3.4_spmd} | conditional | bytes 23913112 | solution.py:406
  52.5 1.5 %collective-permute-done.2.refs_1_ = bf16[2,128,1152]{2,1,0:T(8,128)(2,1)S(1)} collective-permute-done((bf16[2,128,1152]{2,1,0:T(8,128)(2,1)S(1)}, bf16[2,128,1152]{2,1,0:T(8,128)(2,1)S(1)}, u32[]{:S(2)}, u32[]{:S(2)}) %collective-permute-start.2) | collective-permute-done | bytes 589856 | tf_op jit(solution)/shard_map/cond/branch_1_fun/ppermute | solution.py:33
  54.1 1.5 %collective-permute-start.3 = (bf16[128,1280]{1,0:T(8,128)(2,1)S(1)}, bf16[128,1280]{1,0:T(8,128)(2,1)S(1)}, u32[]{:S(2)}, u32[]{:S(2)}) collective-permute-start(bf16[128,1280]{1,0:T(8,128)(2,1)S(1)} %get-tuple-element.31), channel_id=1, source_target_pairs={{0,8},{4,12},{8,0},{12,4},{1,9},{5,13},{9,1},{13,5},{2,10},{6,14},... | collective-permute-start | bytes 983048 | tf_op jit(solution)/shard_map/cond/branch_1_fun/ppermute | solution.py:33
  55.7 8.3 %collective-permute-done.3.refs_1_ = bf16[128,1280]{1,0:T(8,128)(2,1)S(1)} collective-permute-done((bf16[128,1280]{1,0:T(8,128)(2,1)S(1)}, bf16[128,1280]{1,0:T(8,128)(2,1)S(1)}, u32[]{:S(2)}, u32[]{:S(2)}) %collective-permute-start.3) | collective-permute-done | bytes 327712 | tf_op jit(solution)/shard_map/cond/branch_1_fun/ppermute | solution.py:33
  64.0 1.1 %collective-permute-start.4 = (bf16[128,1536]{1,0:T(8,128)(2,1)S(1)}, bf16[128,1536]{1,0:T(8,128)(2,1)S(1)}, u32[]{:S(2)}, u32[]{:S(2)}) collective-permute-start(bf16[128,1536]{1,0:T(8,128)(2,1)S(1)} %join.1), channel_id=1, source_target_pairs={{0,1},{1,0},{2,3},{3,2},{4,5},{5,4},{6,7},{7,6},{8,9},{9,8},{10,11... | collective-permute-start | bytes 1179656 | tf_op jit(solution)/shard_map/cond/branch_1_fun/ppermute | solution.py:33
  65.3 1.5 %collective-permute-start.1 = (bf16[128,1280]{1,0:T(8,128)(2,1)S(1)}, bf16[128,1280]{1,0:T(8,128)(2,1)S(1)}, u32[]{:S(2)}, u32[]{:S(2)}) collective-permute-start(bf16[128,1280]{1,0:T(8,128)(2,1)S(1)} %get-tuple-element.27), channel_id=1, source_target_pairs={{0,8},{4,12},{8,0},{12,4},{1,9},{5,13},{9,1},{13,5},{2,10},{6,14},... | collective-permute-start | bytes 983048 | tf_op jit(solution)/shard_map/cond/branch_1_fun/ppermute | solution.py:33
  66.8 7.2 %collective-permute-done.1.refs_2_ = bf16[128,1280]{1,0:T(8,128)(2,1)S(1)} collective-permute-done((bf16[128,1280]{1,0:T(8,128)(2,1)S(1)}, bf16[128,1280]{1,0:T(8,128)(2,1)S(1)}, u32[]{:S(2)}, u32[]{:S(2)}) %collective-permute-start.1) | collective-permute-done | bytes 327712 | tf_op jit(solution)/shard_map/cond/branch_1_fun/ppermute | solution.py:33
  74.8 1.5 %rows_out.1 = (bf16[128,1024]{1,0:T(8,128)(2,1)}, bf16[128,1024]{1,0:T(8,128)(2,1)}) custom-call(s32[3]{0:T(128)S(1)} %get-tuple-element.23.refs_0_, bf16[128,1280]{1,0:T(8,128)(2,1)S(1)} %get-tuple-element.26.refs_1_, bf16[128,1280]{1,0:T(8,128)(2,1)S(1)} %collective-permute-done.1.refs_2_, bf16[128,1536]{1,0:T(8,128)(2,1)S(1)} %collective-permute-done.4.refs_3_), custom_call_target="tpu_custom_call" | custom-call | bytes 6000000 | tf_op jit(solution)/shard_map/cond/branch_1_fun/rows_out/pallas_call | solution.py:479
  76.3 1.5 %weights_out.1 = (f32[256,256]{1,0:T(8,128)}, f32[256,256]{1,0:T(8,128)}, f32[256,256]{1,0:T(8,128)}) custom-call(s32[3]{0:T(128)S(1)} %pad_add_fusion.refs_0_, bf16[256,384]{1,0:T(8,128)(2,1)S(1)} %get-tuple-element.84.refs_1_, bf16[256,384]{1,0:T(8,128)(2,1)S(1)} %collective-permute-done.16.refs_2_, bf16[256,384]{1,0:T(8,128)(2,1)S(1)} %collective-permute-done.17.refs_3_, ...), custom_call_target="tpu_custom_call" | custom-call | bytes 6000000 | tf_op jit(solution)/shard_map/weights_out/pallas_call | solution.py:585
  (40 shorter events, 5.4 us)
Async XLA Ops:
  0.7 12.3 %copy-start.3 = (s32[1,2]{1,0:T(1,128)S(1)}, s32[1,2]{1,0:T(1,128)}, u32[]{:S(2)}) copy-start(s32[1,2]{1,0:T(1,128)} %param.11) | copy-start | bytes 28
  4.0 22.4 %collective-permute-start.10 = (bf16[128,1664]{1,0:T(8,128)(2,1)}, bf16[128,1664]{1,0:T(8,128)(2,1)S(1)}, u32[]{:S(2)}, u32[]{:S(2)}) collective-permute-start(bf16[128,1664]{1,0:T(8,128)(2,1)} %get-tuple-element.72), channel_id=1, source_target_pairs={{0,1},{1,0},{2,3},{3,2},{4,5},{5,4},{6,7},{7,6},{8,9},{9,8},{10,11... | collective-permute-start | bytes 1277960 | tf_op jit(solution)/shard_map/ppermute | solution.py:33
  7.2 9.4 %collective-permute-start.6 = (bf16[128,1280]{1,0:T(8,128)(2,1)}, bf16[128,1280]{1,0:T(8,128)(2,1)S(1)}, u32[]{:S(2)}, u32[]{:S(2)}) collective-permute-start(bf16[128,1280]{1,0:T(8,128)(2,1)} %get-tuple-element.65), channel_id=1, source_target_pairs={{0,8},{4,12},{8,0},{12,4},{1,9},{5,13},{9,1},{13,5},{2,10},{6,14},... | collective-permute-start | bytes 983048 | tf_op jit(solution)/shard_map/ppermute | solution.py:33
  8.6 20.0 %collective-permute-start.9 = (bf16[256,384]{1,0:T(8,128)(2,1)}, bf16[256,384]{1,0:T(8,128)(2,1)S(1)}, u32[]{:S(2)}, u32[]{:S(2)}) collective-permute-start(bf16[256,384]{1,0:T(8,128)(2,1)} %get-tuple-element.69), channel_id=1, source_target_pairs={{0,3},{1,2},{2,1},{3,0},{4,7},{5,6},{6,5},{7,4},{8,11},{9,10},{10,... | collective-permute-start | bytes 589832 | tf_op jit(solution)/shard_map/ppermute | solution.py:33
  11.1 18.7 %collective-permute-start.7 = (bf16[256,384]{1,0:T(8,128)(2,1)}, bf16[256,384]{1,0:T(8,128)(2,1)S(1)}, u32[]{:S(2)}, u32[]{:S(2)}) collective-permute-start(bf16[256,384]{1,0:T(8,128)(2,1)} %get-tuple-element.69), channel_id=1, source_target_pairs={{0,1},{1,0},{2,3},{3,2},{4,5},{5,4},{6,7},{7,6},{8,9},{9,8},{10,11... | collective-permute-start | bytes 589832 | tf_op jit(solution)/shard_map/ppermute | solution.py:33
  11.8 18.0 %collective-permute-start.8 = (bf16[256,384]{1,0:T(8,128)(2,1)}, bf16[256,384]{1,0:T(8,128)(2,1)S(1)}, u32[]{:S(2)}, u32[]{:S(2)}) collective-permute-start(bf16[256,384]{1,0:T(8,128)(2,1)} %get-tuple-element.68.refs_6_.refs_8_), channel_id=1, source_target_pairs={{0,2},{1,3},{2,0},{3,1},{4,6},{5,7},{6,4},{7,5},{8,10},{9,11},{10,... | collective-permute-start | bytes 589832 | tf_op jit(solution)/shard_map/ppermute | solution.py:33
  16.6 2.2 %collective-permute-start.5 = (bf16[256,1152]{1,0:T(8,128)(2,1)S(1)}, bf16[256,1152]{1,0:T(8,128)(2,1)}, u32[]{:S(2)}, u32[]{:S(2)}) collective-permute-start(bf16[256,1152]{1,0:T(8,128)(2,1)S(1)} %maximum_maximum_fusion), channel_id=1, source_target_pairs={{0,4},{4,0},{8,12},{12,8},{1,5},{5,1},{9,13},{13,9},{2,6},{6,2},{1... | collective-permute-start | bytes 1769480 | tf_op jit(solution)/shard_map/cond/branch_1_fun/ppermute | solution.py:33
  26.4 3.4 %copy-start = (bf16[1,128,1024]{2,1,0:T(8,128)(2,1)S(1)}, bf16[1,128,1024]{2,1,0:T(8,128)(2,1)}, u32[]{:S(2)}) copy-start(bf16[1,128,1024]{2,1,0:T(8,128)(2,1)} %param.10) | copy-start | bytes 786436
  26.4 3.4 %copy-start.1 = (bf16[256,384]{1,0:T(8,128)(2,1)S(1)}, bf16[256,384]{1,0:T(8,128)(2,1)}, u32[]{:S(2)}) copy-start(bf16[256,384]{1,0:T(8,128)(2,1)} %get-tuple-element.68.refs_6_.refs_8_) | copy-start | bytes 589828
  26.5 3.4 %copy-start.2 = (bf16[128,128]{1,0:T(8,128)(2,1)S(1)}, bf16[128,128]{1,0:T(8,128)(2,1)}, u32[]{:S(2)}) copy-start(bf16[128,128]{1,0:T(8,128)(2,1)} %get-tuple-element.67.refs_5_) | copy-start | bytes 98308
  26.5 11.3 %collective-permute-start.12 = (bf16[64,1280]{1,0:T(8,128)(2,1)S(1)}, bf16[64,1280]{1,0:T(8,128)(2,1)S(1)}, u32[]{:S(2)}, u32[]{:S(2)}) collective-permute-start(bf16[64,1280]{1,0:T(8,128)(2,1)S(1)} %pad_maximum_fusion), channel_id=1, source_target_pairs={{0,8},{4,12},{8,0},{12,4},{1,9},{5,13},{9,1},{13,5},{2,10},{6,14},... | collective-permute-start | bytes 491528 | tf_op jit(solution)/shard_map/ppermute | solution.py:33
  28.6 11.0 %collective-permute-start.11 = (bf16[128,1664]{1,0:T(8,128)(2,1)S(1)}, bf16[128,1664]{1,0:T(8,128)(2,1)S(1)}, u32[]{:S(2)}, u32[]{:S(2)}) collective-permute-start(bf16[128,1664]{1,0:T(8,128)(2,1)S(1)} %collective-permute-done.10.refs_2_), channel_id=1, source_target_pairs={{0,4},{4,0},{8,12},{12,8},{1,5},{5,1},{9,13},{13,9},{2,6},{6,2},{1... | collective-permute-start | bytes 1277960 | tf_op jit(solution)/shard_map/ppermute | solution.py:33
  28.6 9.3 %collective-permute-start.13 = (bf16[64,1280]{1,0:T(8,128)(2,1)S(1)}, bf16[64,1280]{1,0:T(8,128)(2,1)S(1)}, u32[]{:S(2)}, u32[]{:S(2)}) collective-permute-start(bf16[64,1280]{1,0:T(8,128)(2,1)S(1)} %pad_maximum_fusion.1), channel_id=1, source_target_pairs={{0,8},{4,12},{8,0},{12,4},{1,9},{5,13},{9,1},{13,5},{2,10},{6,14},... | collective-permute-start | bytes 491528 | tf_op jit(solution)/shard_map/ppermute | solution.py:33
  37.9 1.5 %collective-permute-start.14 = (bf16[64,1280]{1,0:T(8,128)(2,1)S(1)}, bf16[64,1280]{1,0:T(8,128)(2,1)S(1)}, u32[]{:S(2)}, u32[]{:S(2)}) collective-permute-start(bf16[64,1280]{1,0:T(8,128)(2,1)S(1)} %collective-permute-done.12.refs_4_), channel_id=1, source_target_pairs={{0,4},{4,0},{8,12},{12,8},{1,5},{5,1},{9,13},{13,9},{2,6},{6,2},{1... | collective-permute-start | bytes 491528 | tf_op jit(solution)/shard_map/ppermute | solution.py:33
  37.9 1.6 %collective-permute-start.15 = (bf16[64,1280]{1,0:T(8,128)(2,1)S(1)}, bf16[64,1280]{1,0:T(8,128)(2,1)S(1)}, u32[]{:S(2)}, u32[]{:S(2)}) collective-permute-start(bf16[64,1280]{1,0:T(8,128)(2,1)S(1)} %collective-permute-done.13.refs_5_), channel_id=1, source_target_pairs={{0,4},{4,0},{8,12},{12,8},{1,5},{5,1},{9,13},{13,9},{2,6},{6,2},{1... | collective-permute-start | bytes 491528 | tf_op jit(solution)/shard_map/ppermute | solution.py:33
  46.7 29.6 %collective-permute-start.16 = (bf16[256,384]{1,0:T(8,128)(2,1)S(1)}, bf16[256,384]{1,0:T(8,128)(2,1)S(1)}, u32[]{:S(2)}, u32[]{:S(2)}) collective-permute-start(bf16[256,384]{1,0:T(8,128)(2,1)S(1)} %get-tuple-element.85), channel_id=1, source_target_pairs={{0,1},{1,0},{2,3},{3,2},{4,5},{5,4},{6,7},{7,6},{8,9},{9,8},{10,11... | collective-permute-start | bytes 589832 | tf_op jit(solution)/shard_map/ppermute | solution.py:33
  49.6 26.7 %collective-permute-start.17 = (bf16[256,384]{1,0:T(8,128)(2,1)S(1)}, bf16[256,384]{1,0:T(8,128)(2,1)S(1)}, u32[]{:S(2)}, u32[]{:S(2)}) collective-permute-start(bf16[256,384]{1,0:T(8,128)(2,1)S(1)} %get-tuple-element.86), channel_id=1, source_target_pairs={{0,2},{1,3},{2,0},{3,1},{4,6},{5,7},{6,4},{7,5},{8,10},{9,11},{10,... | collective-permute-start | bytes 589832 | tf_op jit(solution)/shard_map/ppermute | solution.py:33
  51.1 25.2 %collective-permute-start.18 = (bf16[256,384]{1,0:T(8,128)(2,1)S(1)}, bf16[256,384]{1,0:T(8,128)(2,1)S(1)}, u32[]{:S(2)}, u32[]{:S(2)}) collective-permute-start(bf16[256,384]{1,0:T(8,128)(2,1)S(1)} %get-tuple-element.87), channel_id=1, source_target_pairs={{0,3},{1,2},{2,1},{3,0},{4,7},{5,6},{6,5},{7,4},{8,11},{9,10},{10,... | collective-permute-start | bytes 589832 | tf_op jit(solution)/shard_map/ppermute | solution.py:33
  52.0 2.0 %collective-permute-start.2 = (bf16[2,128,1152]{2,1,0:T(8,128)(2,1)S(1)}, bf16[2,128,1152]{2,1,0:T(8,128)(2,1)S(1)}, u32[]{:S(2)}, u32[]{:S(2)}) collective-permute-start(bf16[2,128,1152]{2,1,0:T(8,128)(2,1)S(1)} %get-tuple-element.29), channel_id=1, source_target_pairs={{0,4},{4,0},{8,12},{12,8},{1,5},{5,1},{9,13},{13,9},{2,6},{6,2},{1... | collective-permute-start | bytes 1769480 | tf_op jit(solution)/shard_map/cond/branch_1_fun/ppermute | solution.py:33
  52.0 13.1 %collective-permute-start = (bf16[2,128,1152]{2,1,0:T(8,128)(2,1)S(1)}, bf16[2,128,1152]{2,1,0:T(8,128)(2,1)S(1)}, u32[]{:S(2)}, u32[]{:S(2)}) collective-permute-start(bf16[2,128,1152]{2,1,0:T(8,128)(2,1)S(1)} %get-tuple-element.25), channel_id=1, source_target_pairs={{0,4},{4,0},{8,12},{12,8},{1,5},{5,1},{9,13},{13,9},{2,6},{6,2},{1... | collective-permute-start | bytes 1769480 | tf_op jit(solution)/shard_map/cond/branch_1_fun/ppermute | solution.py:33
  54.1 9.8 %collective-permute-start.3 = (bf16[128,1280]{1,0:T(8,128)(2,1)S(1)}, bf16[128,1280]{1,0:T(8,128)(2,1)S(1)}, u32[]{:S(2)}, u32[]{:S(2)}) collective-permute-start(bf16[128,1280]{1,0:T(8,128)(2,1)S(1)} %get-tuple-element.31), channel_id=1, source_target_pairs={{0,8},{4,12},{8,0},{12,4},{1,9},{5,13},{9,1},{13,5},{2,10},{6,14},... | collective-permute-start | bytes 983048 | tf_op jit(solution)/shard_map/cond/branch_1_fun/ppermute | solution.py:33
  64.0 10.7 %collective-permute-start.4 = (bf16[128,1536]{1,0:T(8,128)(2,1)S(1)}, bf16[128,1536]{1,0:T(8,128)(2,1)S(1)}, u32[]{:S(2)}, u32[]{:S(2)}) collective-permute-start(bf16[128,1536]{1,0:T(8,128)(2,1)S(1)} %join.1), channel_id=1, source_target_pairs={{0,1},{1,0},{2,3},{3,2},{4,5},{5,4},{6,7},{7,6},{8,9},{9,8},{10,11... | collective-permute-start | bytes 1179656 | tf_op jit(solution)/shard_map/cond/branch_1_fun/ppermute | solution.py:33
  65.3 8.7 %collective-permute-start.1 = (bf16[128,1280]{1,0:T(8,128)(2,1)S(1)}, bf16[128,1280]{1,0:T(8,128)(2,1)S(1)}, u32[]{:S(2)}, u32[]{:S(2)}) collective-permute-start(bf16[128,1280]{1,0:T(8,128)(2,1)S(1)} %get-tuple-element.27), channel_id=1, source_target_pairs={{0,8},{4,12},{8,0},{12,4},{1,9},{5,13},{9,1},{13,5},{2,10},{6,14},... | collective-permute-start | bytes 983048 | tf_op jit(solution)/shard_map/cond/branch_1_fun/ppermute | solution.py:33

commit v6 on v5

--- a/solution.py
+++ b/solution.py
@@ -18,7 +18,6 @@
 BF16 = jnp.bfloat16
 
 
-PACK_VMEM = 56 * 1024 * 1024
 SMALL = pltpu.CompilerParams(vmem_limit_bytes=8 * 1024 * 1024)
 
 
@@ -75,6 +74,9 @@
     ]
     for copy in copies:
         copy.start()
+    pair_s[...] = jnp.zeros_like(pair_s)
+    if SPAN < chunks:
+        dkv_s[...] = jnp.zeros_like(dkv_s)
     for copy in copies:
         copy.wait()
     if far_ids is None:
@@ -83,9 +85,6 @@
         chosen = [noted[:1, 64 * k : 64 * k + 1].astype(F32).astype(jnp.int32) for k in range(2)]
         chosen = [jnp.broadcast_to(value, (1, rows)) for value in chosen]
 
-    pair_s[...] = jnp.zeros_like(pair_s)
-    if SPAN < chunks:
-        dkv_s[...] = jnp.zeros_like(dkv_s)
     tile = min(512, length)
 
     @pl.loop(0, length // tile)
@@ -220,34 +219,38 @@
     return [total, mine[:, model:], theirs[:, model:]]
 
 
-def combine_kernel(*refs, model):
-    count = len(refs) - 2
-    keep_ref, got_ref = refs[:2]
-    for t in range(count):
-        out_ref = refs[2 + t]
-        lo = 0
-        for value in add_and_join(keep_ref[t], got_ref[t], model):
-            out_ref[:, lo : lo + value.shape[1]] = value
-            lo += value.shape[1]
+def put(out_ref, first, values):
+    size = values[0].shape[0]
+    lo = 0
+    for value in values:
+        out_ref[first : first + size, lo : lo + value.shape[1]] = value
+        lo += value.shape[1]
+
+
+def combine_kernel(keep_ref, got_ref, *outs, model):
+    for t in range(keep_ref.shape[0]):
+        put(outs[t], 0, add_and_join(keep_ref[t], got_ref[t], model))
 
 
 def join_kernel(mine_ref, theirs_ref, out_ref, *, model):
-    lo = 0
-    for value in add_and_join(mine_ref[...], theirs_ref[...], model):
-        out_ref[:, lo : lo + value.shape[1]] = value
-        lo += value.shape[1]
-
-
-def final_kernel(where_ref, *refs, model, seqs, chunks):
-    far_ref, grad_ref, context_ref = refs[-3:]
-    if len(refs) == 5:
-        total, mine, near = add_and_join(refs[0][...], refs[1][...], model)
+    put(out_ref, 0, add_and_join(mine_ref[...], theirs_ref[...], model))
+
+
+def final_kernel(where_ref, *refs, model, seqs, chunks, parts):
+    outs = refs[-5:]
+    grad_ref, context_ref = outs[:2]
+    ins = refs[: -5 - parts]
+    moved = refs[-5 - parts : -5]
+    if len(ins) == 2:
+        total = ins[0][:, :model]
+        mine = ins[0][:, model:]
+        far = ins[1][...]
+    else:
+        total, mine, near = add_and_join(ins[0][...], ins[1][...], model)
         mine = jnp.concatenate([mine, near], axis=1)
-    else:
-        total = refs[0][:, :model]
-        mine = refs[0][:, model:]
-    grad_ref[...] = (total.astype(F32) + far_ref[:, :model].astype(F32)).astype(BF16)
-    theirs = far_ref[:, model:]
+        far = ins[2][...]
+    grad_ref[...] = (total.astype(F32) + far[:, :model].astype(F32)).astype(BF16)
+    theirs = far[:, model:]
     groups = seqs * chunks
     width = model // groups
     values = [mine[:, k * width : (k + 1) * width] for k in range(groups // 2)]
@@ -261,33 +264,31 @@
     for o in range(groups):
         lo = ((o % chunks) * seqs + o // chunks) * width
         context_ref[:, lo : lo + width] = values[o]
-
-
-def sum_kernel(where_ref, *refs, parts, seqs, width):
-    outs = refs[parts:]
     for m in range(3):
         sums = []
         for i in range(seqs):
-            acc = refs[i][:, m * width : (m + 1) * width].astype(F32)
+            acc = moved[i][:, m * width : (m + 1) * width].astype(F32)
             for j in range(i + seqs, parts, seqs):
-                acc = acc + refs[j][:, m * width : (m + 1) * width].astype(F32)
+                acc = acc + moved[j][:, m * width : (m + 1) * width].astype(F32)
             sums.append(acc)
         if seqs == 1:
-            outs[m][...] = sums[0]
+            outs[2 + m][...] = sums[0]
         else:
             flip = where_ref[2] != 0
-            outs[m][:, :width] = jnp.where(flip, sums[1], sums[0])
-            outs[m][:, width:] = jnp.where(flip, sums[0], sums[1])
-
-
-def pack_kernel(where_ref, chosen_ref, *refs, lefts, seqs, chunks, width, noted):
+            outs[2 + m][:, :width] = jnp.where(flip, sums[1], sums[0])
+            outs[2 + m][:, width:] = jnp.where(flip, sums[0], sums[1])
+
+
+def pack_kernel(where_ref, blocks_ref, *refs, lefts, seqs, chunks, width, noted):
     tokens, up = refs[:2]
     weight_refs = refs[2:5]
     hops = len(lefts)
     sends = refs[5 : 5 + hops]
     own_up = refs[5 + hops]
     weight_sends = refs[6 + hops : 6 + hops + seqs]
-    sems = refs[6 + hops + seqs]
+    note, blocks, sems = refs[6 + hops + seqs :]
+    fetch = pltpu.make_async_copy(blocks_ref, blocks, sems.at[sems.shape[0] - 1])
+    fetch.start()
     model = tokens.shape[1]
 
     def columns(offset):
@@ -315,12 +316,12 @@
     ]
     for copy in copies:
         copy.start()
+    fetch.wait()
     if noted:
+        lane = lax.broadcasted_iota(jnp.int32, note.shape, 1)
+        note[...] = jnp.where(lane < 64, blocks[0, 0], blocks[0, 1]).astype(F32).astype(BF16)
         lo = model + lefts[0] * width
-        shape = (tokens.shape[0], 128)
-        lane = lax.broadcasted_iota(jnp.int32, shape, 1)
-        both = jnp.where(lane < 64, chosen_ref[0], chosen_ref[1])
-        sends[0][:, lo : lo + 128] = both.astype(F32).astype(BF16)
+        sends[0][:, lo : lo + 128] = note[...]
     for copy in copies:
         copy.wait()
 
@@ -333,7 +334,7 @@
     chunks = lax.axis_size("ctx")
     parts = lax.axis_size("dp")
     seqs = 1
-    if chunks == 4 and parts % 2 == 0 and model % 1024 == 0 and HEADS % 8 == 0:
+    if chunks == 4 and parts % 2 == 0 and model % 1024 == 0 and HEADS % 8 == 0 and rows % 32 == 0:
         seqs = 2
     groups = chunks * seqs
     width = model // groups
@@ -364,15 +365,23 @@
             ),
             out_shape=tuple(jax.ShapeDtypeStruct((rows, size), BF16) for size in sizes + [width])
             + (jax.ShapeDtypeStruct((model // parts, 3 * width), BF16),) * seqs,
-            in_specs=[smem, smem] + [hbm] * 5,
+            in_specs=[smem] + [hbm] * 6,
             out_specs=(vmem,) * (len(hops) + 1 + seqs),
             scratch_shapes=[
-                pltpu.SemaphoreType.DMA((len(hops) + sum(lefts) + 1 + 3 * seqs,)),
+                pltpu.VMEM((rows, 128), BF16),
+                pltpu.SMEM((1, 2), jnp.int32),
+                pltpu.SemaphoreType.DMA((len(hops) + sum(lefts) + 2 + 3 * seqs,)),
             ],
-            compiler_params=pltpu.CompilerParams(vmem_limit_bytes=PACK_VMEM),
+            compiler_params=SMALL,
             cost_estimate=cost(2),
             name="pack",
-        )(where, chosen, own_tokens, upstream, w_query, w_key, w_value)
+        )(
+            where,
+            *[
+                pltpu.with_memory_space_constraint(value, pltpu.HBM)
+                for value in (global_blocks, own_tokens, upstream, w_query, w_key, w_value)
+            ],
+        )
         own_sends = outs[: len(hops)]
         own_up = outs[len(hops)]
         sends = outs[len(hops) + 1 :]
@@ -453,12 +462,12 @@
         return results[:parts], results[parts], results[parts + 1]
 
     def combine(keep, got):
-        count = keep.shape[0]
+        kinds = (jax.ShapeDtypeStruct((rows, model + 2 * width), BF16),) * keep.shape[0]
         return pl.pallas_call(
             lambda *refs: combine_kernel(*refs, model=model),
-            out_shape=(jax.ShapeDtypeStruct((rows, model + 2 * width), BF16),) * count,
+            out_shape=kinds,
             in_specs=[vmem] * 2,
-            out_specs=(vmem,) * count,
+            out_specs=(vmem,) * len(kinds),
             compiler_params=SMALL,
             cost_estimate=cost(1),
             name="combine",
@@ -467,23 +476,13 @@
     def join(mine, theirs):
         return pl.pallas_call(
             lambda *refs: join_kernel(*refs, model=model),
-            out_shape=jax.ShapeDtypeStruct((rows, 2 * mine.shape[1] - model), BF16),
+            out_shape=jax.ShapeDtypeStruct((mine.shape[0], 2 * mine.shape[1] - model), BF16),
             in_specs=[vmem] * 2,
             out_specs=vmem,
             compiler_params=SMALL,
             cost_estimate=cost(1),
             name="join",
         )(mine, theirs)
-
-    def finish(*values):
-        return pl.pallas_call(
-            lambda *refs: final_kernel(*refs, model=model, seqs=seqs, chunks=chunks),
-            out_shape=(jax.ShapeDtypeStruct((rows, model), BF16),) * 2,
-            in_specs=[smem] + [vmem] * len(values),
-            compiler_params=SMALL,
-            cost_estimate=cost(2),
-            name="rows_out",
-        )(where, *values)
 
     if seqs == 2:
         line_hop, far_hop, near_hop = [hop[:2] for hop in hops]
@@ -540,15 +539,18 @@
 
         grad_w, *rest = both(tz, tx, shared, own_tokens, own_up, *weights)
 
-        def collect(keep, send, keep_other, send_other):
-            held, far = combine(keep_other, xor_permute(send_other, *near_hop))
-            mine, near = combine(keep, xor_permute(send, *near_hop))
-            held = join(held, xor_permute(far, *far_hop))
-            far = xor_permute(held, *line_hop)
-            return finish(mine, xor_permute(near, *far_hop), far)
-
+        keep, send, keep_other, send_other = rest
+        got_other = xor_permute(send_other, *near_hop)
+        got = xor_permute(send, *near_hop)
         moved = [grad_w[0]] + [xor_permute(grad_w[j], "dp", j) for j in range(1, parts)]
-        grad_tokens, context = guarded(collect, *rest)
+
+        def collect(keep, got, keep_other, got_other):
+            held, far = combine(keep_other, got_other)
+            far = xor_permute(join(held, xor_permute(far, *far_hop)), *line_hop)
+            mine, near = combine(keep, got)
+            return mine, xor_permute(near, *far_hop), far
+
+        ins = guarded(collect, keep, got, keep_other, got_other)
     else:
 
         def spread(first, *own):
@@ -577,19 +579,20 @@
             for axis, bit, _ in reversed(hops[1:-1]):
                 theirs = [xor_permute(value, axis, bit) for value in held[1::2]]
                 held = [join(*pair) for pair in zip(held[::2], theirs)]
-            return finish(held[0], xor_permute(held[1], *hops[0][:2]))
+            return held[0], xor_permute(held[1], *hops[0][:2])
 
         moved = [grad_w[0]] + [xor_permute(grad_w[j], "dp", j) for j in range(1, parts)]
-        grad_tokens, context = guarded(collect, keep, send)
-
-    final = pl.pallas_call(
-        lambda *refs: sum_kernel(*refs, parts=parts, seqs=seqs, width=width),
-        out_shape=(jax.ShapeDtypeStruct((model // parts, seqs * width), F32),) * 3,
-        in_specs=[smem] + [vmem] * parts,
+        ins = guarded(collect, keep, send)
+
+    grad_tokens, context, *final = pl.pallas_call(
+        lambda *refs: final_kernel(*refs, model=model, seqs=seqs, chunks=chunks, parts=parts),
+        out_shape=(jax.ShapeDtypeStruct((rows, model), BF16),) * 2
+        + (jax.ShapeDtypeStruct((model // parts, seqs * width), F32),) * 3,
+        in_specs=[smem] + [vmem] * (len(ins) + len(moved)),
         compiler_params=SMALL,
         cost_estimate=cost(2),
-        name="weights_out",
-    )(where, *moved)
+        name="finish",
+    )(where, *ins, *moved)
     return (context[None], grad_tokens[None], *final)
 
 

time: 77.9 us -> 75.6 us (0.970)
  Pallas kernels: 21.6 us -> 19.8 us
    pallas_call x1, Pallas kernels: 3.31 us -> 2.06 us  [per_device(): pl.pallas_call(lambda *refs: pack_kernel(*refs, lefts=lefts, seqs=seqs, c...]
    pallas_call x2 -> x1, Pallas kernels: 2.92 us -> 2.27 us  [per_device(): pl.pallas_call(lambda *refs: final_kernel(*refs, model=model, seqs=seqs,...]
  transfers between devices with their start and end apart: 19 -> 19, of which waited for: 10 -> 9; matrix products, arithmetic and copies ran while one was open for 0% -> 0% of each run, Pallas kernels for 13% -> 21%
where the time goes in v6:
time: 75.6 us; the launch traced here: 75.4 us
  waiting for transfers between devices  33.2 us (44%)
  starting transfers between devices  21.3 us (28%)
  Pallas kernels  19.8 us (26%)
  between operations  0.78 us (1%)
    ppermute x19, waiting for transfers between devices, xor_permute(): return lax.ppermute(value, axis, [(i, i ^ bit) for i in range(count)])  33.2 us
    ppermute x19, starting transfers between devices, xor_permute(): return lax.ppermute(value, axis, [(i, i ^ bit) for i in range(count)])  21.3 us
    pallas_call x2, Pallas kernels, attend(): pl.pallas_call(lambda *refs: attention_kernel(*refs, sources=sources, chu...  15.2 us
    pallas_call x1, Pallas kernels, per_device(): pl.pallas_call(lambda *refs: final_kernel(*refs, model=model, seqs=seqs,...  2.27 us
    pallas_call x1, Pallas kernels, per_device(): pl.pallas_call(lambda *refs: pack_kernel(*refs, lefts=lefts, seqs=seqs, c...  2.06 us
  transfers between devices with their start and end apart: 19, of which 9 were waited for; matrix products, arithmetic and copies ran while one was open for 0% of the time, Pallas kernels for 21%

profile of v6, /device:TPU:0, one launch (start us, length us, event | category | flops | bytes accessed | tf_op | source)
XLA Modules:
  0.0 75.4 jit_solution(15667215492298978484)
XLA Ops:
  0.7 2.1 %pack.1 = (bf16[128,1664]{1,0:T(8,128)(2,1)S(1)}, bf16[128,1280]{1,0:T(8,128)(2,1)S(1)}, bf16[128,1152]{1,0:T(8,128)(2,1)S(1)}, bf16[128,128]{1,0:T(8,128)(2,1)S...) custom-call(s32[3]{0:T(128)S(1)} %pad_add_fusion.refs_0_, s32[1,2]{1,0:T(1,128)} %refs_1_.1, ...), custom_call_target="tpu_custom_call" | custom-call | bytes 6000000 | tf_op jit(solution)/shard_map/pack/pallas_call | solution.py:362
  2.8 3.1 %collective-permute-start.9 = (bf16[128,1664]{1,0:T(8,128)(2,1)S(1)}, bf16[128,1664]{1,0:T(8,128)(2,1)S(1)}, u32[]{:S(2)}, u32[]{:S(2)}) collective-permute-start(bf16[128,1664]{1,0:T(8,128)(2,1)S(1)} %get-tuple-element.66), channel_id=1, source_target_pairs={{0,1},{1,0},{2,3},{3,2},{4,5},{5,4},{6,7},{7,6},{8,9},{9,8},{10,11... | collective-permute-start | bytes 1277960 | tf_op jit(solution)/shard_map/ppermute | solution.py:32
  5.9 1.5 %collective-permute-start.4 = (bf16[128,1280]{1,0:T(8,128)(2,1)S(1)}, bf16[128,1280]{1,0:T(8,128)(2,1)S(1)}, u32[]{:S(2)}, u32[]{:S(2)}) collective-permute-start(bf16[128,1280]{1,0:T(8,128)(2,1)S(1)} %get-tuple-element.59), channel_id=1, source_target_pairs={{0,8},{4,12},{8,0},{12,4},{1,9},{5,13},{9,1},{13,5},{2,10},{6,14},... | collective-permute-start | bytes 983048 | tf_op jit(solution)/shard_map/ppermute | solution.py:32
  7.4 2.5 %collective-permute-start.7 = (bf16[256,384]{1,0:T(8,128)(2,1)S(1)}, bf16[256,384]{1,0:T(8,128)(2,1)S(1)}, u32[]{:S(2)}, u32[]{:S(2)}) collective-permute-start(bf16[256,384]{1,0:T(8,128)(2,1)S(1)} %get-tuple-element.63), channel_id=1, source_target_pairs={{0,3},{1,2},{2,1},{3,0},{4,7},{5,6},{6,5},{7,4},{8,11},{9,10},{10,... | collective-permute-start | bytes 589832 | tf_op jit(solution)/shard_map/ppermute | solution.py:32
  10.5 1.2 %collective-permute-start.6 = (bf16[256,384]{1,0:T(8,128)(2,1)S(1)}, bf16[256,384]{1,0:T(8,128)(2,1)S(1)}, u32[]{:S(2)}, u32[]{:S(2)}) collective-permute-start(bf16[256,384]{1,0:T(8,128)(2,1)S(1)} %get-tuple-element.62.refs_6_.refs_8_), channel_id=1, source_target_pairs={{0,2},{1,3},{2,0},{3,1},{4,6},{5,7},{6,4},{7,5},{8,10},{9,11},{10,... | collective-permute-start | bytes 589832 | tf_op jit(solution)/shard_map/ppermute | solution.py:32
  11.8 3.3 %collective-permute-done.4.refs_4_ = bf16[128,1280]{1,0:T(8,128)(2,1)S(1)} collective-permute-done((bf16[128,1280]{1,0:T(8,128)(2,1)S(1)}, bf16[128,1280]{1,0:T(8,128)(2,1)S(1)}, u32[]{:S(2)}, u32[]{:S(2)}) %collective-permute-start.4) | collective-permute-done | bytes 327712 | tf_op jit(solution)/shard_map/ppermute | solution.py:32
  15.1 2.3 %conditional.2 = (bf16[256,1152]{1,0:T(8,128)(2,1)}) conditional(s32[]{:T(128)} %bitcast.3, () %tuple.24, (bf16[128,1280]{1,0:T(8,128)(2,1)S(1)}, bf16[128,1152]{1,0:T(8,128)(2,1)S(1)}) %tuple.25), branch_computations={%region_0.1_spmd, %region_1.2_spmd} | conditional | flops 1769472 | bytes 4128816 | solution.py:415
  15.3 2.1 %collective-permute-done.3 = bf16[256,1152]{1,0:T(8,128)(2,1)} collective-permute-done((bf16[256,1152]{1,0:T(8,128)(2,1)S(1)}, bf16[256,1152]{1,0:T(8,128)(2,1)}, u32[]{:S(2)}, u32[]{:S(2)}) %collective-permute-start.3) | collective-permute-done | bytes 589856 | tf_op jit(solution)/shard_map/cond/branch_1_fun/ppermute | solution.py:32
  17.4 7.6 %collective-permute-done.9.refs_2_ = bf16[128,1664]{1,0:T(8,128)(2,1)S(1)} collective-permute-done((bf16[128,1664]{1,0:T(8,128)(2,1)S(1)}, bf16[128,1664]{1,0:T(8,128)(2,1)S(1)}, u32[]{:S(2)}, u32[]{:S(2)}) %collective-permute-start.9) | collective-permute-done | bytes 426016 | tf_op jit(solution)/shard_map/ppermute | solution.py:32
  25.0 2.1 %collective-permute-start.11 = (bf16[64,1280]{1,0:T(8,128)(2,1)S(1)}, bf16[64,1280]{1,0:T(8,128)(2,1)S(1)}, u32[]{:S(2)}, u32[]{:S(2)}) collective-permute-start(bf16[64,1280]{1,0:T(8,128)(2,1)S(1)} %pad_maximum_fusion), channel_id=1, source_target_pairs={{0,8},{4,12},{8,0},{12,4},{1,9},{5,13},{9,1},{13,5},{2,10},{6,14},... | collective-permute-start | bytes 491528 | tf_op jit(solution)/shard_map/ppermute | solution.py:32
  27.3 1.1 %collective-permute-done.5.refs_7_.refs_9_ = bf16[256,384]{1,0:T(8,128)(2,1)S(1)} collective-permute-done((bf16[256,384]{1,0:T(8,128)(2,1)S(1)}, bf16[256,384]{1,0:T(8,128)(2,1)S(1)}, u32[]{:S(2)}, u32[]{:S(2)}) %collective-permute-start.5) | collective-permute-done | bytes 196640 | tf_op jit(solution)/shard_map/ppermute | solution.py:32
  28.4 8.0 %attention.2 = (f32[256,384]{1,0:T(8,128)S(1)}, f32[256,384]{1,0:T(8,128)S(1)}, f32[256,384]{1,0:T(8,128)S(1)}, f32[256,384]{1,0:T(8,128)S(1)}, bf16[2,128,1152]...) custom-call(s32[3]{0:T(128)S(1)} %pad_add_fusion.refs_0_, s32[2]{0:T(128)S(1)} %bitcast.13, ...), custom_call_target="tpu_custom_call" | custom-call | bytes 21000000 | tf_op jit(solution)/shard_map/attention/pallas_call | solution.py:426
  38.1 7.2 %attention.3 = (bf16[256,384]{1,0:T(8,128)(2,1)S(1)}, bf16[256,384]{1,0:T(8,128)(2,1)S(1)}, bf16[256,384]{1,0:T(8,128)(2,1)S(1)}, bf16[256,384]{1,0:T(8,128)(2,1...) custom-call(s32[3]{0:T(128)S(1)} %pad_add_fusion.refs_0_, s32[2]{0:T(128)S(1)} %bitcast.14, ...), custom_call_target="tpu_custom_call" | custom-call | bytes 21000000 | tf_op jit(solution)/shard_map/attention/pallas_call | solution.py:426
  45.6 2.8 %collective-permute-start.16 = (bf16[256,384]{1,0:T(8,128)(2,1)S(1)}, bf16[256,384]{1,0:T(8,128)(2,1)S(1)}, u32[]{:S(2)}, u32[]{:S(2)}) collective-permute-start(bf16[256,384]{1,0:T(8,128)(2,1)S(1)} %get-tuple-element.80), channel_id=1, source_target_pairs={{0,1},{1,0},{2,3},{3,2},{4,5},{5,4},{6,7},{7,6},{8,9},{9,8},{10,11... | collective-permute-start | bytes 589832 | tf_op jit(solution)/shard_map/ppermute | solution.py:32
  48.4 1.5 %collective-permute-start.17 = (bf16[256,384]{1,0:T(8,128)(2,1)S(1)}, bf16[256,384]{1,0:T(8,128)(2,1)S(1)}, u32[]{:S(2)}, u32[]{:S(2)}) collective-permute-start(bf16[256,384]{1,0:T(8,128)(2,1)S(1)} %get-tuple-element.81), channel_id=1, source_target_pairs={{0,2},{1,3},{2,0},{3,1},{4,6},{5,7},{6,4},{7,5},{8,10},{9,11},{10,... | collective-permute-start | bytes 589832 | tf_op jit(solution)/shard_map/ppermute | solution.py:32
  50.0 0.8 %collective-permute-start.18 = (bf16[256,384]{1,0:T(8,128)(2,1)S(1)}, bf16[256,384]{1,0:T(8,128)(2,1)S(1)}, u32[]{:S(2)}, u32[]{:S(2)}) collective-permute-start(bf16[256,384]{1,0:T(8,128)(2,1)S(1)} %get-tuple-element.82), channel_id=1, source_target_pairs={{0,3},{1,2},{2,1},{3,0},{4,7},{5,6},{6,5},{7,4},{8,11},{9,10},{10,... | collective-permute-start | bytes 589832 | tf_op jit(solution)/shard_map/ppermute | solution.py:32
  50.8 22.3 %conditional.3 = (bf16[128,1280]{1,0:T(8,128)(2,1)S(1)}, bf16[128,1280]{1,0:T(8,128)(2,1)}, bf16[128,1536]{1,0:T(8,128)(2,1)}) conditional(s32[]{:T(128)} %bitcast.3, () %tuple.23, (bf16[2,128,1152]{2,1,0:T(8,128)(2,1)S(1)}, bf16[2,128,1152]{2,1,0:T(8,128)(2,1)S(1)}, bf16[2,128,1152]{2,1,0:T(8,128)(2,1)S(1)}, ...), branch_computations={%region_2.3_spmd, %region_3.4_spmd} | conditional | bytes 13194448 | solution.py:415
  50.9 1.5 %collective-permute-start.1 = (bf16[128,1280]{1,0:T(8,128)(2,1)S(1)}, bf16[128,1280]{1,0:T(8,128)(2,1)S(1)}, u32[]{:S(2)}, u32[]{:S(2)}) collective-permute-start(bf16[128,1280]{1,0:T(8,128)(2,1)S(1)} %get-tuple-element.24), channel_id=1, source_target_pairs={{0,8},{4,12},{8,0},{12,4},{1,9},{5,13},{9,1},{13,5},{2,10},{6,14},... | collective-permute-start | bytes 983048 | tf_op jit(solution)/shard_map/cond/branch_1_fun/ppermute | solution.py:32
  52.4 7.9 %collective-permute-done.1.refs_1_ = bf16[128,1280]{1,0:T(8,128)(2,1)S(1)} collective-permute-done((bf16[128,1280]{1,0:T(8,128)(2,1)S(1)}, bf16[128,1280]{1,0:T(8,128)(2,1)S(1)}, u32[]{:S(2)}, u32[]{:S(2)}) %collective-permute-start.1) | collective-permute-done | bytes 327712 | tf_op jit(solution)/shard_map/cond/branch_1_fun/ppermute | solution.py:32
  60.4 0.9 %collective-permute-start.2 = (bf16[128,1536]{1,0:T(8,128)(2,1)S(1)}, bf16[128,1536]{1,0:T(8,128)(2,1)}, u32[]{:S(2)}, u32[]{:S(2)}) collective-permute-start(bf16[128,1536]{1,0:T(8,128)(2,1)S(1)} %join.1), channel_id=1, source_target_pairs={{0,1},{1,0},{2,3},{3,2},{4,5},{5,4},{6,7},{7,6},{8,9},{9,8},{10,11... | collective-permute-start | bytes 1179656 | tf_op jit(solution)/shard_map/cond/branch_1_fun/ppermute | solution.py:32
  61.4 1.5 %collective-permute-start = (bf16[128,1280]{1,0:T(8,128)(2,1)S(1)}, bf16[128,1280]{1,0:T(8,128)(2,1)}, u32[]{:S(2)}, u32[]{:S(2)}) collective-permute-start(bf16[128,1280]{1,0:T(8,128)(2,1)S(1)} %get-tuple-element.20), channel_id=1, source_target_pairs={{0,8},{4,12},{8,0},{12,4},{1,9},{5,13},{9,1},{13,5},{2,10},{6,14},... | collective-permute-start | bytes 983048 | tf_op jit(solution)/shard_map/cond/branch_1_fun/ppermute | solution.py:32
  62.9 6.5 %collective-permute-done = bf16[128,1280]{1,0:T(8,128)(2,1)} collective-permute-done((bf16[128,1280]{1,0:T(8,128)(2,1)S(1)}, bf16[128,1280]{1,0:T(8,128)(2,1)}, u32[]{:S(2)}, u32[]{:S(2)}) %collective-permute-start) | collective-permute-done | bytes 327712 | tf_op jit(solution)/shard_map/cond/branch_1_fun/ppermute | solution.py:32
  69.4 3.7 %collective-permute-done.2 = bf16[128,1536]{1,0:T(8,128)(2,1)} collective-permute-done((bf16[128,1536]{1,0:T(8,128)(2,1)S(1)}, bf16[128,1536]{1,0:T(8,128)(2,1)}, u32[]{:S(2)}, u32[]{:S(2)}) %collective-permute-start.2) | collective-permute-done | bytes 393248 | tf_op jit(solution)/shard_map/cond/branch_1_fun/ppermute | solution.py:32
  73.1 2.3 %finish.1 = (bf16[128,1024]{1,0:T(8,128)(2,1)}, bf16[128,1024]{1,0:T(8,128)(2,1)}, f32[256,256]{1,0:T(8,128)}, f32[256,256]{1,0:T(8,128)}, f32[256,256]{1,0:T(8,128)}) custom-call(s32[3]{0:T(128)S(1)} %pad_add_fusion.refs_0_, bf16[128,1280]{1,0:T(8,128)(2,1)S(1)} %get-tuple-element.76.refs_1_, bf16[128,1280]{1,0:T(8,128)(2,1)} %get-tuple-element.77.refs_2_, ...), custom_call_target="tpu_custom_call" | custom-call | bytes 6000000 | tf_op jit(solution)/shard_map/finish/pallas_call | solution.py:587
  (35 shorter events, 3.5 us)
Async XLA Ops:
  0.7 11.1 %copy-start.1 = (s32[1,2]{1,0:T(1,128)S(1)}, s32[1,2]{1,0:T(1,128)}, u32[]{:S(2)}) copy-start(s32[1,2]{1,0:T(1,128)} %refs_1_.1) | copy-start | bytes 28
  2.8 22.2 %collective-permute-start.9 = (bf16[128,1664]{1,0:T(8,128)(2,1)S(1)}, bf16[128,1664]{1,0:T(8,128)(2,1)S(1)}, u32[]{:S(2)}, u32[]{:S(2)}) collective-permute-start(bf16[128,1664]{1,0:T(8,128)(2,1)S(1)} %get-tuple-element.66), channel_id=1, source_target_pairs={{0,1},{1,0},{2,3},{3,2},{4,5},{5,4},{6,7},{7,6},{8,9},{9,8},{10,11... | collective-permute-start | bytes 1277960 | tf_op jit(solution)/shard_map/ppermute | solution.py:32
  5.9 9.2 %collective-permute-start.4 = (bf16[128,1280]{1,0:T(8,128)(2,1)S(1)}, bf16[128,1280]{1,0:T(8,128)(2,1)S(1)}, u32[]{:S(2)}, u32[]{:S(2)}) collective-permute-start(bf16[128,1280]{1,0:T(8,128)(2,1)S(1)} %get-tuple-element.59), channel_id=1, source_target_pairs={{0,8},{4,12},{8,0},{12,4},{1,9},{5,13},{9,1},{13,5},{2,10},{6,14},... | collective-permute-start | bytes 983048 | tf_op jit(solution)/shard_map/ppermute | solution.py:32
  7.4 19.7 %collective-permute-start.7 = (bf16[256,384]{1,0:T(8,128)(2,1)S(1)}, bf16[256,384]{1,0:T(8,128)(2,1)S(1)}, u32[]{:S(2)}, u32[]{:S(2)}) collective-permute-start(bf16[256,384]{1,0:T(8,128)(2,1)S(1)} %get-tuple-element.63), channel_id=1, source_target_pairs={{0,3},{1,2},{2,1},{3,0},{4,7},{5,6},{6,5},{7,4},{8,11},{9,10},{10,... | collective-permute-start | bytes 589832 | tf_op jit(solution)/shard_map/ppermute | solution.py:32
  9.9 18.5 %collective-permute-start.5 = (bf16[256,384]{1,0:T(8,128)(2,1)S(1)}, bf16[256,384]{1,0:T(8,128)(2,1)S(1)}, u32[]{:S(2)}, u32[]{:S(2)}) collective-permute-start(bf16[256,384]{1,0:T(8,128)(2,1)S(1)} %get-tuple-element.63), channel_id=1, source_target_pairs={{0,1},{1,0},{2,3},{3,2},{4,5},{5,4},{6,7},{7,6},{8,9},{9,8},{10,11... | collective-permute-start | bytes 589832 | tf_op jit(solution)/shard_map/ppermute | solution.py:32
  10.5 17.8 %collective-permute-start.6 = (bf16[256,384]{1,0:T(8,128)(2,1)S(1)}, bf16[256,384]{1,0:T(8,128)(2,1)S(1)}, u32[]{:S(2)}, u32[]{:S(2)}) collective-permute-start(bf16[256,384]{1,0:T(8,128)(2,1)S(1)} %get-tuple-element.62.refs_6_.refs_8_), channel_id=1, source_target_pairs={{0,2},{1,3},{2,0},{3,1},{4,6},{5,7},{6,4},{7,5},{8,10},{9,11},{10,... | collective-permute-start | bytes 589832 | tf_op jit(solution)/shard_map/ppermute | solution.py:32
  15.2 2.2 %collective-permute-start.3 = (bf16[256,1152]{1,0:T(8,128)(2,1)S(1)}, bf16[256,1152]{1,0:T(8,128)(2,1)}, u32[]{:S(2)}, u32[]{:S(2)}) collective-permute-start(bf16[256,1152]{1,0:T(8,128)(2,1)S(1)} %maximum_maximum_fusion), channel_id=1, source_target_pairs={{0,4},{4,0},{8,12},{12,8},{1,5},{5,1},{9,13},{13,9},{2,6},{6,2},{1... | collective-permute-start | bytes 1769480 | tf_op jit(solution)/shard_map/cond/branch_1_fun/ppermute | solution.py:32
  25.0 3.4 %copy-start = (bf16[1,128,1024]{2,1,0:T(8,128)(2,1)S(1)}, bf16[1,128,1024]{2,1,0:T(8,128)(2,1)}, u32[]{:S(2)}) copy-start(bf16[1,128,1024]{2,1,0:T(8,128)(2,1)} %param.10) | copy-start | bytes 786436
  25.0 11.3 %collective-permute-start.11 = (bf16[64,1280]{1,0:T(8,128)(2,1)S(1)}, bf16[64,1280]{1,0:T(8,128)(2,1)S(1)}, u32[]{:S(2)}, u32[]{:S(2)}) collective-permute-start(bf16[64,1280]{1,0:T(8,128)(2,1)S(1)} %pad_maximum_fusion), channel_id=1, source_target_pairs={{0,8},{4,12},{8,0},{12,4},{1,9},{5,13},{9,1},{13,5},{2,10},{6,14},... | collective-permute-start | bytes 491528 | tf_op jit(solution)/shard_map/ppermute | solution.py:32
  27.1 11.0 %collective-permute-start.10 = (bf16[128,1664]{1,0:T(8,128)(2,1)S(1)}, bf16[128,1664]{1,0:T(8,128)(2,1)S(1)}, u32[]{:S(2)}, u32[]{:S(2)}) collective-permute-start(bf16[128,1664]{1,0:T(8,128)(2,1)S(1)} %collective-permute-done.9.refs_2_), channel_id=1, source_target_pairs={{0,4},{4,0},{8,12},{12,8},{1,5},{5,1},{9,13},{13,9},{2,6},{6,2},{1... | collective-permute-start | bytes 1277960 | tf_op jit(solution)/shard_map/ppermute | solution.py:32
  27.1 9.3 %collective-permute-start.12 = (bf16[64,1280]{1,0:T(8,128)(2,1)S(1)}, bf16[64,1280]{1,0:T(8,128)(2,1)S(1)}, u32[]{:S(2)}, u32[]{:S(2)}) collective-permute-start(bf16[64,1280]{1,0:T(8,128)(2,1)S(1)} %pad_maximum_fusion.1), channel_id=1, source_target_pairs={{0,8},{4,12},{8,0},{12,4},{1,9},{5,13},{9,1},{13,5},{2,10},{6,14},... | collective-permute-start | bytes 491528 | tf_op jit(solution)/shard_map/ppermute | solution.py:32
  36.4 1.5 %collective-permute-start.13 = (bf16[64,1280]{1,0:T(8,128)(2,1)S(1)}, bf16[64,1280]{1,0:T(8,128)(2,1)S(1)}, u32[]{:S(2)}, u32[]{:S(2)}) collective-permute-start(bf16[64,1280]{1,0:T(8,128)(2,1)S(1)} %collective-permute-done.11.refs_4_), channel_id=1, source_target_pairs={{0,4},{4,0},{8,12},{12,8},{1,5},{5,1},{9,13},{13,9},{2,6},{6,2},{1... | collective-permute-start | bytes 491528 | tf_op jit(solution)/shard_map/ppermute | solution.py:32
  36.5 1.6 %collective-permute-start.14 = (bf16[64,1280]{1,0:T(8,128)(2,1)S(1)}, bf16[64,1280]{1,0:T(8,128)(2,1)S(1)}, u32[]{:S(2)}, u32[]{:S(2)}) collective-permute-start(bf16[64,1280]{1,0:T(8,128)(2,1)S(1)} %collective-permute-done.12.refs_5_), channel_id=1, source_target_pairs={{0,4},{4,0},{8,12},{12,8},{1,5},{5,1},{9,13},{13,9},{2,6},{6,2},{1... | collective-permute-start | bytes 491528 | tf_op jit(solution)/shard_map/ppermute | solution.py:32
  37.0 13.8 %collective-permute-start.8 = (bf16[2,128,1152]{2,1,0:T(8,128)(2,1)S(1)}, bf16[2,128,1152]{2,1,0:T(8,128)(2,1)S(1)}, u32[]{:S(2)}, u32[]{:S(2)}) collective-permute-start(bf16[2,128,1152]{2,1,0:T(8,128)(2,1)S(1)} %get-tuple-element.65), channel_id=1, source_target_pairs={{0,4},{4,0},{8,12},{12,8},{1,5},{5,1},{9,13},{13,9},{2,6},{6,2},{1... | collective-permute-start | bytes 1769480 | tf_op jit(solution)/shard_map/ppermute | solution.py:32
  45.3 5.5 %collective-permute-start.15 = (bf16[2,128,1152]{2,1,0:T(8,128)(2,1)S(1)}, bf16[2,128,1152]{2,1,0:T(8,128)(2,1)S(1)}, u32[]{:S(2)}, u32[]{:S(2)}) collective-permute-start(bf16[2,128,1152]{2,1,0:T(8,128)(2,1)S(1)} %get-tuple-element.75), channel_id=1, source_target_pairs={{0,4},{4,0},{8,12},{12,8},{1,5},{5,1},{9,13},{13,9},{2,6},{6,2},{1... | collective-permute-start | bytes 1769480 | tf_op jit(solution)/shard_map/ppermute | solution.py:32
  45.6 27.5 %collective-permute-start.16 = (bf16[256,384]{1,0:T(8,128)(2,1)S(1)}, bf16[256,384]{1,0:T(8,128)(2,1)S(1)}, u32[]{:S(2)}, u32[]{:S(2)}) collective-permute-start(bf16[256,384]{1,0:T(8,128)(2,1)S(1)} %get-tuple-element.80), channel_id=1, source_target_pairs={{0,1},{1,0},{2,3},{3,2},{4,5},{5,4},{6,7},{7,6},{8,9},{9,8},{10,11... | collective-permute-start | bytes 589832 | tf_op jit(solution)/shard_map/ppermute | solution.py:32
  48.4 24.7 %collective-permute-start.17 = (bf16[256,384]{1,0:T(8,128)(2,1)S(1)}, bf16[256,384]{1,0:T(8,128)(2,1)S(1)}, u32[]{:S(2)}, u32[]{:S(2)}) collective-permute-start(bf16[256,384]{1,0:T(8,128)(2,1)S(1)} %get-tuple-element.81), channel_id=1, source_target_pairs={{0,2},{1,3},{2,0},{3,1},{4,6},{5,7},{6,4},{7,5},{8,10},{9,11},{10,... | collective-permute-start | bytes 589832 | tf_op jit(solution)/shard_map/ppermute | solution.py:32
  50.0 23.1 %collective-permute-start.18 = (bf16[256,384]{1,0:T(8,128)(2,1)S(1)}, bf16[256,384]{1,0:T(8,128)(2,1)S(1)}, u32[]{:S(2)}, u32[]{:S(2)}) collective-permute-start(bf16[256,384]{1,0:T(8,128)(2,1)S(1)} %get-tuple-element.82), channel_id=1, source_target_pairs={{0,3},{1,2},{2,1},{3,0},{4,7},{5,6},{6,5},{7,4},{8,11},{9,10},{10,... | collective-permute-start | bytes 589832 | tf_op jit(solution)/shard_map/ppermute | solution.py:32
  50.9 9.4 %collective-permute-start.1 = (bf16[128,1280]{1,0:T(8,128)(2,1)S(1)}, bf16[128,1280]{1,0:T(8,128)(2,1)S(1)}, u32[]{:S(2)}, u32[]{:S(2)}) collective-permute-start(bf16[128,1280]{1,0:T(8,128)(2,1)S(1)} %get-tuple-element.24), channel_id=1, source_target_pairs={{0,8},{4,12},{8,0},{12,4},{1,9},{5,13},{9,1},{13,5},{2,10},{6,14},... | collective-permute-start | bytes 983048 | tf_op jit(solution)/shard_map/cond/branch_1_fun/ppermute | solution.py:32
  60.4 12.7 %collective-permute-start.2 = (bf16[128,1536]{1,0:T(8,128)(2,1)S(1)}, bf16[128,1536]{1,0:T(8,128)(2,1)}, u32[]{:S(2)}, u32[]{:S(2)}) collective-permute-start(bf16[128,1536]{1,0:T(8,128)(2,1)S(1)} %join.1), channel_id=1, source_target_pairs={{0,1},{1,0},{2,3},{3,2},{4,5},{5,4},{6,7},{7,6},{8,9},{9,8},{10,11... | collective-permute-start | bytes 1179656 | tf_op jit(solution)/shard_map/cond/branch_1_fun/ppermute | solution.py:32
  61.4 8.0 %collective-permute-start = (bf16[128,1280]{1,0:T(8,128)(2,1)S(1)}, bf16[128,1280]{1,0:T(8,128)(2,1)}, u32[]{:S(2)}, u32[]{:S(2)}) collective-permute-start(bf16[128,1280]{1,0:T(8,128)(2,1)S(1)} %get-tuple-element.20), channel_id=1, source_target_pairs={{0,8},{4,12},{8,0},{12,4},{1,9},{5,13},{9,1},{13,5},{2,10},{6,14},... | collective-permute-start | bytes 983048 | tf_op jit(solution)/shard_map/cond/branch_1_fun/ppermute | solution.py:32

commit v7 on v6

--- a/solution.py
+++ b/solution.py
@@ -33,14 +33,15 @@
 
 
 def attention_kernel(
-    where_ref, chosen_ref, *refs, sources, chunks, far_ids, carry, rows, heads, hdim, parts, scale
+    where_ref, chosen_ref, *refs, sources, shares, chunks, far_ids, carry, rows, heads, hdim, parts, scale
 ):
     half = chunks // 2
     count = 1 + max(max(source[0], source[3]) for source in sources)
     buffers = refs[:count]
-    weight_refs = refs[count : count + parts]
-    carried = refs[count + parts : count + 2 * parts] if carry == "in" else None
-    outs = refs[count + (2 if carry == "in" else 1) * parts :]
+    weight_refs = refs[count : count + len(shares)]
+    refs = refs[count + len(shares) :]
+    carried = refs[:parts] if carry == "in" else None
+    outs = refs[parts:] if carry == "in" else refs
     grad_w_refs = outs[:parts]
     keep_ref, send_ref = outs[parts : parts + 2]
     (
@@ -54,9 +55,13 @@
     line = where_ref[1]
 
     copies = []
-    for j in range(parts):
-        start = pl.multiple_of((line ^ j) * part_rows, part_rows)
-        copies.append((weight_refs[j], weight.at[pl.ds(start, part_rows), :]))
+    for ref, (j, side) in zip(weight_refs, shares):
+        size = ref.shape[0]
+        start = (line ^ j) * part_rows
+        if side is not None:
+            start = start + (where_ref[3] ^ side) * size
+        target = pl.ds(pl.multiple_of(start, size), size)
+        copies.append((ref, weight.at[target, :]))
     at = 0
     for index, first, size, up, start in sources:
         target = pl.ds(at, size)
@@ -279,14 +284,15 @@
             outs[2 + m][:, width:] = jnp.where(flip, sums[0], sums[1])
 
 
-def pack_kernel(where_ref, blocks_ref, *refs, lefts, seqs, chunks, width, noted):
+def pack_kernel(where_ref, blocks_ref, *refs, lefts, seqs, chunks, width, noted, halves):
     tokens, up = refs[:2]
     weight_refs = refs[2:5]
     hops = len(lefts)
     sends = refs[5 : 5 + hops]
     own_up = refs[5 + hops]
     weight_sends = refs[6 + hops : 6 + hops + seqs]
-    note, blocks, sems = refs[6 + hops + seqs :]
+    half_sends = refs[6 + hops + seqs : 6 + hops + seqs + halves]
+    note, blocks, sems = refs[6 + hops + seqs + halves :]
     fetch = pltpu.make_async_copy(blocks_ref, blocks, sems.at[sems.shape[0] - 1])
     fetch.start()
     model = tokens.shape[1]
@@ -304,12 +310,14 @@
     copies.append((up.at[:, columns(0)], own_up))
     for i in range(seqs):
         for m in range(3):
-            copies.append(
-                (
-                    weight_refs[m].at[:, columns(i * chunks)],
-                    weight_sends[i].at[:, m * width : (m + 1) * width],
-                )
-            )
+            source = weight_refs[m].at[:, columns(i * chunks)]
+            lanes = slice(m * width, (m + 1) * width)
+            copies.append((source, weight_sends[i].at[:, lanes]))
+            if i < halves:
+                size = half_sends[i].shape[0]
+                part = pl.ds(pl.multiple_of(where_ref[3] * size, size), size)
+                source = weight_refs[m].at[part, columns(i * chunks)]
+                copies.append((source, half_sends[i].at[:, lanes]))
     copies = [
         pltpu.make_async_copy(source, target, sems.at[index])
         for index, (source, target) in enumerate(copies)
@@ -343,7 +351,7 @@
     line = lax.axis_index("dp")
     side = line % seqs
 
-    where = jnp.stack([position, line, side]).astype(jnp.int32)
+    where = jnp.stack([position, line, side, lax.axis_index("groups")]).astype(jnp.int32)
     hops = [("dp", 1, chunks)] if seqs == 2 else []
     bit = chunks // 2
     while bit:
@@ -357,20 +365,28 @@
     lefts = [groups >> (k + 1) for k in range(len(hops))]
     packed = width % 128 == 0
     noted = 128 if seqs == 2 else 0
+    halves = 1 if seqs == 2 and lax.axis_size("groups") == 2 else 0
     if packed:
         sizes = [model + left * width + (noted if k == 0 else 0) for k, left in enumerate(lefts)]
         outs = pl.pallas_call(
             lambda *refs: pack_kernel(
-                *refs, lefts=lefts, seqs=seqs, chunks=chunks, width=width, noted=noted
+                *refs,
+                lefts=lefts,
+                seqs=seqs,
+                chunks=chunks,
+                width=width,
+                noted=noted,
+                halves=halves,
             ),
             out_shape=tuple(jax.ShapeDtypeStruct((rows, size), BF16) for size in sizes + [width])
-            + (jax.ShapeDtypeStruct((model // parts, 3 * width), BF16),) * seqs,
+            + (jax.ShapeDtypeStruct((model // parts, 3 * width), BF16),) * seqs
+            + (jax.ShapeDtypeStruct((model // parts // 2, 3 * width), BF16),) * halves,
             in_specs=[smem] + [hbm] * 6,
-            out_specs=(vmem,) * (len(hops) + 1 + seqs),
+            out_specs=(vmem,) * (len(hops) + 1 + seqs + halves),
             scratch_shapes=[
                 pltpu.VMEM((rows, 128), BF16),
                 pltpu.SMEM((1, 2), jnp.int32),
-                pltpu.SemaphoreType.DMA((len(hops) + sum(lefts) + 2 + 3 * seqs,)),
+                pltpu.SemaphoreType.DMA((len(hops) + sum(lefts) + 2 + 3 * (seqs + halves),)),
             ],
             compiler_params=SMALL,
             cost_estimate=cost(2),
@@ -384,7 +400,8 @@
         )
         own_sends = outs[: len(hops)]
         own_up = outs[len(hops)]
-        sends = outs[len(hops) + 1 :]
+        sends = outs[len(hops) + 1 : len(hops) + 1 + seqs]
+        half_sends = outs[len(hops) + 1 + seqs :]
     else:
 
         def slice_of(value, offset):
@@ -405,8 +422,14 @@
 
     arrived = [xor_permute(own_sends[k], *hops[k][:2]) for k in range(seqs)]
     weights = [sends[0]]
+    shares = [(0, None)]
+    fetched = []
     for j in range(1, parts):
-        weights.append(xor_permute(sends[j % seqs], "dp", j))
+        if j == 2 and halves:
+            fetched.append(xor_permute(half_sends[j % seqs], "dp", j))
+        else:
+            weights.append(xor_permute(sends[j % seqs], "dp", j))
+            shares.append((j, None))
 
     length = chunks * rows
     live = global_blocks[0, 0] >= 0
@@ -421,12 +444,13 @@
             *operands,
         )
 
-    def attend(buffers, sources, weights, carry=None, carried=(), far_ids=None):
+    def attend(buffers, sources, weights, shares, carry=None, carried=(), far_ids=None):
         kind = F32 if carry == "out" else BF16
         results = pl.pallas_call(
             lambda *refs: attention_kernel(
                 *refs,
                 sources=sources,
+                shares=shares,
                 chunks=chunks,
                 far_ids=far_ids,
                 carry=carry,
@@ -439,7 +463,7 @@
             out_shape=(jax.ShapeDtypeStruct((model // parts, 3 * width), kind),) * parts
             + (jax.ShapeDtypeStruct((chunks // 2, rows, model + width), BF16),) * 2,
             in_specs=[smem] * 2
-            + [pl.BlockSpec(memory_space=pl.ANY)] * (len(buffers) + parts)
+            + [pl.BlockSpec(memory_space=pl.ANY)] * (len(buffers) + len(weights))
             + [vmem] * len(carried),
             out_specs=(vmem,) * (parts + 2),
             scratch_shapes=[
@@ -453,7 +477,7 @@
                 pltpu.VMEM((length, 3 * width), BF16),
                 pltpu.VMEM((length, width), BF16),
                 pltpu.VMEM((16, 128), BF16),
-                pltpu.SemaphoreType.DMA((2 * len(sources) + parts + 1,)),
+                pltpu.SemaphoreType.DMA((2 * len(sources) + len(weights) + 1,)),
             ],
             compiler_params=pltpu.CompilerParams(vmem_limit_bytes=24 * 1024 * 1024),
             cost_estimate=cost(14 // seqs),
@@ -488,11 +512,16 @@
         line_hop, far_hop, near_hop = [hop[:2] for hop in hops]
         tz, tx = arrived
 
-        def share(own, tx):
+        def share(own, tx, *fetched):
             rest = jnp.concatenate([tx[:, :model], tx[:, model + width :]], axis=1)
-            return xor_permute(jnp.concatenate([own, rest], axis=0), *near_hop)
-
-        shared = guarded(share, own_sends[2], tx)
+            shared = xor_permute(jnp.concatenate([own, rest], axis=0), *near_hop)
+            return (shared, *[xor_permute(value, "groups", 1) for value in fetched])
+
+        shared, *others = guarded(share, own_sends[2], tx, *fetched)
+        tz, shared = lax.optimization_barrier((tz, shared))
+        for j, (here, there) in enumerate(zip(fetched, others), 2):
+            weights += [here, there]
+            shares += [(j, 0), (j, 1)]
 
         def both(tz, tx, shared, own_tokens, own_up, *weights):
             lo = model + 2 * width
@@ -513,6 +542,7 @@
                     (1, rows, rows, 1, model),
                 ),
                 weights,
+                shares,
                 carry="out",
             )
             first = list(first)
@@ -531,6 +561,7 @@
                     (5, 0, part, 5, up),
                 ),
                 weights,
+                shares,
                 carry="in",
                 carried=first,
                 far_ids=model + 4 * width,
@@ -571,7 +602,7 @@
         ups = [own_up] + [value[:, model : model + width] for value in pieces]
         buffers = [own_tokens] + [value[:, :model] for value in pieces] + ups
         grad_w, keep, send = attend(
-            buffers, [(o, 0, rows, groups + o, 0) for o in range(groups)], weights
+            buffers, [(o, 0, rows, groups + o, 0) for o in range(groups)], weights, shares
         )
 
         def collect(keep, send):

time: 75.6 us -> 74.5 us (0.985)
  waiting for transfers between devices: 33.2 us -> 30.2 us
  starting transfers between devices: 21.3 us -> 22.7 us
    ppermute x19 -> x20, waiting for transfers between devices: 33.2 us -> 30.2 us  [xor_permute(): return lax.ppermute(value, axis, [(i, i ^ bit) for i in range(count)])]
    ppermute x19 -> x20, starting transfers between devices: 21.3 us -> 22.7 us  [xor_permute(): return lax.ppermute(value, axis, [(i, i ^ bit) for i in range(count)])]
  transfers between devices with their start and end apart: 19 -> 20, of which waited for: 9 -> 8; matrix products, arithmetic and copies ran while one was open for 0% -> 0% of each run, Pallas kernels for 21% -> 21%
where the time goes in v7:
time: 74.5 us; the launch traced here: 74.2 us
  waiting for transfers between devices  30.2 us (41%)
  starting transfers between devices  22.7 us (30%)
  Pallas kernels  20.3 us (27%)
  between operations  0.79 us (1%)
    ppermute x20, waiting for transfers between devices, xor_permute(): return lax.ppermute(value, axis, [(i, i ^ bit) for i in range(count)])  30.2 us
    ppermute x20, starting transfers between devices, xor_permute(): return lax.ppermute(value, axis, [(i, i ^ bit) for i in range(count)])  22.7 us
    pallas_call x2, Pallas kernels, attend(): pl.pallas_call(lambda *refs: attention_kernel(*refs, sources=sources, sha...  15.6 us
    pallas_call x1, Pallas kernels, per_device(): pl.pallas_call(lambda *refs: final_kernel(*refs, model=model, seqs=seqs,...  2.27 us
    pallas_call x1, Pallas kernels, per_device(): pl.pallas_call(lambda *refs: pack_kernel(*refs, lefts=lefts, seqs=seqs, c...  2.12 us
  transfers between devices with their start and end apart: 20, of which 8 were waited for; matrix products, arithmetic and copies ran while one was open for 0% of the time, Pallas kernels for 21%

profile of v7, /device:TPU:0, one launch (start us, length us, event | category | flops | bytes accessed | tf_op | source)
XLA Modules:
  0.0 74.2 jit_solution(15586525523435783004)
XLA Ops:
  0.7 2.1 %pack.1 = (bf16[128,1664]{1,0:T(8,128)(2,1)S(1)}, bf16[128,1280]{1,0:T(8,128)(2,1)S(1)}, bf16[128,1152]{1,0:T(8,128)(2,1)S(1)}, bf16[128,128]{1,0:T(8,128)(2,1)S...) custom-call(s32[4]{0:T(128)S(1)} %pad_add_fusion.refs_0_, ...), custom_call_target="tpu_custom_call" | custom-call | bytes 6000000 | tf_op jit(solution)/shard_map/pack/pallas_call | solution.py:371
  2.8 3.1 %collective-permute-start.5 = (bf16[128,1664]{1,0:T(8,128)(2,1)S(1)}, bf16[128,1664]{1,0:T(8,128)(2,1)S(1)}, u32[]{:S(2)}, u32[]{:S(2)}) collective-permute-start(bf16[128,1664]{1,0:T(8,128)(2,1)S(1)} %get-tuple-element.64), channel_id=1, source_target_pairs={{0,1},{1,0},{2,3},{3,2},{4,5},{5,4},{6,7},{7,6},{8,9},{9,8},{10,11... | collective-permute-start | bytes 1277960 | tf_op jit(solution)/shard_map/ppermute | solution.py:32
  6.0 1.5 %collective-permute-start.6 = (bf16[128,1280]{1,0:T(8,128)(2,1)S(1)}, bf16[128,1280]{1,0:T(8,128)(2,1)S(1)}, u32[]{:S(2)}, u32[]{:S(2)}) collective-permute-start(bf16[128,1280]{1,0:T(8,128)(2,1)S(1)} %get-tuple-element.65), channel_id=1, source_target_pairs={{0,8},{4,12},{8,0},{12,4},{1,9},{5,13},{9,1},{13,5},{2,10},{6,14},... | collective-permute-start | bytes 983048 | tf_op jit(solution)/shard_map/ppermute | solution.py:32
  7.5 2.6 %collective-permute-start.7 = (bf16[128,384]{1,0:T(8,128)(2,1)S(1)}, bf16[128,384]{1,0:T(8,128)(2,1)S(1)}, u32[]{:S(2)}, u32[]{:S(2)}) collective-permute-start(bf16[128,384]{1,0:T(8,128)(2,1)S(1)} %get-tuple-element.67), channel_id=1, source_target_pairs={{0,2},{1,3},{2,0},{3,1},{4,6},{5,7},{6,4},{7,5},{8,10},{9,11},{10,... | collective-permute-start | bytes 294920 | tf_op jit(solution)/shard_map/ppermute | solution.py:32
  10.3 0.7 collective-permute-start.8
  11.0 7.3 %collective-permute-done.7.refs_9_.refs_11_ = bf16[128,384]{1,0:T(8,128)(2,1)S(1)} collective-permute-done((bf16[128,384]{1,0:T(8,128)(2,1)S(1)}, bf16[128,384]{1,0:T(8,128)(2,1)S(1)}, u32[]{:S(2)}, u32[]{:S(2)}) %collective-permute-start.7) | collective-permute-done | bytes 98336 | tf_op jit(solution)/shard_map/ppermute | solution.py:32
  18.3 5.5 %conditional.2 = (bf16[256,1152]{1,0:T(8,128)(2,1)}, bf16[128,384]{1,0:T(8,128)(2,1)}) conditional(s32[]{:T(128)} %bitcast.4, () %tuple.27, (bf16[128,1280]{1,0:T(8,128)(2,1)S(1)}, bf16[128,1152]{1,0:T(8,128)(2,1)S(1)}, bf16[128,384]{1,0:T(8,128)(2,1)S(1)}) %tuple.28), branch_computations={%region_0.1_spmd, %region_1.2_spmd} | conditional | flops 1769472 | bytes 4522080 | solution.py:438
  18.5 1.6 %collective-permute-start.4 = (bf16[128,384]{1,0:T(8,128)(2,1)S(1)}, bf16[128,384]{1,0:T(8,128)(2,1)}, u32[]{:S(2)}, u32[]{:S(2)}) collective-permute-start(bf16[128,384]{1,0:T(8,128)(2,1)S(1)} %get-tuple-element.16), channel_id=1, source_target_pairs={{0,16},{16,0},{1,17},{17,1},{2,18},{18,2},{3,19},{19,3},{4,20},{20... | collective-permute-start | bytes 294920 | tf_op jit(solution)/shard_map/cond/branch_1_fun/ppermute | solution.py:32
  20.0 3.7 %collective-permute-done.4 = bf16[128,384]{1,0:T(8,128)(2,1)} collective-permute-done((bf16[128,384]{1,0:T(8,128)(2,1)S(1)}, bf16[128,384]{1,0:T(8,128)(2,1)}, u32[]{:S(2)}, u32[]{:S(2)}) %collective-permute-start.4) | collective-permute-done | bytes 98336 | tf_op jit(solution)/shard_map/cond/branch_1_fun/ppermute | solution.py:32
  23.9 1.6 %collective-permute-start.12 = (bf16[64,1280]{1,0:T(8,128)(2,1)S(1)}, bf16[64,1280]{1,0:T(8,128)(2,1)S(1)}, u32[]{:S(2)}, u32[]{:S(2)}) collective-permute-start(bf16[64,1280]{1,0:T(8,128)(2,1)S(1)} %pad_maximum_fusion), channel_id=1, source_target_pairs={{0,8},{4,12},{8,0},{12,4},{1,9},{5,13},{9,1},{13,5},{2,10},{6,14},... | collective-permute-start | bytes 491528 | tf_op jit(solution)/shard_map/ppermute | solution.py:32
  26.3 7.9 %attention.2 = (f32[256,384]{1,0:T(8,128)S(1)}, f32[256,384]{1,0:T(8,128)S(1)}, f32[256,384]{1,0:T(8,128)S(1)}, f32[256,384]{1,0:T(8,128)S(1)}, bf16[2,128,1152]...) custom-call(s32[4]{0:T(128)S(1)} %pad_add_fusion.refs_0_, s32[2]{0:T(128)S(1)} %bitcast.14, ...), custom_call_target="tpu_custom_call" | custom-call | bytes 21000000 | tf_op jit(solution)/shard_map/attention/pallas_call | solution.py:449
  34.9 0.8 %collective-permute-done.14.refs_6_ = bf16[64,1280]{1,0:T(8,128)(2,1)S(1)} collective-permute-done((bf16[64,1280]{1,0:T(8,128)(2,1)S(1)}, bf16[64,1280]{1,0:T(8,128)(2,1)S(1)}, u32[]{:S(2)}, u32[]{:S(2)}) %collective-permute-start.14) | collective-permute-done | bytes 163872 | tf_op jit(solution)/shard_map/ppermute | solution.py:32
  35.9 7.7 %attention.3 = (bf16[256,384]{1,0:T(8,128)(2,1)S(1)}, bf16[256,384]{1,0:T(8,128)(2,1)S(1)}, bf16[256,384]{1,0:T(8,128)(2,1)S(1)}, bf16[256,384]{1,0:T(8,128)(2,1...) custom-call(s32[4]{0:T(128)S(1)} %pad_add_fusion.refs_0_, s32[2]{0:T(128)S(1)} %bitcast.15, ...), custom_call_target="tpu_custom_call" | custom-call | bytes 21000000 | tf_op jit(solution)/shard_map/attention/pallas_call | solution.py:449
  44.0 3.3 %collective-permute-start.17 = (bf16[256,384]{1,0:T(8,128)(2,1)S(1)}, bf16[256,384]{1,0:T(8,128)(2,1)S(1)}, u32[]{:S(2)}, u32[]{:S(2)}) collective-permute-start(bf16[256,384]{1,0:T(8,128)(2,1)S(1)} %get-tuple-element.90), channel_id=1, source_target_pairs={{0,1},{1,0},{2,3},{3,2},{4,5},{5,4},{6,7},{7,6},{8,9},{9,8},{10,11... | collective-permute-start | bytes 589832 | tf_op jit(solution)/shard_map/ppermute | solution.py:32
  47.3 1.1 %collective-permute-start.18 = (bf16[256,384]{1,0:T(8,128)(2,1)S(1)}, bf16[256,384]{1,0:T(8,128)(2,1)S(1)}, u32[]{:S(2)}, u32[]{:S(2)}) collective-permute-start(bf16[256,384]{1,0:T(8,128)(2,1)S(1)} %get-tuple-element.91), channel_id=1, source_target_pairs={{0,2},{1,3},{2,0},{3,1},{4,6},{5,7},{6,4},{7,5},{8,10},{9,11},{10,... | collective-permute-start | bytes 589832 | tf_op jit(solution)/shard_map/ppermute | solution.py:32
  48.4 1.3 %collective-permute-start.19 = (bf16[256,384]{1,0:T(8,128)(2,1)S(1)}, bf16[256,384]{1,0:T(8,128)(2,1)S(1)}, u32[]{:S(2)}, u32[]{:S(2)}) collective-permute-start(bf16[256,384]{1,0:T(8,128)(2,1)S(1)} %get-tuple-element.92), channel_id=1, source_target_pairs={{0,3},{1,2},{2,1},{3,0},{4,7},{5,6},{6,5},{7,4},{8,11},{9,10},{10,... | collective-permute-start | bytes 589832 | tf_op jit(solution)/shard_map/ppermute | solution.py:32
  49.7 22.3 %conditional.3 = (bf16[128,1280]{1,0:T(8,128)(2,1)S(1)}, bf16[128,1280]{1,0:T(8,128)(2,1)}, bf16[128,1536]{1,0:T(8,128)(2,1)}) conditional(s32[]{:T(128)} %bitcast.4, () %tuple.26, (bf16[2,128,1152]{2,1,0:T(8,128)(2,1)S(1)}, bf16[2,128,1152]{2,1,0:T(8,128)(2,1)S(1)}, bf16[2,128,1152]{2,1,0:T(8,128)(2,1)S(1)}, ...), branch_computations={%region_2.3_spmd, %region_3.4_spmd} | conditional | bytes 13194448 | solution.py:438
  49.8 1.6 %collective-permute-start.1 = (bf16[128,1280]{1,0:T(8,128)(2,1)S(1)}, bf16[128,1280]{1,0:T(8,128)(2,1)S(1)}, u32[]{:S(2)}, u32[]{:S(2)}) collective-permute-start(bf16[128,1280]{1,0:T(8,128)(2,1)S(1)} %get-tuple-element.24), channel_id=1, source_target_pairs={{0,8},{4,12},{8,0},{12,4},{1,9},{5,13},{9,1},{13,5},{2,10},{6,14},... | collective-permute-start | bytes 983048 | tf_op jit(solution)/shard_map/cond/branch_1_fun/ppermute | solution.py:32
  51.4 7.8 %collective-permute-done.1.refs_1_ = bf16[128,1280]{1,0:T(8,128)(2,1)S(1)} collective-permute-done((bf16[128,1280]{1,0:T(8,128)(2,1)S(1)}, bf16[128,1280]{1,0:T(8,128)(2,1)S(1)}, u32[]{:S(2)}, u32[]{:S(2)}) %collective-permute-start.1) | collective-permute-done | bytes 327712 | tf_op jit(solution)/shard_map/cond/branch_1_fun/ppermute | solution.py:32
  59.2 0.9 %collective-permute-start.2 = (bf16[128,1536]{1,0:T(8,128)(2,1)S(1)}, bf16[128,1536]{1,0:T(8,128)(2,1)}, u32[]{:S(2)}, u32[]{:S(2)}) collective-permute-start(bf16[128,1536]{1,0:T(8,128)(2,1)S(1)} %join.1), channel_id=1, source_target_pairs={{0,1},{1,0},{2,3},{3,2},{4,5},{5,4},{6,7},{7,6},{8,9},{9,8},{10,11... | collective-permute-start | bytes 1179656 | tf_op jit(solution)/shard_map/cond/branch_1_fun/ppermute | solution.py:32
  60.3 1.6 %collective-permute-start = (bf16[128,1280]{1,0:T(8,128)(2,1)S(1)}, bf16[128,1280]{1,0:T(8,128)(2,1)}, u32[]{:S(2)}, u32[]{:S(2)}) collective-permute-start(bf16[128,1280]{1,0:T(8,128)(2,1)S(1)} %get-tuple-element.20), channel_id=1, source_target_pairs={{0,8},{4,12},{8,0},{12,4},{1,9},{5,13},{9,1},{13,5},{2,10},{6,14},... | collective-permute-start | bytes 983048 | tf_op jit(solution)/shard_map/cond/branch_1_fun/ppermute | solution.py:32
  61.9 6.4 %collective-permute-done = bf16[128,1280]{1,0:T(8,128)(2,1)} collective-permute-done((bf16[128,1280]{1,0:T(8,128)(2,1)S(1)}, bf16[128,1280]{1,0:T(8,128)(2,1)}, u32[]{:S(2)}, u32[]{:S(2)}) %collective-permute-start) | collective-permute-done | bytes 327712 | tf_op jit(solution)/shard_map/cond/branch_1_fun/ppermute | solution.py:32
  68.2 3.7 %collective-permute-done.2 = bf16[128,1536]{1,0:T(8,128)(2,1)} collective-permute-done((bf16[128,1536]{1,0:T(8,128)(2,1)S(1)}, bf16[128,1536]{1,0:T(8,128)(2,1)}, u32[]{:S(2)}, u32[]{:S(2)}) %collective-permute-start.2) | collective-permute-done | bytes 393248 | tf_op jit(solution)/shard_map/cond/branch_1_fun/ppermute | solution.py:32
  72.0 2.3 %finish.1 = (bf16[128,1024]{1,0:T(8,128)(2,1)}, bf16[128,1024]{1,0:T(8,128)(2,1)}, f32[256,256]{1,0:T(8,128)}, f32[256,256]{1,0:T(8,128)}, f32[256,256]{1,0:T(8,128)}) custom-call(s32[4]{0:T(128)S(1)} %pad_add_fusion.refs_0_, bf16[128,1280]{1,0:T(8,128)(2,1)S(1)} %get-tuple-element.86.refs_1_, bf16[128,1280]{1,0:T(8,128)(2,1)} %get-tuple-element.87.refs_2_, ...), custom_call_target="tpu_custom_call" | custom-call | bytes 6000000 | tf_op jit(solution)/shard_map/finish/pallas_call | solution.py:618
  (37 shorter events, 3.0 us)
Async XLA Ops:
  0.7 10.2 %copy-start.1 = (s32[1,2]{1,0:T(1,128)S(1)}, s32[1,2]{1,0:T(1,128)}, u32[]{:S(2)}) copy-start(s32[1,2]{1,0:T(1,128)} %refs_1_.1) | copy-start | bytes 28
  2.8 20.9 %collective-permute-start.5 = (bf16[128,1664]{1,0:T(8,128)(2,1)S(1)}, bf16[128,1664]{1,0:T(8,128)(2,1)S(1)}, u32[]{:S(2)}, u32[]{:S(2)}) collective-permute-start(bf16[128,1664]{1,0:T(8,128)(2,1)S(1)} %get-tuple-element.64), channel_id=1, source_target_pairs={{0,1},{1,0},{2,3},{3,2},{4,5},{5,4},{6,7},{7,6},{8,9},{9,8},{10,11... | collective-permute-start | bytes 1277960 | tf_op jit(solution)/shard_map/ppermute | solution.py:32
  6.0 12.3 %collective-permute-start.6 = (bf16[128,1280]{1,0:T(8,128)(2,1)S(1)}, bf16[128,1280]{1,0:T(8,128)(2,1)S(1)}, u32[]{:S(2)}, u32[]{:S(2)}) collective-permute-start(bf16[128,1280]{1,0:T(8,128)(2,1)S(1)} %get-tuple-element.65), channel_id=1, source_target_pairs={{0,8},{4,12},{8,0},{12,4},{1,9},{5,13},{9,1},{13,5},{2,10},{6,14},... | collective-permute-start | bytes 983048 | tf_op jit(solution)/shard_map/ppermute | solution.py:32
  7.5 10.8 %collective-permute-start.7 = (bf16[128,384]{1,0:T(8,128)(2,1)S(1)}, bf16[128,384]{1,0:T(8,128)(2,1)S(1)}, u32[]{:S(2)}, u32[]{:S(2)}) collective-permute-start(bf16[128,384]{1,0:T(8,128)(2,1)S(1)} %get-tuple-element.67), channel_id=1, source_target_pairs={{0,2},{1,3},{2,0},{3,1},{4,6},{5,7},{6,4},{7,5},{8,10},{9,11},{10,... | collective-permute-start | bytes 294920 | tf_op jit(solution)/shard_map/ppermute | solution.py:32
  10.0 16.1 %collective-permute-start.9 = (bf16[256,384]{1,0:T(8,128)(2,1)S(1)}, bf16[256,384]{1,0:T(8,128)(2,1)S(1)}, u32[]{:S(2)}, u32[]{:S(2)}) collective-permute-start(bf16[256,384]{1,0:T(8,128)(2,1)S(1)} %get-tuple-element.72), channel_id=1, source_target_pairs={{0,3},{1,2},{2,1},{3,0},{4,7},{5,6},{6,5},{7,4},{8,11},{9,10},{10,... | collective-permute-start | bytes 589832 | tf_op jit(solution)/shard_map/ppermute | solution.py:32
  10.3 16.1 %collective-permute-start.8 = (bf16[256,384]{1,0:T(8,128)(2,1)S(1)}, bf16[256,384]{1,0:T(8,128)(2,1)S(1)}, u32[]{:S(2)}, u32[]{:S(2)}) collective-permute-start(bf16[256,384]{1,0:T(8,128)(2,1)S(1)} %get-tuple-element.72), channel_id=1, source_target_pairs={{0,1},{1,0},{2,3},{3,2},{4,5},{5,4},{6,7},{7,6},{8,9},{9,8},{10,11... | collective-permute-start | bytes 589832 | tf_op jit(solution)/shard_map/ppermute | solution.py:32
  18.4 5.4 %collective-permute-start.3 = (bf16[256,1152]{1,0:T(8,128)(2,1)S(1)}, bf16[256,1152]{1,0:T(8,128)(2,1)}, u32[]{:S(2)}, u32[]{:S(2)}) collective-permute-start(bf16[256,1152]{1,0:T(8,128)(2,1)S(1)} %maximum_maximum_fusion), channel_id=1, source_target_pairs={{0,4},{4,0},{8,12},{12,8},{1,5},{5,1},{9,13},{13,9},{2,6},{6,2},{1... | collective-permute-start | bytes 1769480 | tf_op jit(solution)/shard_map/cond/branch_1_fun/ppermute | solution.py:32
  18.5 5.3 %collective-permute-start.4 = (bf16[128,384]{1,0:T(8,128)(2,1)S(1)}, bf16[128,384]{1,0:T(8,128)(2,1)}, u32[]{:S(2)}, u32[]{:S(2)}) collective-permute-start(bf16[128,384]{1,0:T(8,128)(2,1)S(1)} %get-tuple-element.16), channel_id=1, source_target_pairs={{0,16},{16,0},{1,17},{17,1},{2,18},{18,2},{3,19},{19,3},{4,20},{20... | collective-permute-start | bytes 294920 | tf_op jit(solution)/shard_map/cond/branch_1_fun/ppermute | solution.py:32
  23.8 2.6 %copy-start = (bf16[1,128,1024]{2,1,0:T(8,128)(2,1)S(1)}, bf16[1,128,1024]{2,1,0:T(8,128)(2,1)}, u32[]{:S(2)}) copy-start(bf16[1,128,1024]{2,1,0:T(8,128)(2,1)} %param.10) | copy-start | bytes 786436
  23.8 12.1 %collective-permute-start.11 = (bf16[128,1664]{1,0:T(8,128)(2,1)S(1)}, bf16[128,1664]{1,0:T(8,128)(2,1)S(1)}, u32[]{:S(2)}, u32[]{:S(2)}) collective-permute-start(bf16[128,1664]{1,0:T(8,128)(2,1)S(1)} %collective-permute-done.5.refs_2_), channel_id=1, source_target_pairs={{0,4},{4,0},{8,12},{12,8},{1,5},{5,1},{9,13},{13,9},{2,6},{6,2},{1... | collective-permute-start | bytes 1277960 | tf_op jit(solution)/shard_map/ppermute | solution.py:32
  23.9 10.3 %collective-permute-start.12 = (bf16[64,1280]{1,0:T(8,128)(2,1)S(1)}, bf16[64,1280]{1,0:T(8,128)(2,1)S(1)}, u32[]{:S(2)}, u32[]{:S(2)}) collective-permute-start(bf16[64,1280]{1,0:T(8,128)(2,1)S(1)} %pad_maximum_fusion), channel_id=1, source_target_pairs={{0,8},{4,12},{8,0},{12,4},{1,9},{5,13},{9,1},{13,5},{2,10},{6,14},... | collective-permute-start | bytes 491528 | tf_op jit(solution)/shard_map/ppermute | solution.py:32
  25.5 8.7 %collective-permute-start.13 = (bf16[64,1280]{1,0:T(8,128)(2,1)S(1)}, bf16[64,1280]{1,0:T(8,128)(2,1)S(1)}, u32[]{:S(2)}, u32[]{:S(2)}) collective-permute-start(bf16[64,1280]{1,0:T(8,128)(2,1)S(1)} %pad_maximum_fusion.1), channel_id=1, source_target_pairs={{0,8},{4,12},{8,0},{12,4},{1,9},{5,13},{9,1},{13,5},{2,10},{6,14},... | collective-permute-start | bytes 491528 | tf_op jit(solution)/shard_map/ppermute | solution.py:32
  34.2 1.5 %collective-permute-start.14 = (bf16[64,1280]{1,0:T(8,128)(2,1)S(1)}, bf16[64,1280]{1,0:T(8,128)(2,1)S(1)}, u32[]{:S(2)}, u32[]{:S(2)}) collective-permute-start(bf16[64,1280]{1,0:T(8,128)(2,1)S(1)} %collective-permute-done.12.refs_4_), channel_id=1, source_target_pairs={{0,4},{4,0},{8,12},{12,8},{1,5},{5,1},{9,13},{13,9},{2,6},{6,2},{1... | collective-permute-start | bytes 491528 | tf_op jit(solution)/shard_map/ppermute | solution.py:32
  34.3 1.6 %collective-permute-start.15 = (bf16[64,1280]{1,0:T(8,128)(2,1)S(1)}, bf16[64,1280]{1,0:T(8,128)(2,1)S(1)}, u32[]{:S(2)}, u32[]{:S(2)}) collective-permute-start(bf16[64,1280]{1,0:T(8,128)(2,1)S(1)} %collective-permute-done.13.refs_5_), channel_id=1, source_target_pairs={{0,4},{4,0},{8,12},{12,8},{1,5},{5,1},{9,13},{13,9},{2,6},{6,2},{1... | collective-permute-start | bytes 491528 | tf_op jit(solution)/shard_map/ppermute | solution.py:32
  34.8 14.8 %collective-permute-start.10 = (bf16[2,128,1152]{2,1,0:T(8,128)(2,1)S(1)}, bf16[2,128,1152]{2,1,0:T(8,128)(2,1)S(1)}, u32[]{:S(2)}, u32[]{:S(2)}) collective-permute-start(bf16[2,128,1152]{2,1,0:T(8,128)(2,1)S(1)} %get-tuple-element.75), channel_id=1, source_target_pairs={{0,4},{4,0},{8,12},{12,8},{1,5},{5,1},{9,13},{13,9},{2,6},{6,2},{1... | collective-permute-start | bytes 1769480 | tf_op jit(solution)/shard_map/ppermute | solution.py:32
  43.7 6.0 %collective-permute-start.16 = (bf16[2,128,1152]{2,1,0:T(8,128)(2,1)S(1)}, bf16[2,128,1152]{2,1,0:T(8,128)(2,1)S(1)}, u32[]{:S(2)}, u32[]{:S(2)}) collective-permute-start(bf16[2,128,1152]{2,1,0:T(8,128)(2,1)S(1)} %get-tuple-element.85), channel_id=1, source_target_pairs={{0,4},{4,0},{8,12},{12,8},{1,5},{5,1},{9,13},{13,9},{2,6},{6,2},{1... | collective-permute-start | bytes 1769480 | tf_op jit(solution)/shard_map/ppermute | solution.py:32
  44.0 27.9 %collective-permute-start.17 = (bf16[256,384]{1,0:T(8,128)(2,1)S(1)}, bf16[256,384]{1,0:T(8,128)(2,1)S(1)}, u32[]{:S(2)}, u32[]{:S(2)}) collective-permute-start(bf16[256,384]{1,0:T(8,128)(2,1)S(1)} %get-tuple-element.90), channel_id=1, source_target_pairs={{0,1},{1,0},{2,3},{3,2},{4,5},{5,4},{6,7},{7,6},{8,9},{9,8},{10,11... | collective-permute-start | bytes 589832 | tf_op jit(solution)/shard_map/ppermute | solution.py:32
  47.3 24.7 %collective-permute-start.18 = (bf16[256,384]{1,0:T(8,128)(2,1)S(1)}, bf16[256,384]{1,0:T(8,128)(2,1)S(1)}, u32[]{:S(2)}, u32[]{:S(2)}) collective-permute-start(bf16[256,384]{1,0:T(8,128)(2,1)S(1)} %get-tuple-element.91), channel_id=1, source_target_pairs={{0,2},{1,3},{2,0},{3,1},{4,6},{5,7},{6,4},{7,5},{8,10},{9,11},{10,... | collective-permute-start | bytes 589832 | tf_op jit(solution)/shard_map/ppermute | solution.py:32
  48.4 23.6 %collective-permute-start.19 = (bf16[256,384]{1,0:T(8,128)(2,1)S(1)}, bf16[256,384]{1,0:T(8,128)(2,1)S(1)}, u32[]{:S(2)}, u32[]{:S(2)}) collective-permute-start(bf16[256,384]{1,0:T(8,128)(2,1)S(1)} %get-tuple-element.92), channel_id=1, source_target_pairs={{0,3},{1,2},{2,1},{3,0},{4,7},{5,6},{6,5},{7,4},{8,11},{9,10},{10,... | collective-permute-start | bytes 589832 | tf_op jit(solution)/shard_map/ppermute | solution.py:32
  49.8 9.4 %collective-permute-start.1 = (bf16[128,1280]{1,0:T(8,128)(2,1)S(1)}, bf16[128,1280]{1,0:T(8,128)(2,1)S(1)}, u32[]{:S(2)}, u32[]{:S(2)}) collective-permute-start(bf16[128,1280]{1,0:T(8,128)(2,1)S(1)} %get-tuple-element.24), channel_id=1, source_target_pairs={{0,8},{4,12},{8,0},{12,4},{1,9},{5,13},{9,1},{13,5},{2,10},{6,14},... | collective-permute-start | bytes 983048 | tf_op jit(solution)/shard_map/cond/branch_1_fun/ppermute | solution.py:32
  59.2 12.7 %collective-permute-start.2 = (bf16[128,1536]{1,0:T(8,128)(2,1)S(1)}, bf16[128,1536]{1,0:T(8,128)(2,1)}, u32[]{:S(2)}, u32[]{:S(2)}) collective-permute-start(bf16[128,1536]{1,0:T(8,128)(2,1)S(1)} %join.1), channel_id=1, source_target_pairs={{0,1},{1,0},{2,3},{3,2},{4,5},{5,4},{6,7},{7,6},{8,9},{9,8},{10,11... | collective-permute-start | bytes 1179656 | tf_op jit(solution)/shard_map/cond/branch_1_fun/ppermute | solution.py:32
  60.3 8.0 %collective-permute-start = (bf16[128,1280]{1,0:T(8,128)(2,1)S(1)}, bf16[128,1280]{1,0:T(8,128)(2,1)}, u32[]{:S(2)}, u32[]{:S(2)}) collective-permute-start(bf16[128,1280]{1,0:T(8,128)(2,1)S(1)} %get-tuple-element.20), channel_id=1, source_target_pairs={{0,8},{4,12},{8,0},{12,4},{1,9},{5,13},{9,1},{13,5},{2,10},{6,14},... | collective-permute-start | bytes 983048 | tf_op jit(solution)/shard_map/cond/branch_1_fun/ppermute | solution.py:32

commit v8 on v7

--- a/solution.py
+++ b/solution.py
@@ -92,7 +92,7 @@
 
     tile = min(512, length)
 
-    @pl.loop(0, length // tile)
+    @pl.loop(0, length // tile, unroll=length == tile)
     def _(t):
         at = pl.ds(pl.multiple_of(t * tile, tile), tile)
         out = jnp.dot(all_tokens[at, :], weight[...], preferred_element_type=F32)
@@ -122,7 +122,7 @@
 
     span = min(SPAN, chunks)
 
-    @pl.loop(0, chunks // span)
+    @pl.loop(0, chunks // span, unroll=chunks == span)
     def _(t):
         first, second = chosen
         shape = (block_count, 1, rows)
@@ -207,7 +207,7 @@
             out = out + carried[j][...]
         grad_w_refs[j][...] = out.astype(grad_w_refs[j].dtype)
 
-    @pl.loop(0, half)
+    @pl.loop(0, half, unroll=half == 2)
     def _(t):
         at = pl.ds(pl.multiple_of(t * 2 * rows, 2 * rows), 2 * rows)
         out = lax.dot_general(grads[at, :], weight[...], NT, preferred_element_type=F32)

time: 74.5 us -> 74.1 us (level)
  transfers between devices with their start and end apart: 20 -> 20, of which waited for: 8 -> 9; matrix products, arithmetic and copies ran while one was open for 0% -> 0% of each run, Pallas kernels for 21% -> 21%
where the time goes in v8:
time: 74.1 us; the launch traced here: 73.9 us
  waiting for transfers between devices  30.5 us (41%)
  starting transfers between devices  22.8 us (31%)
  Pallas kernels  19.6 us (26%)
  between operations  0.78 us (1%)
    ppermute x20, waiting for transfers between devices, xor_permute(): return lax.ppermute(value, axis, [(i, i ^ bit) for i in range(count)])  30.5 us
    ppermute x20, starting transfers between devices, xor_permute(): return lax.ppermute(value, axis, [(i, i ^ bit) for i in range(count)])  22.8 us
    pallas_call x2, Pallas kernels, attend(): pl.pallas_call(lambda *refs: attention_kernel(*refs, sources=sources, sha...  14.9 us
    pallas_call x1, Pallas kernels, per_device(): pl.pallas_call(lambda *refs: final_kernel(*refs, model=model, seqs=seqs,...  2.27 us
    pallas_call x1, Pallas kernels, per_device(): pl.pallas_call(lambda *refs: pack_kernel(*refs, lefts=lefts, seqs=seqs, c...  2.12 us
  transfers between devices with their start and end apart: 20, of which 9 were waited for; matrix products, arithmetic and copies ran while one was open for 0% of the time, Pallas kernels for 21%

profile of v8, /device:TPU:0, one launch (start us, length us, event | category | flops | bytes accessed | tf_op | source)
XLA Modules:
  0.0 73.9 jit_solution(8816745835069014641)
XLA Ops:
  0.7 2.1 %pack.1 = (bf16[128,1664]{1,0:T(8,128)(2,1)S(1)}, bf16[128,1280]{1,0:T(8,128)(2,1)S(1)}, bf16[128,1152]{1,0:T(8,128)(2,1)S(1)}, bf16[128,128]{1,0:T(8,128)(2,1)S...) custom-call(s32[4]{0:T(128)S(1)} %pad_add_fusion.refs_0_, ...), custom_call_target="tpu_custom_call" | custom-call | bytes 6000000 | tf_op jit(solution)/shard_map/pack/pallas_call | solution.py:371
  2.8 3.1 %collective-permute-start.5 = (bf16[128,1664]{1,0:T(8,128)(2,1)S(1)}, bf16[128,1664]{1,0:T(8,128)(2,1)S(1)}, u32[]{:S(2)}, u32[]{:S(2)}) collective-permute-start(bf16[128,1664]{1,0:T(8,128)(2,1)S(1)} %get-tuple-element.64), channel_id=1, source_target_pairs={{0,1},{1,0},{2,3},{3,2},{4,5},{5,4},{6,7},{7,6},{8,9},{9,8},{10,11... | collective-permute-start | bytes 1277960 | tf_op jit(solution)/shard_map/ppermute | solution.py:32
  6.0 1.5 %collective-permute-start.6 = (bf16[128,1280]{1,0:T(8,128)(2,1)S(1)}, bf16[128,1280]{1,0:T(8,128)(2,1)S(1)}, u32[]{:S(2)}, u32[]{:S(2)}) collective-permute-start(bf16[128,1280]{1,0:T(8,128)(2,1)S(1)} %get-tuple-element.65), channel_id=1, source_target_pairs={{0,8},{4,12},{8,0},{12,4},{1,9},{5,13},{9,1},{13,5},{2,10},{6,14},... | collective-permute-start | bytes 983048 | tf_op jit(solution)/shard_map/ppermute | solution.py:32
  7.5 2.6 %collective-permute-start.7 = (bf16[128,384]{1,0:T(8,128)(2,1)S(1)}, bf16[128,384]{1,0:T(8,128)(2,1)S(1)}, u32[]{:S(2)}, u32[]{:S(2)}) collective-permute-start(bf16[128,384]{1,0:T(8,128)(2,1)S(1)} %get-tuple-element.67), channel_id=1, source_target_pairs={{0,2},{1,3},{2,0},{3,1},{4,6},{5,7},{6,4},{7,5},{8,10},{9,11},{10,... | collective-permute-start | bytes 294920 | tf_op jit(solution)/shard_map/ppermute | solution.py:32
  10.3 0.7 collective-permute-start.8
  11.0 7.3 %collective-permute-done.7.refs_9_.refs_11_ = bf16[128,384]{1,0:T(8,128)(2,1)S(1)} collective-permute-done((bf16[128,384]{1,0:T(8,128)(2,1)S(1)}, bf16[128,384]{1,0:T(8,128)(2,1)S(1)}, u32[]{:S(2)}, u32[]{:S(2)}) %collective-permute-start.7) | collective-permute-done | bytes 98336 | tf_op jit(solution)/shard_map/ppermute | solution.py:32
  18.3 5.5 %conditional.2 = (bf16[256,1152]{1,0:T(8,128)(2,1)}, bf16[128,384]{1,0:T(8,128)(2,1)}) conditional(s32[]{:T(128)} %bitcast.4, () %tuple.27, (bf16[128,1280]{1,0:T(8,128)(2,1)S(1)}, bf16[128,1152]{1,0:T(8,128)(2,1)S(1)}, bf16[128,384]{1,0:T(8,128)(2,1)S(1)}) %tuple.28), branch_computations={%region_0.1_spmd, %region_1.2_spmd} | conditional | flops 1769472 | bytes 4522080 | solution.py:438
  18.5 1.6 %collective-permute-start.4 = (bf16[128,384]{1,0:T(8,128)(2,1)S(1)}, bf16[128,384]{1,0:T(8,128)(2,1)}, u32[]{:S(2)}, u32[]{:S(2)}) collective-permute-start(bf16[128,384]{1,0:T(8,128)(2,1)S(1)} %get-tuple-element.16), channel_id=1, source_target_pairs={{0,16},{16,0},{1,17},{17,1},{2,18},{18,2},{3,19},{19,3},{4,20},{20... | collective-permute-start | bytes 294920 | tf_op jit(solution)/shard_map/cond/branch_1_fun/ppermute | solution.py:32
  20.0 3.7 %collective-permute-done.4 = bf16[128,384]{1,0:T(8,128)(2,1)} collective-permute-done((bf16[128,384]{1,0:T(8,128)(2,1)S(1)}, bf16[128,384]{1,0:T(8,128)(2,1)}, u32[]{:S(2)}, u32[]{:S(2)}) %collective-permute-start.4) | collective-permute-done | bytes 98336 | tf_op jit(solution)/shard_map/cond/branch_1_fun/ppermute | solution.py:32
  23.9 1.6 %collective-permute-start.12 = (bf16[64,1280]{1,0:T(8,128)(2,1)S(1)}, bf16[64,1280]{1,0:T(8,128)(2,1)S(1)}, u32[]{:S(2)}, u32[]{:S(2)}) collective-permute-start(bf16[64,1280]{1,0:T(8,128)(2,1)S(1)} %pad_maximum_fusion), channel_id=1, source_target_pairs={{0,8},{4,12},{8,0},{12,4},{1,9},{5,13},{9,1},{13,5},{2,10},{6,14},... | collective-permute-start | bytes 491528 | tf_op jit(solution)/shard_map/ppermute | solution.py:32
  26.3 7.5 %attention.2 = (f32[256,384]{1,0:T(8,128)S(1)}, f32[256,384]{1,0:T(8,128)S(1)}, f32[256,384]{1,0:T(8,128)S(1)}, f32[256,384]{1,0:T(8,128)S(1)}, bf16[2,128,1152]...) custom-call(s32[4]{0:T(128)S(1)} %pad_add_fusion.refs_0_, s32[2]{0:T(128)S(1)} %bitcast.14, ...), custom_call_target="tpu_custom_call" | custom-call | bytes 21000000 | tf_op jit(solution)/shard_map/attention/pallas_call | solution.py:449
  34.6 0.9 %collective-permute-done.14.refs_6_ = bf16[64,1280]{1,0:T(8,128)(2,1)S(1)} collective-permute-done((bf16[64,1280]{1,0:T(8,128)(2,1)S(1)}, bf16[64,1280]{1,0:T(8,128)(2,1)S(1)}, u32[]{:S(2)}, u32[]{:S(2)}) %collective-permute-start.14) | collective-permute-done | bytes 163872 | tf_op jit(solution)/shard_map/ppermute | solution.py:32
  35.7 7.4 %attention.3 = (bf16[256,384]{1,0:T(8,128)(2,1)S(1)}, bf16[256,384]{1,0:T(8,128)(2,1)S(1)}, bf16[256,384]{1,0:T(8,128)(2,1)S(1)}, bf16[256,384]{1,0:T(8,128)(2,1...) custom-call(s32[4]{0:T(128)S(1)} %pad_add_fusion.refs_0_, s32[2]{0:T(128)S(1)} %bitcast.15, ...), custom_call_target="tpu_custom_call" | custom-call | bytes 21000000 | tf_op jit(solution)/shard_map/attention/pallas_call | solution.py:449
  43.5 3.5 %collective-permute-start.17 = (bf16[256,384]{1,0:T(8,128)(2,1)S(1)}, bf16[256,384]{1,0:T(8,128)(2,1)S(1)}, u32[]{:S(2)}, u32[]{:S(2)}) collective-permute-start(bf16[256,384]{1,0:T(8,128)(2,1)S(1)} %get-tuple-element.90), channel_id=1, source_target_pairs={{0,1},{1,0},{2,3},{3,2},{4,5},{5,4},{6,7},{7,6},{8,9},{9,8},{10,11... | collective-permute-start | bytes 589832 | tf_op jit(solution)/shard_map/ppermute | solution.py:32
  47.0 0.7 collective-permute-start.18
  47.7 1.6 %collective-permute-start.19 = (bf16[256,384]{1,0:T(8,128)(2,1)S(1)}, bf16[256,384]{1,0:T(8,128)(2,1)S(1)}, u32[]{:S(2)}, u32[]{:S(2)}) collective-permute-start(bf16[256,384]{1,0:T(8,128)(2,1)S(1)} %get-tuple-element.92), channel_id=1, source_target_pairs={{0,3},{1,2},{2,1},{3,0},{4,7},{5,6},{6,5},{7,4},{8,11},{9,10},{10,... | collective-permute-start | bytes 589832 | tf_op jit(solution)/shard_map/ppermute | solution.py:32
  49.3 22.3 %conditional.3 = (bf16[128,1280]{1,0:T(8,128)(2,1)S(1)}, bf16[128,1280]{1,0:T(8,128)(2,1)}, bf16[128,1536]{1,0:T(8,128)(2,1)}) conditional(s32[]{:T(128)} %bitcast.4, () %tuple.26, (bf16[2,128,1152]{2,1,0:T(8,128)(2,1)S(1)}, bf16[2,128,1152]{2,1,0:T(8,128)(2,1)S(1)}, bf16[2,128,1152]{2,1,0:T(8,128)(2,1)S(1)}, ...), branch_computations={%region_2.3_spmd, %region_3.4_spmd} | conditional | bytes 13194448 | solution.py:438
  49.5 1.6 %collective-permute-start.1 = (bf16[128,1280]{1,0:T(8,128)(2,1)S(1)}, bf16[128,1280]{1,0:T(8,128)(2,1)S(1)}, u32[]{:S(2)}, u32[]{:S(2)}) collective-permute-start(bf16[128,1280]{1,0:T(8,128)(2,1)S(1)} %get-tuple-element.24), channel_id=1, source_target_pairs={{0,8},{4,12},{8,0},{12,4},{1,9},{5,13},{9,1},{13,5},{2,10},{6,14},... | collective-permute-start | bytes 983048 | tf_op jit(solution)/shard_map/cond/branch_1_fun/ppermute | solution.py:32
  51.1 7.8 %collective-permute-done.1.refs_1_ = bf16[128,1280]{1,0:T(8,128)(2,1)S(1)} collective-permute-done((bf16[128,1280]{1,0:T(8,128)(2,1)S(1)}, bf16[128,1280]{1,0:T(8,128)(2,1)S(1)}, u32[]{:S(2)}, u32[]{:S(2)}) %collective-permute-start.1) | collective-permute-done | bytes 327712 | tf_op jit(solution)/shard_map/cond/branch_1_fun/ppermute | solution.py:32
  58.9 0.9 %collective-permute-start.2 = (bf16[128,1536]{1,0:T(8,128)(2,1)S(1)}, bf16[128,1536]{1,0:T(8,128)(2,1)}, u32[]{:S(2)}, u32[]{:S(2)}) collective-permute-start(bf16[128,1536]{1,0:T(8,128)(2,1)S(1)} %join.1), channel_id=1, source_target_pairs={{0,1},{1,0},{2,3},{3,2},{4,5},{5,4},{6,7},{7,6},{8,9},{9,8},{10,11... | collective-permute-start | bytes 1179656 | tf_op jit(solution)/shard_map/cond/branch_1_fun/ppermute | solution.py:32
  59.9 1.6 %collective-permute-start = (bf16[128,1280]{1,0:T(8,128)(2,1)S(1)}, bf16[128,1280]{1,0:T(8,128)(2,1)}, u32[]{:S(2)}, u32[]{:S(2)}) collective-permute-start(bf16[128,1280]{1,0:T(8,128)(2,1)S(1)} %get-tuple-element.20), channel_id=1, source_target_pairs={{0,8},{4,12},{8,0},{12,4},{1,9},{5,13},{9,1},{13,5},{2,10},{6,14},... | collective-permute-start | bytes 983048 | tf_op jit(solution)/shard_map/cond/branch_1_fun/ppermute | solution.py:32
  61.5 6.4 %collective-permute-done = bf16[128,1280]{1,0:T(8,128)(2,1)} collective-permute-done((bf16[128,1280]{1,0:T(8,128)(2,1)S(1)}, bf16[128,1280]{1,0:T(8,128)(2,1)}, u32[]{:S(2)}, u32[]{:S(2)}) %collective-permute-start) | collective-permute-done | bytes 327712 | tf_op jit(solution)/shard_map/cond/branch_1_fun/ppermute | solution.py:32
  67.9 3.7 %collective-permute-done.2 = bf16[128,1536]{1,0:T(8,128)(2,1)} collective-permute-done((bf16[128,1536]{1,0:T(8,128)(2,1)S(1)}, bf16[128,1536]{1,0:T(8,128)(2,1)}, u32[]{:S(2)}, u32[]{:S(2)}) %collective-permute-start.2) | collective-permute-done | bytes 393248 | tf_op jit(solution)/shard_map/cond/branch_1_fun/ppermute | solution.py:32
  71.7 2.3 %finish.1 = (bf16[128,1024]{1,0:T(8,128)(2,1)}, bf16[128,1024]{1,0:T(8,128)(2,1)}, f32[256,256]{1,0:T(8,128)}, f32[256,256]{1,0:T(8,128)}, f32[256,256]{1,0:T(8,128)}) custom-call(s32[4]{0:T(128)S(1)} %pad_add_fusion.refs_0_, bf16[128,1280]{1,0:T(8,128)(2,1)S(1)} %get-tuple-element.86.refs_1_, bf16[128,1280]{1,0:T(8,128)(2,1)} %get-tuple-element.87.refs_2_, ...), custom_call_target="tpu_custom_call" | custom-call | bytes 6000000 | tf_op jit(solution)/shard_map/finish/pallas_call | solution.py:618
  (37 shorter events, 3.1 us)
Async XLA Ops:
  0.7 10.2 %copy-start.1 = (s32[1,2]{1,0:T(1,128)S(1)}, s32[1,2]{1,0:T(1,128)}, u32[]{:S(2)}) copy-start(s32[1,2]{1,0:T(1,128)} %refs_1_.1) | copy-start | bytes 28
  2.8 20.9 %collective-permute-start.5 = (bf16[128,1664]{1,0:T(8,128)(2,1)S(1)}, bf16[128,1664]{1,0:T(8,128)(2,1)S(1)}, u32[]{:S(2)}, u32[]{:S(2)}) collective-permute-start(bf16[128,1664]{1,0:T(8,128)(2,1)S(1)} %get-tuple-element.64), channel_id=1, source_target_pairs={{0,1},{1,0},{2,3},{3,2},{4,5},{5,4},{6,7},{7,6},{8,9},{9,8},{10,11... | collective-permute-start | bytes 1277960 | tf_op jit(solution)/shard_map/ppermute | solution.py:32
  6.0 12.3 %collective-permute-start.6 = (bf16[128,1280]{1,0:T(8,128)(2,1)S(1)}, bf16[128,1280]{1,0:T(8,128)(2,1)S(1)}, u32[]{:S(2)}, u32[]{:S(2)}) collective-permute-start(bf16[128,1280]{1,0:T(8,128)(2,1)S(1)} %get-tuple-element.65), channel_id=1, source_target_pairs={{0,8},{4,12},{8,0},{12,4},{1,9},{5,13},{9,1},{13,5},{2,10},{6,14},... | collective-permute-start | bytes 983048 | tf_op jit(solution)/shard_map/ppermute | solution.py:32
  7.5 10.8 %collective-permute-start.7 = (bf16[128,384]{1,0:T(8,128)(2,1)S(1)}, bf16[128,384]{1,0:T(8,128)(2,1)S(1)}, u32[]{:S(2)}, u32[]{:S(2)}) collective-permute-start(bf16[128,384]{1,0:T(8,128)(2,1)S(1)} %get-tuple-element.67), channel_id=1, source_target_pairs={{0,2},{1,3},{2,0},{3,1},{4,6},{5,7},{6,4},{7,5},{8,10},{9,11},{10,... | collective-permute-start | bytes 294920 | tf_op jit(solution)/shard_map/ppermute | solution.py:32
  10.0 16.1 %collective-permute-start.9 = (bf16[256,384]{1,0:T(8,128)(2,1)S(1)}, bf16[256,384]{1,0:T(8,128)(2,1)S(1)}, u32[]{:S(2)}, u32[]{:S(2)}) collective-permute-start(bf16[256,384]{1,0:T(8,128)(2,1)S(1)} %get-tuple-element.72), channel_id=1, source_target_pairs={{0,3},{1,2},{2,1},{3,0},{4,7},{5,6},{6,5},{7,4},{8,11},{9,10},{10,... | collective-permute-start | bytes 589832 | tf_op jit(solution)/shard_map/ppermute | solution.py:32
  10.3 16.1 %collective-permute-start.8 = (bf16[256,384]{1,0:T(8,128)(2,1)S(1)}, bf16[256,384]{1,0:T(8,128)(2,1)S(1)}, u32[]{:S(2)}, u32[]{:S(2)}) collective-permute-start(bf16[256,384]{1,0:T(8,128)(2,1)S(1)} %get-tuple-element.72), channel_id=1, source_target_pairs={{0,1},{1,0},{2,3},{3,2},{4,5},{5,4},{6,7},{7,6},{8,9},{9,8},{10,11... | collective-permute-start | bytes 589832 | tf_op jit(solution)/shard_map/ppermute | solution.py:32
  18.4 5.4 %collective-permute-start.3 = (bf16[256,1152]{1,0:T(8,128)(2,1)S(1)}, bf16[256,1152]{1,0:T(8,128)(2,1)}, u32[]{:S(2)}, u32[]{:S(2)}) collective-permute-start(bf16[256,1152]{1,0:T(8,128)(2,1)S(1)} %maximum_maximum_fusion), channel_id=1, source_target_pairs={{0,4},{4,0},{8,12},{12,8},{1,5},{5,1},{9,13},{13,9},{2,6},{6,2},{1... | collective-permute-start | bytes 1769480 | tf_op jit(solution)/shard_map/cond/branch_1_fun/ppermute | solution.py:32
  18.5 5.3 %collective-permute-start.4 = (bf16[128,384]{1,0:T(8,128)(2,1)S(1)}, bf16[128,384]{1,0:T(8,128)(2,1)}, u32[]{:S(2)}, u32[]{:S(2)}) collective-permute-start(bf16[128,384]{1,0:T(8,128)(2,1)S(1)} %get-tuple-element.16), channel_id=1, source_target_pairs={{0,16},{16,0},{1,17},{17,1},{2,18},{18,2},{3,19},{19,3},{4,20},{20... | collective-permute-start | bytes 294920 | tf_op jit(solution)/shard_map/cond/branch_1_fun/ppermute | solution.py:32
  23.8 2.6 %copy-start = (bf16[1,128,1024]{2,1,0:T(8,128)(2,1)S(1)}, bf16[1,128,1024]{2,1,0:T(8,128)(2,1)}, u32[]{:S(2)}) copy-start(bf16[1,128,1024]{2,1,0:T(8,128)(2,1)} %param.10) | copy-start | bytes 786436
  23.8 11.9 %collective-permute-start.11 = (bf16[128,1664]{1,0:T(8,128)(2,1)S(1)}, bf16[128,1664]{1,0:T(8,128)(2,1)S(1)}, u32[]{:S(2)}, u32[]{:S(2)}) collective-permute-start(bf16[128,1664]{1,0:T(8,128)(2,1)S(1)} %collective-permute-done.5.refs_2_), channel_id=1, source_target_pairs={{0,4},{4,0},{8,12},{12,8},{1,5},{5,1},{9,13},{13,9},{2,6},{6,2},{1... | collective-permute-start | bytes 1277960 | tf_op jit(solution)/shard_map/ppermute | solution.py:32
  23.9 10.0 %collective-permute-start.12 = (bf16[64,1280]{1,0:T(8,128)(2,1)S(1)}, bf16[64,1280]{1,0:T(8,128)(2,1)S(1)}, u32[]{:S(2)}, u32[]{:S(2)}) collective-permute-start(bf16[64,1280]{1,0:T(8,128)(2,1)S(1)} %pad_maximum_fusion), channel_id=1, source_target_pairs={{0,8},{4,12},{8,0},{12,4},{1,9},{5,13},{9,1},{13,5},{2,10},{6,14},... | collective-permute-start | bytes 491528 | tf_op jit(solution)/shard_map/ppermute | solution.py:32
  25.5 8.6 %collective-permute-start.13 = (bf16[64,1280]{1,0:T(8,128)(2,1)S(1)}, bf16[64,1280]{1,0:T(8,128)(2,1)S(1)}, u32[]{:S(2)}, u32[]{:S(2)}) collective-permute-start(bf16[64,1280]{1,0:T(8,128)(2,1)S(1)} %pad_maximum_fusion.1), channel_id=1, source_target_pairs={{0,8},{4,12},{8,0},{12,4},{1,9},{5,13},{9,1},{13,5},{2,10},{6,14},... | collective-permute-start | bytes 491528 | tf_op jit(solution)/shard_map/ppermute | solution.py:32
  34.1 1.4 %collective-permute-start.14 = (bf16[64,1280]{1,0:T(8,128)(2,1)S(1)}, bf16[64,1280]{1,0:T(8,128)(2,1)S(1)}, u32[]{:S(2)}, u32[]{:S(2)}) collective-permute-start(bf16[64,1280]{1,0:T(8,128)(2,1)S(1)} %collective-permute-done.12.refs_4_), channel_id=1, source_target_pairs={{0,4},{4,0},{8,12},{12,8},{1,5},{5,1},{9,13},{13,9},{2,6},{6,2},{1... | collective-permute-start | bytes 491528 | tf_op jit(solution)/shard_map/ppermute | solution.py:32
  34.1 1.6 %collective-permute-start.15 = (bf16[64,1280]{1,0:T(8,128)(2,1)S(1)}, bf16[64,1280]{1,0:T(8,128)(2,1)S(1)}, u32[]{:S(2)}, u32[]{:S(2)}) collective-permute-start(bf16[64,1280]{1,0:T(8,128)(2,1)S(1)} %collective-permute-done.13.refs_5_), channel_id=1, source_target_pairs={{0,4},{4,0},{8,12},{12,8},{1,5},{5,1},{9,13},{13,9},{2,6},{6,2},{1... | collective-permute-start | bytes 491528 | tf_op jit(solution)/shard_map/ppermute | solution.py:32
  34.6 14.7 %collective-permute-start.10 = (bf16[2,128,1152]{2,1,0:T(8,128)(2,1)S(1)}, bf16[2,128,1152]{2,1,0:T(8,128)(2,1)S(1)}, u32[]{:S(2)}, u32[]{:S(2)}) collective-permute-start(bf16[2,128,1152]{2,1,0:T(8,128)(2,1)S(1)} %get-tuple-element.75), channel_id=1, source_target_pairs={{0,4},{4,0},{8,12},{12,8},{1,5},{5,1},{9,13},{13,9},{2,6},{6,2},{1... | collective-permute-start | bytes 1769480 | tf_op jit(solution)/shard_map/ppermute | solution.py:32
  43.2 6.2 %collective-permute-start.16 = (bf16[2,128,1152]{2,1,0:T(8,128)(2,1)S(1)}, bf16[2,128,1152]{2,1,0:T(8,128)(2,1)S(1)}, u32[]{:S(2)}, u32[]{:S(2)}) collective-permute-start(bf16[2,128,1152]{2,1,0:T(8,128)(2,1)S(1)} %get-tuple-element.85), channel_id=1, source_target_pairs={{0,4},{4,0},{8,12},{12,8},{1,5},{5,1},{9,13},{13,9},{2,6},{6,2},{1... | collective-permute-start | bytes 1769480 | tf_op jit(solution)/shard_map/ppermute | solution.py:32
  43.5 28.1 %collective-permute-start.17 = (bf16[256,384]{1,0:T(8,128)(2,1)S(1)}, bf16[256,384]{1,0:T(8,128)(2,1)S(1)}, u32[]{:S(2)}, u32[]{:S(2)}) collective-permute-start(bf16[256,384]{1,0:T(8,128)(2,1)S(1)} %get-tuple-element.90), channel_id=1, source_target_pairs={{0,1},{1,0},{2,3},{3,2},{4,5},{5,4},{6,7},{7,6},{8,9},{9,8},{10,11... | collective-permute-start | bytes 589832 | tf_op jit(solution)/shard_map/ppermute | solution.py:32
  47.0 24.7 %collective-permute-start.18 = (bf16[256,384]{1,0:T(8,128)(2,1)S(1)}, bf16[256,384]{1,0:T(8,128)(2,1)S(1)}, u32[]{:S(2)}, u32[]{:S(2)}) collective-permute-start(bf16[256,384]{1,0:T(8,128)(2,1)S(1)} %get-tuple-element.91), channel_id=1, source_target_pairs={{0,2},{1,3},{2,0},{3,1},{4,6},{5,7},{6,4},{7,5},{8,10},{9,11},{10,... | collective-permute-start | bytes 589832 | tf_op jit(solution)/shard_map/ppermute | solution.py:32
  47.7 23.9 %collective-permute-start.19 = (bf16[256,384]{1,0:T(8,128)(2,1)S(1)}, bf16[256,384]{1,0:T(8,128)(2,1)S(1)}, u32[]{:S(2)}, u32[]{:S(2)}) collective-permute-start(bf16[256,384]{1,0:T(8,128)(2,1)S(1)} %get-tuple-element.92), channel_id=1, source_target_pairs={{0,3},{1,2},{2,1},{3,0},{4,7},{5,6},{6,5},{7,4},{8,11},{9,10},{10,... | collective-permute-start | bytes 589832 | tf_op jit(solution)/shard_map/ppermute | solution.py:32
  49.5 9.4 %collective-permute-start.1 = (bf16[128,1280]{1,0:T(8,128)(2,1)S(1)}, bf16[128,1280]{1,0:T(8,128)(2,1)S(1)}, u32[]{:S(2)}, u32[]{:S(2)}) collective-permute-start(bf16[128,1280]{1,0:T(8,128)(2,1)S(1)} %get-tuple-element.24), channel_id=1, source_target_pairs={{0,8},{4,12},{8,0},{12,4},{1,9},{5,13},{9,1},{13,5},{2,10},{6,14},... | collective-permute-start | bytes 983048 | tf_op jit(solution)/shard_map/cond/branch_1_fun/ppermute | solution.py:32
  58.9 12.7 %collective-permute-start.2 = (bf16[128,1536]{1,0:T(8,128)(2,1)S(1)}, bf16[128,1536]{1,0:T(8,128)(2,1)}, u32[]{:S(2)}, u32[]{:S(2)}) collective-permute-start(bf16[128,1536]{1,0:T(8,128)(2,1)S(1)} %join.1), channel_id=1, source_target_pairs={{0,1},{1,0},{2,3},{3,2},{4,5},{5,4},{6,7},{7,6},{8,9},{9,8},{10,11... | collective-permute-start | bytes 1179656 | tf_op jit(solution)/shard_map/cond/branch_1_fun/ppermute | solution.py:32
  59.9 8.0 %collective-permute-start = (bf16[128,1280]{1,0:T(8,128)(2,1)S(1)}, bf16[128,1280]{1,0:T(8,128)(2,1)}, u32[]{:S(2)}, u32[]{:S(2)}) collective-permute-start(bf16[128,1280]{1,0:T(8,128)(2,1)S(1)} %get-tuple-element.20), channel_id=1, source_target_pairs={{0,8},{4,12},{8,0},{12,4},{1,9},{5,13},{9,1},{13,5},{2,10},{6,14},... | collective-permute-start | bytes 983048 | tf_op jit(solution)/shard_map/cond/branch_1_fun/ppermute | solution.py:32
